TPU v7x, 32 devices: a whole 2x2x4 slice. The times are simulated.
32 devices in a mesh: space: 16 (over z, y, core), filt: 2 (over x).
Axes of the slice: x: 2, y: 2, z: 4, core: 2. Of those that a mesh axis runs over, the one named last changes fastest.
Arguments:
- volume: bfloat16 [64, 32, 4, 256], P(None, 'space', 'filt'), may hold values from -6 to 6
- first_weight: bfloat16 [27, 64, 64], replicated, may hold values from -0.15625 to 0.15625
- second_weight: bfloat16 [27, 128, 64], P(None, 'filt'), may hold values from -0.15625 to 0.15625
- cotangent: bfloat16 [128, 16, 2, 128], P('filt', 'space'), may hold values from -24 to 24
Outputs:
- features: bfloat16 [128, 16, 2, 128], P('filt', 'space')
- volume_grad: bfloat16 [64, 32, 4, 256], P(None, 'space', 'filt')
- first_grad: float32 [27, 64, 64], replicated
- second_grad: float32 [27, 128, 64], P(None, 'filt')
All inputs are finite; a program needn't handle non-finite values.
Results may differ from a plain program's by a relative error of at most 0.019.
Values may be sent and summed in bfloat16 or wider, within the bound.
No kernel may reach another device: no remote copies, remote signals or barrier semaphores. Data moves between devices by JAX's collectives and lax.ppermute only.
A program may use at most 64 MiB of HBM per device.

v0:
```python
import jax
import jax.numpy as jnp
from jax import lax
from jax.sharding import PartitionSpec as P


def extended(cells, sides, width):
    for axis, dim in sides:
        count = lax.axis_size(axis)
        ends = count - 1
        head = lax.slice_in_dim(cells, 0, width, axis=dim)
        tail = lax.slice_in_dim(cells, cells.shape[dim] - width, cells.shape[dim], axis=dim)
        cells = jnp.concatenate(
            [
                lax.ppermute(tail, axis, [(i, (i + 1) % count) for i in range(ends)]),
                cells,
                lax.ppermute(head, axis, [((i + 1) % count, i) for i in range(ends)]),
            ],
            axis=dim,
        )
    return cells


def silu_slope(values):
    sigmoid_part = jax.nn.sigmoid(values)
    return sigmoid_part * (1.0 + values * (1.0 - sigmoid_part))


def pad_depth(volume_field):
    return jnp.pad(volume_field, ((0, 0), (0, 0), (0, 0), (1, 1)))


def window(padded, offset_x, offset_y, offset_z, extents):
    extent_x, extent_y, extent_z = extents
    section = lax.slice(
        padded,
        (0, offset_x, offset_y, offset_z),
        (padded.shape[0], offset_x + extent_x, offset_y + extent_y, offset_z + extent_z),
    )
    return section.reshape(padded.shape[0], extent_x * extent_y * extent_z)


def conv_forward(padded, weight, extents):
    outputs, inputs = (weight.shape[1], weight.shape[2])
    running = jnp.zeros((outputs, extents[0] * extents[1] * extents[2]), jnp.float32)
    for offset_x in range(3):
        for offset_y in range(3):
            tap_base = offset_x * 9 + offset_y * 3
            stacked = jnp.concatenate(
                [window(padded, offset_x, offset_y, offset_z, extents) for offset_z in range(3)],
                axis=0,
            )
            matrices = jnp.transpose(weight[tap_base : tap_base + 3], (1, 0, 2)).reshape(
                outputs, 3 * inputs
            )
            running = running + jnp.dot(matrices, stacked, preferred_element_type=jnp.float32)
    return running


def conv_transpose(padded, weight, extents):
    outputs, inputs = (weight.shape[1], weight.shape[2])
    running = jnp.zeros((inputs, extents[0] * extents[1] * extents[2]), jnp.float32)
    for offset_x in range(3):
        for offset_y in range(3):
            tap_base = offset_x * 9 + offset_y * 3
            stacked = jnp.concatenate(
                [window(padded, offset_x, offset_y, offset_z, extents) for offset_z in range(3)],
                axis=0,
            )
            tap_block = weight[24 - tap_base : 27 - tap_base][::-1]
            matrices = jnp.transpose(tap_block, (2, 0, 1)).reshape(inputs, 3 * outputs)
            running = running + jnp.dot(matrices, stacked, preferred_element_type=jnp.float32)
    return running


def conv_weights(grad_rows, padded, extents):
    outputs, inputs = (grad_rows.shape[0], padded.shape[0])
    blocks = []
    for offset_x in range(3):
        for offset_y in range(3):
            stacked = jnp.concatenate(
                [window(padded, offset_x, offset_y, offset_z, extents) for offset_z in range(3)],
                axis=0,
            )
            section = lax.dot_general(
                grad_rows, stacked, (((1,), (1,)), ((), ())), preferred_element_type=jnp.float32
            )
            blocks.append(jnp.transpose(section.reshape(outputs, 3, inputs), (1, 0, 2)))
    return jnp.concatenate(blocks, axis=0)


def pool_cells(hidden):
    channels, size_x, size_y, size_z = hidden.shape
    pair_table = (jnp.arange(size_z)[:, None] // 2 == jnp.arange(size_z // 2)[None, :]).astype(
        jnp.bfloat16
    )
    depth_sums = jnp.dot(hidden.reshape(-1, size_z), pair_table, preferred_element_type=jnp.float32)
    depth_sums = depth_sums.reshape(channels, size_x // 2, 2, size_y // 2, 2, size_z // 2)
    return (0.125 * depth_sums.sum(axis=(2, 4))).astype(jnp.bfloat16)


def spread_cells(grad_field):
    scaled = 0.125 * grad_field
    scaled = jnp.repeat(scaled, 2, axis=1)
    scaled = jnp.repeat(scaled, 2, axis=2)
    return jnp.repeat(scaled, 2, axis=3)


def local(volume, first_weight, second_weight, cotangent):
    count_space = lax.axis_size("space")
    count_filt = lax.axis_size("filt")
    channels = volume.shape[0]
    fine_shape = volume.shape[1:]
    fine_cells = fine_shape[0] * fine_shape[1] * fine_shape[2] * count_space * count_filt
    fine_scale = 1.0 / fine_cells**0.5
    padded_in = pad_depth(extended(volume, (("space", 1), ("filt", 2)), 1))
    first_pre = conv_forward(padded_in, first_weight, fine_shape)
    hidden = jax.nn.silu(first_pre).astype(jnp.bfloat16).reshape((channels,) + fine_shape)
    pooled = pool_cells(hidden)
    brick_shape = pooled.shape[1:]
    brick_cells = brick_shape[0] * brick_shape[1] * brick_shape[2]
    bottom_scale = 1.0 / (brick_cells * count_space * count_filt) ** 0.5
    filters = second_weight.shape[1]
    whole_weight = lax.all_gather(second_weight, "filt", axis=1, tiled=True)
    total_filters = whole_weight.shape[1]
    padded_pool = pad_depth(extended(pooled, (("space", 1), ("filt", 2)), 1))
    second_pre = conv_forward(padded_pool, whole_weight, brick_shape)
    local_out = jax.nn.silu(second_pre).astype(jnp.bfloat16).reshape((total_filters,) + brick_shape)
    features = lax.all_to_all(local_out, "filt", split_axis=0, concat_axis=2, tiled=True)
    local_cot = lax.all_to_all(cotangent, "filt", split_axis=2, concat_axis=0, tiled=True)
    down_grad = (
        local_cot.reshape(total_filters, -1).astype(jnp.float32) * silu_slope(second_pre)
    ).astype(jnp.bfloat16)
    summed = lax.psum(conv_weights(down_grad, padded_pool, brick_shape), ("space", "filt"))
    second_grad = (
        lax.dynamic_slice_in_dim(summed, lax.axis_index("filt") * filters, filters, 1)
        * bottom_scale
    )
    padded_down = pad_depth(
        extended(down_grad.reshape((total_filters,) + brick_shape), (("space", 1), ("filt", 2)), 1)
    )

    def add_group(group_index, running):
        group_rows = lax.dynamic_slice_in_dim(padded_down, group_index * filters, filters, 0)
        tap_block = lax.dynamic_slice_in_dim(whole_weight, group_index * filters, filters, 1)
        section = conv_transpose(group_rows, tap_block, brick_shape)
        return running + lax.optimization_barrier(section.astype(jnp.bfloat16)).astype(jnp.float32)

    pool_grad = lax.fori_loop(
        0, count_filt, add_group, jnp.zeros((channels, brick_cells), jnp.float32)
    )
    hidden_grad = spread_cells(pool_grad.reshape((channels,) + brick_shape))
    first_down = (hidden_grad.reshape(channels, -1) * silu_slope(first_pre)).astype(jnp.bfloat16)
    first_grad = (
        lax.psum(conv_weights(first_down, padded_in, fine_shape), ("space", "filt")) * fine_scale
    )
    padded_back = pad_depth(
        extended(first_down.reshape((channels,) + fine_shape), (("space", 1), ("filt", 2)), 1)
    )
    volume_grad = (
        conv_transpose(padded_back, first_weight, fine_shape)
        .astype(jnp.bfloat16)
        .reshape((channels,) + fine_shape)
    )
    return (features, volume_grad, first_grad, second_grad)


def solution(mesh):
    placed = (
        P(None, "space", "filt", None),
        P(),
        P(None, "filt", None),
        P("filt", "space", None, None),
    )
    return jax.shard_map(
        local,
        mesh=mesh,
        in_specs=placed,
        out_specs=(
            P("filt", "space", None, None),
            P(None, "space", "filt", None),
            P(),
            P(None, "filt", None),
        ),
        check_vma=False,
    )
```

profile of v0, /device:TPU:1, one launch (start us, length us, event | category | flops | bytes accessed | tf_op | source)
XLA Modules:
  0.0 315.8 jit_solution(11860188222224926915)
XLA Ops:
  8.5 3.9 %all-to-all-start.1 = ((bf16[64,1,2,128]{3,0,1,2:T(8,128)(2,1)}), bf16[64,1,2,128]{3,0,1,2:T(8,128)(2,1)}, u32[]{:S(2)}, u32[]{:S(2)}) async-start(bf16[64,1,2,128]{3,0,1,2:T(8,128)(2,1)} %copy.107), calls=%async_computation.1 | async-start | bytes 65536 | tf_op jit(solution)/shard_map/all_to_all | solution.py:130
  13.4 2.3 collective-permute-start.1
  15.7 4.2 %collective-permute-start = (bf16[64,1,2,256]{3,2,1,0:T(2,128)(2,1)S(1)}, bf16[64,1,2,256]{3,2,1,0:T(2,128)(2,1)S(1)}, u32[]{:S(2)}, u32[]{:S(2)}) collective-permute-start(bf16[64,1,2,256]{3,2,1,0:T(2,128)(2,1)S(1)} %get-tuple-element.277), channel_id=1, source_target_pairs={{0,2},{2,4},{4,6},{6,8},{8,10},{10,12},{12,14},{14,16},{16,18},{18... | collective-permute-start | bytes 196616 | tf_op jit(solution)/shard_map/ppermute | solution.py:15
  21.2 13.8 %all_gather.3 = bf16[27,128,64]{2,0,1:T(8,128)(2,1)S(1)} all-gather(bf16[27,64,64]{2,0,1:T(8,128)(2,1)S(1)} %copy.96), channel_id=1, replica_groups=mesh['space'=16,'filt'=2] {'filt'}, dimensions={1}, use_global_device_ids=true | all-gather | bytes 663552 | tf_op jit(solution)/shard_map/all_gather | solution.py:124
  37.9 3.6 %collective-permute-start.2 = (bf16[64,4,1,256]{3,2,1,0:T(2,128)(2,1)}, bf16[64,4,1,256]{3,2,1,0:T(2,128)(2,1)S(1)}, u32[]{:S(2)}, u32[]{:S(2)}) collective-permute-start(bf16[64,4,1,256]{3,2,1,0:T(2,128)(2,1)} %get-tuple-element.266), channel_id=1, source_target_pairs={{0,1},{2,3},{4,5},{6,7},{8,9},{10,11},{12,13},{14,15},{16,17},{18,... | collective-permute-start | bytes 393224 | tf_op jit(solution)/shard_map/ppermute | solution.py:15
  41.5 1.5 collective-permute-start.3
  45.3 1.8 copy.153
  48.1 1.6 copy.151
  49.7 1.6 copy.150
  51.3 1.6 copy.149
  69.9 1.7 pad_maximum_fusion.9
  75.4 2.4 select_maximum_fusion.2
  77.8 2.9 fusion.157
  92.8 2.2 collective-permute-start.5
  95.0 3.5 %collective-permute-start.4 = (bf16[64,1,1,128]{3,0,2,1:T(8,128)(2,1)S(1)}, bf16[64,1,1,128]{3,0,2,1:T(8,128)(2,1)S(1)}, u32[]{:S(2)}, u32[]{:S(2)}) collective-permute-start(bf16[64,1,1,128]{3,0,2,1:T(8,128)(2,1)S(1)} %fusion.245), channel_id=1, source_target_pairs={{0,2},{2,4},{4,6},{6,8},{8,10},{10,12},{12,14},{14,16},{16,18},{18... | collective-permute-start | bytes 49160 | tf_op jit(solution)/shard_map/ppermute | solution.py:15
  100.8 4.5 %collective-permute-start.6 = (bf16[64,3,1,128]{3,0,2,1:T(8,128)(2,1)S(1)}, bf16[64,3,1,128]{3,0,2,1:T(8,128)(2,1)S(1)}, u32[]{:S(2)}, u32[]{:S(2)}) collective-permute-start(bf16[64,3,1,128]{3,0,2,1:T(8,128)(2,1)S(1)} %pad_maximum_fusion.18), channel_id=1, source_target_pairs={{0,1},{2,3},{4,5},{6,7},{8,9},{10,11},{12,13},{14,15},{16,17},{18,... | collective-permute-start | bytes 147464 | tf_op jit(solution)/shard_map/ppermute | solution.py:15
  108.4 1.9 collective-permute-start.9
  110.4 5.0 %collective-permute-start.8 = (bf16[128,1,1,128]{0,3,2,1:T(8,128)(2,1)S(1)}, bf16[128,1,1,128]{0,3,2,1:T(8,128)(2,1)S(1)}, u32[]{:S(2)}, u32[]{:S(2)}) collective-permute-start(bf16[128,1,1,128]{0,3,2,1:T(8,128)(2,1)S(1)} %bitcast.409), channel_id=1, source_target_pairs={{0,2},{2,4},{4,6},{6,8},{8,10},{10,12},{12,14},{14,16},{16,18},{18... | collective-permute-start | bytes 98312 | tf_op jit(solution)/shard_map/ppermute | solution.py:15
  118.5 3.3 %all-to-all-start = ((bf16[2,2,4096]{2,1,0:T(2,128)(2,1)}), bf16[2,2,4096]{2,1,0:T(2,128)(2,1)S(1)}, u32[]{:S(2)}, u32[]{:S(2)}) async-start(bf16[2,2,4096]{2,1,0:T(2,128)(2,1)} %reshape.942), calls=%async_computation | async-start | bytes 65536 | tf_op jit(solution)/shard_map/all_to_all | solution.py:129
  132.8 4.0 %collective-permute-start.10 = (bf16[128,3,1,128]{0,3,2,1:T(8,128)(2,1)S(1)}, bf16[128,3,1,128]{0,3,2,1:T(8,128)(2,1)S(1)}, u32[]{:S(2)}, u32[]{:S(2)}) collective-permute-start(bf16[128,3,1,128]{0,3,2,1:T(8,128)(2,1)S(1)} %pad_maximum_fusion.17), channel_id=1, source_target_pairs={{0,1},{2,3},{4,5},{6,7},{8,9},{10,11},{12,13},{14,15},{16,17},{18,... | collective-permute-start | bytes 294920 | tf_op jit(solution)/shard_map/ppermute | solution.py:15
  138.9 5.5 %while.14 = (s32[]{:T(128)}, f32[64,128]{1,0:T(8,128)}, bf16[27,128,64]{2,1,0:T(8,128)(2,1)S(1)}, bf16[128,3,3,130]{3,0,2,1:T(8,128)(2,1)S(1)}, s32[]{:T(128)}, ...) while((s32[]{:T(128)}, f32[64,128]{1,0:T(8,128)}, ...), condition=%wide.region_2.3_spmd.clone, body=%wide.region_1.2_spmd.clone.sunk | while | flops 29736976 | bytes 3318213 | solution.py:149
  148.5 1.9 collective-permute-start.13
  150.4 3.8 %collective-permute-start.12 = (bf16[64,1,2,256]{3,2,1,0:T(2,128)(2,1)S(1)}, bf16[64,1,2,256]{3,2,1,0:T(2,128)(2,1)S(1)}, u32[]{:S(2)}, u32[]{:S(2)}) collective-permute-start(bf16[64,1,2,256]{3,2,1,0:T(2,128)(2,1)S(1)} %get-tuple-element.272), channel_id=1, source_target_pairs={{0,2},{2,4},{4,6},{6,8},{8,10},{10,12},{12,14},{14,16},{16,18},{18... | collective-permute-start | bytes 196616 | tf_op jit(solution)/shard_map/ppermute | solution.py:15
  156.4 4.0 %collective-permute-start.14 = (bf16[64,4,1,256]{3,2,1,0:T(2,128)(2,1)S(1)}, bf16[64,4,1,256]{3,2,1,0:T(2,128)(2,1)S(1)}, u32[]{:S(2)}, u32[]{:S(2)}) collective-permute-start(bf16[64,4,1,256]{3,2,1,0:T(2,128)(2,1)S(1)} %get-tuple-element.261), channel_id=1, source_target_pairs={{0,1},{2,3},{4,5},{6,7},{8,9},{10,11},{12,13},{14,15},{16,17},{18,... | collective-permute-start | bytes 393224 | tf_op jit(solution)/shard_map/ppermute | solution.py:15
  160.4 1.6 collective-permute-start.15
  163.1 1.7 collective-permute-done.14
  164.9 4.1 %collective-permute-done.15 = bf16[64,4,1,256]{3,2,1,0:T(2,128)(2,1)S(1)} collective-permute-done((bf16[64,4,1,256]{3,2,1,0:T(2,128)(2,1)S(1)}, bf16[64,4,1,256]{3,2,1,0:T(2,128)(2,1)S(1)}, u32[]{:S(2)}, u32[]{:S(2)}) %collective-permute-start.15) | collective-permute-done | bytes 131104 | tf_op jit(solution)/shard_map/ppermute | solution.py:17
  169.0 1.7 pad_maximum_fusion.1
  173.1 2.4 select_maximum_fusion
  175.5 2.9 fusion.156
  186.7 118.6 %all-reduce.7.cloned.1.call-done = (f32[27,64,64]{1,2,0:T(8,128)}, f32[27,128,64]{2,1,0:T(8,128)}) async-done(((f32[27,64,64]{1,2,0:T(8,128)}, f32[27,128,64]{2,1,0:T(8,128)}), (f32[27,64,64]{1,2,0:T(8,128)}, f32[27,128,64]{2,1,0:T(8,128)})) %all-reduce.7.cloned.1.call-update) | async-done | bytes 1327120 | tf_op jit(solution)/shard_map/psum | solution.py:155
  305.4 1.4 broadcast_multiply_fusion
  (475 shorter events, 87.6 us)
Async XLA Ops:
  8.5 90.0 %all-to-all-start.1 = ((bf16[64,1,2,128]{3,0,1,2:T(8,128)(2,1)}), bf16[64,1,2,128]{3,0,1,2:T(8,128)(2,1)}, u32[]{:S(2)}, u32[]{:S(2)}) async-start(bf16[64,1,2,128]{3,0,1,2:T(8,128)(2,1)} %copy.107), calls=%async_computation.1 | async-start | bytes 65536 | tf_op jit(solution)/shard_map/all_to_all | solution.py:130
  13.4 22.9 %collective-permute-start.1 = (bf16[64,1,2,256]{3,2,1,0:T(2,128)(2,1)S(1)}, bf16[64,1,2,256]{3,2,1,0:T(2,128)(2,1)S(1)}, u32[]{:S(2)}, u32[]{:S(2)}) collective-permute-start(bf16[64,1,2,256]{3,2,1,0:T(2,128)(2,1)S(1)} %get-tuple-element.276), channel_id=1, source_target_pairs={{2,0},{4,2},{6,4},{8,6},{10,8},{12,10},{14,12},{16,14},{18,16},{20... | collective-permute-start | bytes 196616 | tf_op jit(solution)/shard_map/ppermute | solution.py:17
  15.7 20.5 %collective-permute-start = (bf16[64,1,2,256]{3,2,1,0:T(2,128)(2,1)S(1)}, bf16[64,1,2,256]{3,2,1,0:T(2,128)(2,1)S(1)}, u32[]{:S(2)}, u32[]{:S(2)}) collective-permute-start(bf16[64,1,2,256]{3,2,1,0:T(2,128)(2,1)S(1)} %get-tuple-element.277), channel_id=1, source_target_pairs={{0,2},{2,4},{4,6},{6,8},{8,10},{10,12},{12,14},{14,16},{16,18},{18... | collective-permute-start | bytes 196616 | tf_op jit(solution)/shard_map/ppermute | solution.py:15
  37.9 32.1 %collective-permute-start.2 = (bf16[64,4,1,256]{3,2,1,0:T(2,128)(2,1)}, bf16[64,4,1,256]{3,2,1,0:T(2,128)(2,1)S(1)}, u32[]{:S(2)}, u32[]{:S(2)}) collective-permute-start(bf16[64,4,1,256]{3,2,1,0:T(2,128)(2,1)} %get-tuple-element.266), channel_id=1, source_target_pairs={{0,1},{2,3},{4,5},{6,7},{8,9},{10,11},{12,13},{14,15},{16,17},{18,... | collective-permute-start | bytes 393224 | tf_op jit(solution)/shard_map/ppermute | solution.py:15
  41.5 28.4 %collective-permute-start.3 = (bf16[64,4,1,256]{3,2,1,0:T(2,128)(2,1)}, bf16[64,4,1,256]{3,2,1,0:T(2,128)(2,1)S(1)}, u32[]{:S(2)}, u32[]{:S(2)}) collective-permute-start(bf16[64,4,1,256]{3,2,1,0:T(2,128)(2,1)} %get-tuple-element.267), channel_id=1, source_target_pairs={{1,0},{3,2},{5,4},{7,6},{9,8},{11,10},{13,12},{15,14},{17,16},{19,... | collective-permute-start | bytes 393224 | tf_op jit(solution)/shard_map/ppermute | solution.py:17
  45.1 15.7 %copy-start.62 = (bf16[64,3,64]{2,0,1:T(8,128)(2,1)S(1)}, bf16[64,3,64]{2,0,1:T(8,128)(2,1)}, u32[]{:S(2)}) copy-start(bf16[64,3,64]{2,0,1:T(8,128)(2,1)} %get-tuple-element.228) | copy-start | bytes 73732
  45.2 16.4 %copy-start.61 = (bf16[64,3,64]{2,0,1:T(8,128)(2,1)S(1)}, bf16[64,3,64]{2,0,1:T(8,128)(2,1)}, u32[]{:S(2)}) copy-start(bf16[64,3,64]{2,0,1:T(8,128)(2,1)} %get-tuple-element.229) | copy-start | bytes 73732
  45.2 17.1 %copy-start.60 = (bf16[64,3,64]{2,0,1:T(8,128)(2,1)S(1)}, bf16[64,3,64]{2,0,1:T(8,128)(2,1)}, u32[]{:S(2)}) copy-start(bf16[64,3,64]{2,0,1:T(8,128)(2,1)} %get-tuple-element.230) | copy-start | bytes 73732
  45.2 17.8 %copy-start.59 = (bf16[64,3,64]{2,0,1:T(8,128)(2,1)S(1)}, bf16[64,3,64]{2,0,1:T(8,128)(2,1)}, u32[]{:S(2)}) copy-start(bf16[64,3,64]{2,0,1:T(8,128)(2,1)} %get-tuple-element.231) | copy-start | bytes 73732
  45.2 18.5 %copy-start.58 = (bf16[3,64,64]{2,1,0:T(8,128)(2,1)S(1)}, bf16[3,64,64]{2,1,0:T(8,128)(2,1)}, u32[]{:S(2)}) copy-start(bf16[3,64,64]{2,1,0:T(8,128)(2,1)} %get-tuple-element.232) | copy-start | bytes 73732
  45.2 19.1 %copy-start.57 = (bf16[3,64,64]{2,1,0:T(8,128)(2,1)S(1)}, bf16[3,64,64]{2,1,0:T(8,128)(2,1)}, u32[]{:S(2)}) copy-start(bf16[3,64,64]{2,1,0:T(8,128)(2,1)} %get-tuple-element.233) | copy-start | bytes 73732
  45.2 19.7 %copy-start.56 = (bf16[3,64,64]{2,1,0:T(8,128)(2,1)S(1)}, bf16[3,64,64]{2,1,0:T(8,128)(2,1)}, u32[]{:S(2)}) copy-start(bf16[3,64,64]{2,1,0:T(8,128)(2,1)} %get-tuple-element.234) | copy-start | bytes 73732
  45.2 20.3 %copy-start.55 = (bf16[3,64,64]{2,1,0:T(8,128)(2,1)S(1)}, bf16[3,64,64]{2,1,0:T(8,128)(2,1)}, u32[]{:S(2)}) copy-start(bf16[3,64,64]{2,1,0:T(8,128)(2,1)} %get-tuple-element.235) | copy-start | bytes 73732
  45.2 20.9 %copy-start.54 = (bf16[3,64,64]{2,1,0:T(8,128)(2,1)S(1)}, bf16[3,64,64]{2,1,0:T(8,128)(2,1)}, u32[]{:S(2)}) copy-start(bf16[3,64,64]{2,1,0:T(8,128)(2,1)} %get-tuple-element.236) | copy-start | bytes 73732
  45.2 21.5 %copy-start.53 = (bf16[3,64,64]{2,1,0:T(8,128)(2,1)S(1)}, bf16[3,64,64]{2,1,0:T(8,128)(2,1)}, u32[]{:S(2)}) copy-start(bf16[3,64,64]{2,1,0:T(8,128)(2,1)} %get-tuple-element.237) | copy-start | bytes 73732
  45.2 22.1 %copy-start.52 = (bf16[3,64,64]{2,1,0:T(8,128)(2,1)S(1)}, bf16[3,64,64]{2,1,0:T(8,128)(2,1)}, u32[]{:S(2)}) copy-start(bf16[3,64,64]{2,1,0:T(8,128)(2,1)} %get-tuple-element.238) | copy-start | bytes 73732
  45.3 22.8 %copy-start.51 = (bf16[3,64,64]{2,1,0:T(8,128)(2,1)S(1)}, bf16[3,64,64]{2,1,0:T(8,128)(2,1)}, u32[]{:S(2)}) copy-start(bf16[3,64,64]{2,1,0:T(8,128)(2,1)} %get-tuple-element.239) | copy-start | bytes 73732
  91.5 15.5 %copy-start.41 = (bf16[3,128,64]{1,2,0:T(8,128)(2,1)S(1)}, bf16[3,128,64]{1,2,0:T(8,128)(2,1)}, u32[]{:S(2)}) copy-start(bf16[3,128,64]{1,2,0:T(8,128)(2,1)} %copy.147) | copy-start | bytes 147460
  92.8 6.6 %collective-permute-start.5 = (bf16[64,1,1,128]{3,0,2,1:T(8,128)(2,1)S(1)}, bf16[64,1,1,128]{3,0,2,1:T(8,128)(2,1)S(1)}, u32[]{:S(2)}, u32[]{:S(2)}) collective-permute-start(bf16[64,1,1,128]{3,0,2,1:T(8,128)(2,1)S(1)} %fusion.245), channel_id=1, source_target_pairs={{2,0},{4,2},{6,4},{8,6},{10,8},{12,10},{14,12},{16,14},{18,16},{20... | collective-permute-start | bytes 49160 | tf_op jit(solution)/shard_map/ppermute | solution.py:17
  95.0 4.4 %collective-permute-start.4 = (bf16[64,1,1,128]{3,0,2,1:T(8,128)(2,1)S(1)}, bf16[64,1,1,128]{3,0,2,1:T(8,128)(2,1)S(1)}, u32[]{:S(2)}, u32[]{:S(2)}) collective-permute-start(bf16[64,1,1,128]{3,0,2,1:T(8,128)(2,1)S(1)} %fusion.245), channel_id=1, source_target_pairs={{0,2},{2,4},{4,6},{6,8},{8,10},{10,12},{12,14},{14,16},{16,18},{18... | collective-permute-start | bytes 49160 | tf_op jit(solution)/shard_map/ppermute | solution.py:15
  99.5 5.8 %collective-permute-start.7 = (bf16[64,3,1,128]{3,0,2,1:T(8,128)(2,1)S(1)}, bf16[64,3,1,128]{3,0,2,1:T(8,128)(2,1)S(1)}, u32[]{:S(2)}, u32[]{:S(2)}) collective-permute-start(bf16[64,3,1,128]{3,0,2,1:T(8,128)(2,1)S(1)} %pad_maximum_fusion.18), channel_id=1, source_target_pairs={{1,0},{3,2},{5,4},{7,6},{9,8},{11,10},{13,12},{15,14},{17,16},{19,... | collective-permute-start | bytes 147464 | tf_op jit(solution)/shard_map/ppermute | solution.py:17
  100.8 5.4 %collective-permute-start.6 = (bf16[64,3,1,128]{3,0,2,1:T(8,128)(2,1)S(1)}, bf16[64,3,1,128]{3,0,2,1:T(8,128)(2,1)S(1)}, u32[]{:S(2)}, u32[]{:S(2)}) collective-permute-start(bf16[64,3,1,128]{3,0,2,1:T(8,128)(2,1)S(1)} %pad_maximum_fusion.18), channel_id=1, source_target_pairs={{0,1},{2,3},{4,5},{6,7},{8,9},{10,11},{12,13},{14,15},{16,17},{18,... | collective-permute-start | bytes 147464 | tf_op jit(solution)/shard_map/ppermute | solution.py:15
  108.4 23.0 %collective-permute-start.9 = (bf16[128,1,1,128]{0,3,2,1:T(8,128)(2,1)S(1)}, bf16[128,1,1,128]{0,3,2,1:T(8,128)(2,1)S(1)}, u32[]{:S(2)}, u32[]{:S(2)}) collective-permute-start(bf16[128,1,1,128]{0,3,2,1:T(8,128)(2,1)S(1)} %bitcast.408), channel_id=1, source_target_pairs={{2,0},{4,2},{6,4},{8,6},{10,8},{12,10},{14,12},{16,14},{18,16},{20... | collective-permute-start | bytes 98312 | tf_op jit(solution)/shard_map/ppermute | solution.py:17
  110.4 21.0 %collective-permute-start.8 = (bf16[128,1,1,128]{0,3,2,1:T(8,128)(2,1)S(1)}, bf16[128,1,1,128]{0,3,2,1:T(8,128)(2,1)S(1)}, u32[]{:S(2)}, u32[]{:S(2)}) collective-permute-start(bf16[128,1,1,128]{0,3,2,1:T(8,128)(2,1)S(1)} %bitcast.409), channel_id=1, source_target_pairs={{0,2},{2,4},{4,6},{6,8},{8,10},{10,12},{12,14},{14,16},{16,18},{18... | collective-permute-start | bytes 98312 | tf_op jit(solution)/shard_map/ppermute | solution.py:15
  118.5 18.3 %all-to-all-start = ((bf16[2,2,4096]{2,1,0:T(2,128)(2,1)}), bf16[2,2,4096]{2,1,0:T(2,128)(2,1)S(1)}, u32[]{:S(2)}, u32[]{:S(2)}) async-start(bf16[2,2,4096]{2,1,0:T(2,128)(2,1)} %reshape.942), calls=%async_computation | async-start | bytes 65536 | tf_op jit(solution)/shard_map/all_to_all | solution.py:129
  121.8 183.5 %all-reduce.7.cloned.1.call-start = ((), (), s32[]{:S(2)}) async-start(), calls=%async_computation.2 | async-start | bytes 5308416 | tf_op jit(solution)/shard_map/psum | solution.py:155
  131.5 6.2 %collective-permute-start.11 = (bf16[128,3,1,128]{0,3,2,1:T(8,128)(2,1)S(1)}, bf16[128,3,1,128]{0,3,2,1:T(8,128)(2,1)S(1)}, u32[]{:S(2)}, u32[]{:S(2)}) collective-permute-start(bf16[128,3,1,128]{0,3,2,1:T(8,128)(2,1)S(1)} %pad_maximum_fusion.17), channel_id=1, source_target_pairs={{1,0},{3,2},{5,4},{7,6},{9,8},{11,10},{13,12},{15,14},{17,16},{19,... | collective-permute-start | bytes 294920 | tf_op jit(solution)/shard_map/ppermute | solution.py:17
  132.8 5.6 %collective-permute-start.10 = (bf16[128,3,1,128]{0,3,2,1:T(8,128)(2,1)S(1)}, bf16[128,3,1,128]{0,3,2,1:T(8,128)(2,1)S(1)}, u32[]{:S(2)}, u32[]{:S(2)}) collective-permute-start(bf16[128,3,1,128]{0,3,2,1:T(8,128)(2,1)S(1)} %pad_maximum_fusion.17), channel_id=1, source_target_pairs={{0,1},{2,3},{4,5},{6,7},{8,9},{10,11},{12,13},{14,15},{16,17},{18,... | collective-permute-start | bytes 294920 | tf_op jit(solution)/shard_map/ppermute | solution.py:15
  148.5 7.1 %collective-permute-start.13 = (bf16[64,1,2,256]{3,2,1,0:T(2,128)(2,1)S(1)}, bf16[64,1,2,256]{3,2,1,0:T(2,128)(2,1)S(1)}, u32[]{:S(2)}, u32[]{:S(2)}) collective-permute-start(bf16[64,1,2,256]{3,2,1,0:T(2,128)(2,1)S(1)} %get-tuple-element.271), channel_id=1, source_target_pairs={{2,0},{4,2},{6,4},{8,6},{10,8},{12,10},{14,12},{16,14},{18,16},{20... | collective-permute-start | bytes 196616 | tf_op jit(solution)/shard_map/ppermute | solution.py:17
  150.4 5.1 %collective-permute-start.12 = (bf16[64,1,2,256]{3,2,1,0:T(2,128)(2,1)S(1)}, bf16[64,1,2,256]{3,2,1,0:T(2,128)(2,1)S(1)}, u32[]{:S(2)}, u32[]{:S(2)}) collective-permute-start(bf16[64,1,2,256]{3,2,1,0:T(2,128)(2,1)S(1)} %get-tuple-element.272), channel_id=1, source_target_pairs={{0,2},{2,4},{4,6},{6,8},{8,10},{10,12},{12,14},{14,16},{16,18},{18... | collective-permute-start | bytes 196616 | tf_op jit(solution)/shard_map/ppermute | solution.py:15
  156.4 8.5 %collective-permute-start.14 = (bf16[64,4,1,256]{3,2,1,0:T(2,128)(2,1)S(1)}, bf16[64,4,1,256]{3,2,1,0:T(2,128)(2,1)S(1)}, u32[]{:S(2)}, u32[]{:S(2)}) collective-permute-start(bf16[64,4,1,256]{3,2,1,0:T(2,128)(2,1)S(1)} %get-tuple-element.261), channel_id=1, source_target_pairs={{0,1},{2,3},{4,5},{6,7},{8,9},{10,11},{12,13},{14,15},{16,17},{18,... | collective-permute-start | bytes 393224 | tf_op jit(solution)/shard_map/ppermute | solution.py:15
  160.4 8.5 %collective-permute-start.15 = (bf16[64,4,1,256]{3,2,1,0:T(2,128)(2,1)S(1)}, bf16[64,4,1,256]{3,2,1,0:T(2,128)(2,1)S(1)}, u32[]{:S(2)}, u32[]{:S(2)}) collective-permute-start(bf16[64,4,1,256]{3,2,1,0:T(2,128)(2,1)S(1)} %get-tuple-element.262), channel_id=1, source_target_pairs={{1,0},{3,2},{5,4},{7,6},{9,8},{11,10},{13,12},{15,14},{17,16},{19,... | collective-permute-start | bytes 393224 | tf_op jit(solution)/shard_map/ppermute | solution.py:17
  (82 other events, 344.6 us)
Sparse Core Ops, SparseCore 0:
  163.1 142.2 all-reduce.6
where the time goes:
time: 318 us; the launch traced here: 316 us
  waiting for transfers between devices  127 us (40%)
  local copies, waits for them, and re-layouts  75.2 us (24%)
  starting transfers between devices  53.8 us (17%)
  between operations  16.3 us (5%)
  matrix products  14.6 us (5%)
  other arithmetic  14.5 us (5%)
  blocking collectives  13.8 us (4%)
    psum x1, waiting for transfers between devices, local(): lax.psum(conv_weights(first_down, padded_in, fine_shape), ('space', 'filt'))  119 us
    ppermute x8, starting transfers between devices, extended(): lax.ppermute(tail, axis, [(i, (i + 1) % count) for i in range(ends)])  32.7 us
    unnamed x237, local copies, waits for them, and re-layouts  25.8 us
    reshape x58, local copies, waits for them, and re-layouts, window(): return section.reshape(padded.shape[0], extent_x * extent_y * extent_z)  17.6 us
    ppermute x8, starting transfers between devices, extended(): lax.ppermute(head, axis, [((i + 1) % count, i) for i in range(ends)])  13.9 us
    all_gather x1, blocking collectives, local(): whole_weight = lax.all_gather(second_weight, 'filt', axis=1, tiled=True)  13.8 us
    concatenate x10, other arithmetic, extended(): jnp.concatenate([lax.ppermute(tail, axis, [(i, (i + 1) % count) for i in...  9.21 us
    rev x27, local copies, waits for them, and re-layouts, conv_transpose(): tap_block = weight[24 - tap_base:27 - tap_base][::-1]  6.46 us
  transfers between devices with their start and end apart: 19, of which 6 were waited for; matrix products, arithmetic and copies ran while one was open for 27% of the time, Pallas kernels for 0%

commit v1 on v0

v1 whole, which is shorter than its diff:
```python
import functools

import jax
import jax.numpy as jnp
from jax import lax
from jax.experimental import pallas as pl
from jax.experimental.pallas import tpu as pltpu
from jax.sharding import PartitionSpec as P

F32 = jnp.float32
BF16 = jnp.bfloat16
VMEM_LIMIT = 56 * 1024 * 1024


def call(body, outs, scratch=(), name=None):
    return pl.pallas_call(
        body,
        out_shape=outs,
        scratch_shapes=scratch,
        name=name,
        compiler_params=pltpu.CompilerParams(vmem_limit_bytes=VMEM_LIMIT),
    )


def shaped(shape, dtype):
    return jax.ShapeDtypeStruct(shape, dtype)


def dot(lhs, rhs):
    return jnp.dot(lhs, rhs, preferred_element_type=F32)


def dot_cells(lhs, rhs):
    return lax.dot_general(lhs, rhs, (((1,), (1,)), ((), ())), preferred_element_type=F32)


def silu_slope(values):
    part = 1.0 / (1.0 + jnp.exp(-values))
    return part * (1.0 + values * (1.0 - part))


def silu(values):
    return values / (1.0 + jnp.exp(-values))


def stack3(cells, depth):
    count = cells.shape[1]
    lane = lax.broadcasted_iota(jnp.int32, cells.shape, 1) % depth
    wide = cells.astype(F32)
    below = jnp.where(lane == 0, 0.0, pltpu.roll(wide, 1, 1)).astype(BF16)
    above = jnp.where(lane == depth - 1, 0.0, pltpu.roll(wide, count - 1, 1)).astype(BF16)
    return jnp.concatenate([below, cells, above], axis=0)


def shifted_rows(cells, offset, depth):
    if offset == 0:
        return cells
    blank = jnp.zeros((cells.shape[0], depth), cells.dtype)
    if cells.shape[1] == depth:
        return blank
    if offset > 0:
        return jnp.concatenate([cells[:, depth:], blank], axis=1)
    return jnp.concatenate([blank, cells[:, :-depth]], axis=1)


def conv_planes(matrices, stacks, planes, outputs, depth):
    results = [None] * planes
    for place in range(planes + 2):
        first = max(0, place - planes + 1)
        last = min(2, place)
        rows = matrices[first * 3 * outputs : (last + 1) * 3 * outputs, :]
        terms = dot(rows, stacks[place])
        for tap_x in range(first, last + 1):
            for tap_y in range(3):
                begin = ((tap_x - first) * 3 + tap_y) * outputs
                term = shifted_rows(terms[begin : begin + outputs], tap_y - 1, depth)
                target = place - tap_x
                results[target] = term if results[target] is None else results[target] + term
    return results


def weight_planes(acc, grads, stacks, depth):
    planes = len(grads)
    outputs = grads[0].shape[0]
    rows = [
        jnp.concatenate([shifted_rows(grad, 1 - tap_y, depth) for tap_y in range(3)], axis=0)
        for grad in grads
    ]
    for tap_x in range(3):
        total = None
        for plane in range(planes):
            term = dot_cells(rows[plane], stacks[plane + tap_x])
            total = term if total is None else total + term
        acc[tap_x * 3 * outputs : (tap_x + 1) * 3 * outputs, :] = total


def pack(acc, target, base, rows):
    half = rows // 2
    target[base : base + rows, :] = acc[:, :128]
    target[base + rows : base + rows + half, :] = jnp.concatenate(
        [acc[:half, 128:], acc[half:, 128:]], axis=1
    )


def unpack(source, base, rows, out, scale):
    half = rows // 2
    outputs = rows // 9
    for pair in range(9):
        main = source[base + pair * outputs : base + (pair + 1) * outputs, :].astype(F32) * scale
        out[3 * pair] = main[:, :64]
        out[3 * pair + 1] = main[:, 64:]
    for piece in range(0, 9 * outputs, 8):
        row = piece if piece < half else piece - half
        tail = source[base + rows + row : base + rows + row + 8, :].astype(F32) * scale
        side = tail[:, :64] if piece < half else tail[:, 64:]
        out[3 * (piece // outputs) + 2, piece % outputs : piece % outputs + 8, :] = side


def halo_places():
    index = lax.axis_index("space")
    ends = lax.axis_size("space") - 1
    a_right = 1 - index % 2
    inside = jnp.logical_and(index > 0, index < ends)
    return a_right, inside


def ordered_halos(got_a, got_b):
    a_right, inside = halo_places()
    got_b = jnp.where(inside, got_b, jnp.zeros_like(got_b))
    left = jnp.where(a_right == 1, got_b, got_a)
    right = jnp.where(a_right == 1, got_a, got_b)
    return left, right


def swap_tables(count):
    table_a = [(i, i ^ 1) for i in range(count)]
    table_b = [(0, 0)]
    for i in range(1, count - 1, 2):
        table_b += [(i, i + 1), (i + 1, i)]
    table_b.append((count - 1, count - 1))
    return table_a, table_b


def halves(shape):
    return pltpu.VMEM(shape, BF16)


def join_rows(target, place, pieces, brick):
    index = lax.axis_index("filt")
    for slot, piece in enumerate(pieces):
        start = pl.multiple_of((index ^ slot) * brick, brick)
        target[place, :, pl.ds(start, brick)] = piece


def local(space, filt, volume, first_weight, second_weight, cotangent):
    channels, planes, brick_y, depth = volume.shape
    filters = second_weight.shape[1]
    table_a, table_b = swap_tables(space)
    fine_y = brick_y * filt
    low_y = fine_y // 2
    low_depth = depth // 2
    fine_cells = fine_y * depth
    low_cells = low_y * low_depth
    brick = brick_y * depth
    fine_scale = 1.0 / (planes * space * fine_cells) ** 0.5
    low_scale = 1.0 / (planes // 2 * space * low_cells) ** 0.5
    low_planes = planes // 2

    def swap_a(piece):
        return lax.ppermute(piece, "space", table_a)

    def swap_b(piece):
        return lax.ppermute(piece, "space", table_b)

    def both(table, slot):
        return [(i * filt + f, j * filt + (f ^ slot)) for i, j in table for f in range(filt)]

    def across(piece, table, slot):
        return lax.ppermute(piece, ("space", "filt"), both(table, slot))

    place = lax.axis_index("space")
    own_table = [(i, i) for i in range(space)]
    brick_rows = jnp.transpose(volume, (1, 0, 2, 3)).reshape(planes, channels, brick)
    odd = place % 2
    edge_a = jnp.where(odd == 1, brick_rows[0], brick_rows[planes - 1])
    edge_b = jnp.where(odd == 1, brick_rows[planes - 1], brick_rows[0])
    own = [brick_rows] + [across(brick_rows, own_table, slot) for slot in range(1, filt)]
    halo_a = [across(edge_a, table_a, slot) for slot in range(filt)]
    halo_b = [across(edge_b, table_b, slot) for slot in range(filt)]

    first_taps = first_weight.reshape(9, 3, channels, channels)
    first_forward = jnp.transpose(first_taps, (0, 2, 1, 3)).reshape(9 * channels, 3 * channels)
    first_back = jnp.transpose(first_taps[::-1, ::-1], (0, 3, 1, 2)).reshape(
        9 * channels, 3 * channels
    )
    second_taps = second_weight.reshape(9, 3, filters, channels)
    second_forward = jnp.transpose(second_taps, (0, 2, 1, 3)).reshape(9 * filters, 3 * channels)
    second_back = jnp.transpose(second_taps[::-1, ::-1], (0, 3, 1, 2)).reshape(
        9 * channels, 3 * filters
    )
    low_cot = cotangent.reshape(filters, low_cells)

    def first_kernel(*refs):
        own_refs = refs[:filt]
        a_refs = refs[filt : 2 * filt]
        b_refs = refs[2 * filt : 3 * filt]
        matrices, pooled_ref, slope_ref, whole_ref = refs[3 * filt : 3 * filt + 4]
        for plane in range(planes):
            join_rows(whole_ref, 1 + plane, [ref[plane] for ref in own_refs], brick)
        halos = [ordered_halos(a[...], b[...]) for a, b in zip(a_refs, b_refs)]
        join_rows(whole_ref, 0, [pair[0] for pair in halos], brick)
        join_rows(whole_ref, planes + 1, [pair[1] for pair in halos], brick)
        stacks = [stack3(whole_ref[p], depth) for p in range(planes + 2)]
        pre = conv_planes(matrices, stacks, planes, channels, depth)
        hidden = [silu(value).astype(BF16) for value in pre]
        for plane in range(planes):
            slope_ref[plane] = silu_slope(pre[plane])
        pairs = (
            lax.broadcasted_iota(jnp.int32, (depth, low_depth), 0) // 2
            == lax.broadcasted_iota(jnp.int32, (depth, low_depth), 1)
        ).astype(BF16)
        for plane in range(low_planes):
            for row in range(low_y):
                rows = jnp.concatenate(
                    [
                        hidden[2 * plane + x][:, (2 * row + y) * depth : (2 * row + y + 1) * depth]
                        for x in range(2)
                        for y in range(2)
                    ],
                    axis=0,
                )
                sums = dot(rows, pairs)
                total = sums[:channels]
                for piece in range(1, 4):
                    total = total + sums[piece * channels : (piece + 1) * channels]
                pooled_ref[:, row * low_depth : (row + 1) * low_depth] = (0.125 * total).astype(
                    BF16
                )

    pooled, slope, whole = call(
        first_kernel,
        (
            shaped((channels, low_cells), BF16),
            shaped((planes, channels, fine_cells), F32),
            shaped((planes + 2, channels, fine_cells), BF16),
        ),
        name="first_conv",
    )(*own, *halo_a, *halo_b, first_forward)

    pool_a, pool_b = swap_a(pooled), swap_b(pooled)

    def second_kernel(own_ref, a_ref, b_ref, matrices, cot_ref, out_ref, down_ref):
        left, right = ordered_halos(a_ref[...], b_ref[...])
        stacks = [stack3(value, low_depth) for value in (left, own_ref[...], right)]
        (pre,) = conv_planes(matrices, stacks, 1, filters, low_depth)
        out_ref[...] = silu(pre).astype(BF16)
        down_ref[...] = (cot_ref[...].astype(F32) * silu_slope(pre)).astype(BF16)

    features, down = call(
        second_kernel,
        (shaped((filters, low_cells), BF16), shaped((filters, low_cells), BF16)),
        name="second_conv",
    )(pooled, pool_a, pool_b, second_forward, low_cot)
    features = features.reshape(filters, 1, low_y, low_depth)

    down_a, down_b = swap_a(down), swap_b(down)

    first_rows, second_rows = 9 * channels, 9 * filters
    packed_first, packed_second = first_rows * 3 // 2, second_rows * 3 // 2
    second_side = space // 4
    unit = 16 * space
    total_rows = -(-(packed_first + packed_second) // unit) * unit
    quarter = total_rows // 4
    chunk = total_rows // space

    def second_weight_kernel(down_ref, own_ref, a_ref, b_ref, out_ref, acc):
        left, right = ordered_halos(a_ref[...], b_ref[...])
        stacks = [stack3(value, low_depth) for value in (left, own_ref[...], right)]
        weight_planes(acc, [down_ref[...]], stacks, low_depth)
        pack(acc, out_ref, 0, second_rows)

    second_part = call(
        second_weight_kernel,
        shaped((packed_second, 128), F32),
        (pltpu.VMEM((second_rows, 3 * channels), F32),),
        name="second_weight",
    )(down, pooled, pool_a, pool_b)

    def group_kernel(own_ref, a_ref, b_ref, matrices, out_ref):
        left, right = ordered_halos(a_ref[...], b_ref[...])
        stacks = [stack3(value, low_depth) for value in (left, own_ref[...], right)]
        (part,) = conv_planes(matrices, stacks, 1, channels, low_depth)
        out_ref[...] = part.astype(BF16)

    part = call(group_kernel, shaped((channels, low_cells), BF16), name="group_part")(
        down, down_a, down_b, second_back
    )
    parts = [part] + [
        lax.ppermute(part, "filt", [(f, f ^ slot) for f in range(filt)])
        for slot in range(1, filt)
    ]

    def grad_kernel(*refs):
        part_refs = refs[:filt]
        slope_ref, whole_ref, second_ref = refs[filt : filt + 3]
        down_ref, edge_a_ref, edge_b_ref = refs[filt + 3 : filt + 6]
        own_ref = refs[filt + 6]
        send_refs = refs[filt + 7 : filt + 10]
        acc, rows_ref = refs[filt + 10 :]
        spread = (
            lax.broadcasted_iota(jnp.int32, (low_depth, depth), 0)
            == lax.broadcasted_iota(jnp.int32, (low_depth, depth), 1) // 2
        ).astype(BF16)
        columns = []
        for row in range(low_y):
            wide = None
            for ref in part_refs:
                term = dot(ref[:, row * low_depth : (row + 1) * low_depth], spread)
                wide = term if wide is None else wide + term
            columns += [0.125 * wide] * 2
        hidden_grad = jnp.concatenate(columns, axis=1)
        grads = [(hidden_grad * slope_ref[p]).astype(BF16) for p in range(planes)]
        for plane in range(planes):
            down_ref[plane] = grads[plane]
        odd = lax.axis_index("space") % 2
        edge_a_ref[...] = jnp.where(odd == 1, grads[0], grads[planes - 1])
        edge_b_ref[...] = jnp.where(odd == 1, grads[planes - 1], grads[0])
        stacks = [stack3(whole_ref[p], depth) for p in range(planes + 2)]
        weight_planes(acc, grads, stacks, depth)
        pack(acc, rows_ref, 0, first_rows)
        rows_ref[packed_first : packed_first + packed_second, :] = second_ref[...]
        if total_rows > packed_first + packed_second:
            rows_ref[packed_first + packed_second :, :] = jnp.zeros(
                (total_rows - packed_first - packed_second, 128), F32
            )
        low = lax.axis_index("space") % 4
        own_ref[...] = rows_ref[pl.ds(pl.multiple_of(low * quarter, 16), quarter), :]
        for k in range(1, 4):
            start = pl.multiple_of((low ^ k) * quarter, 16)
            send_refs[k - 1][...] = rows_ref[pl.ds(start, quarter), :].astype(BF16)

    first_down, fine_edge_a, fine_edge_b, own_rows, *sends = call(
        grad_kernel,
        (
            shaped((planes, channels, fine_cells), BF16),
            shaped((channels, fine_cells), BF16),
            shaped((channels, fine_cells), BF16),
            shaped((quarter, 128), F32),
        )
        + (shaped((quarter, 128), BF16),) * 3,
        (
            pltpu.VMEM((first_rows, 3 * channels), F32),
            pltpu.VMEM((total_rows, 128), F32),
        ),
        name="first_weight",
    )(*parts, slope, whole, second_part)

    near = [[(i, i ^ k) for i in range(space)] for k in range(4)]
    far = [[(i, i ^ (4 * k)) for i in range(space)] for k in range(second_side)]
    got = [lax.ppermute(sends[k - 1], "space", near[k]) for k in range(1, 4)]
    down_halo_a, down_halo_b = swap_a(fine_edge_a), swap_b(fine_edge_b)

    def fold_kernel(own_ref, *refs):
        got_refs, out_refs, rows_ref = refs[:3], refs[3:-1], refs[-1]
        total = own_ref[...]
        for ref in got_refs:
            total = total + ref[...].astype(F32)
        rows_ref[...] = total
        high = lax.axis_index("space") // 4
        out_refs[0][...] = rows_ref[pl.ds(pl.multiple_of(high * chunk, 16), chunk), :]
        for k in range(1, second_side):
            start = pl.multiple_of((high ^ k) * chunk, 16)
            out_refs[k][...] = rows_ref[pl.ds(start, chunk), :].astype(BF16)

    own_chunk, *sends = call(
        fold_kernel,
        (shaped((chunk, 128), F32),) + (shaped((chunk, 128), BF16),) * (second_side - 1),
        (pltpu.VMEM((quarter, 128), F32),),
        name="fold_near",
    )(own_rows, *got)
    got = [lax.ppermute(sends[k - 1], "space", far[k]) for k in range(1, second_side)]

    def volume_kernel(own_ref, a_ref, b_ref, matrices, out_ref, rows_ref):
        left, right = ordered_halos(a_ref[...], b_ref[...])
        values = [left] + [own_ref[p] for p in range(planes)] + [right]
        blank = jnp.zeros((channels, depth), BF16)
        begin = pl.multiple_of(lax.axis_index("filt") * brick, brick)
        stacks = []
        for position, value in enumerate(values):
            rows_ref[position] = jnp.concatenate([blank, value, blank], axis=1)
            stacks.append(stack3(rows_ref[position, :, pl.ds(begin, brick + 2 * depth)], depth))
        results = conv_planes(matrices, stacks, planes, channels, depth)
        for plane in range(planes):
            out_ref[plane] = results[plane][:, depth : depth + brick].astype(BF16)

    volume_grad = call(
        volume_kernel,
        shaped((planes, channels, brick), BF16),
        (halves((planes + 2, channels, fine_cells + 2 * depth)),),
        name="volume_grad",
    )(first_down, down_halo_a, down_halo_b, first_back)
    volume_grad = jnp.transpose(
        volume_grad.reshape(planes, channels, brick_y, depth), (1, 0, 2, 3)
    )

    def sum_kernel(own_ref, *refs):
        total = own_ref[...]
        for ref in refs[:-1]:
            total = total + ref[...].astype(F32)
        refs[-1][...] = total.astype(BF16)

    final_chunk = call(sum_kernel, shaped((chunk, 128), BF16), name="fold_far")(own_chunk, *got)
    pieces = [final_chunk] + [
        lax.ppermute(final_chunk, "space", far[k]) for k in range(1, second_side)
    ]

    def join_kernel(*refs):
        high = lax.axis_index("space") // 4
        for k, ref in enumerate(refs[:-1]):
            refs[-1][pl.ds(pl.multiple_of((high ^ k) * chunk, 16), chunk), :] = ref[...]

    group = call(join_kernel, shaped((quarter, 128), BF16), name="join_far")(*pieces)
    pieces = [group] + [lax.ppermute(group, "space", near[k]) for k in range(1, 4)]

    def final_kernel(*refs):
        first_ref, second_ref, rows_ref = refs[4:]
        low = lax.axis_index("space") % 4
        for k, ref in enumerate(refs[:4]):
            rows_ref[pl.ds(pl.multiple_of((low ^ k) * quarter, 16), quarter), :] = ref[...].astype(
                F32
            )
        unpack(rows_ref, 0, first_rows, first_ref, fine_scale)
        unpack(rows_ref, packed_first, second_rows, second_ref, low_scale)

    first_grad, second_grad = call(
        final_kernel,
        (shaped((27, channels, channels), F32), shaped((27, filters, channels), F32)),
        (pltpu.VMEM((total_rows, 128), F32),),
        name="join_near",
    )(*pieces)
    return (features, volume_grad, first_grad, second_grad)


def solution(mesh):
    placed = (
        P(None, "space", "filt", None),
        P(),
        P(None, "filt", None),
        P("filt", "space", None, None),
    )
    return jax.shard_map(
        functools.partial(local, mesh.shape["space"], mesh.shape["filt"]),
        mesh=mesh,
        in_specs=placed,
        out_specs=(
            P("filt", "space", None, None),
            P(None, "space", "filt", None),
            P(),
            P(None, "filt", None),
        ),
        check_vma=False,
    )
```

time: 318 us -> 94.6 us (0.30)
  waiting for transfers between devices: 127 us -> 12.1 us
  local copies, waits for them, and re-layouts: 75.2 us -> 23 us
  Pallas kernels: 0 us -> 22.5 us
  starting transfers between devices: 53.8 us -> 35.3 us
  between operations: 16.3 us -> 0.97 us
  matrix products: 14.6 us -> 0 us
  other arithmetic: 14.5 us -> 0.11 us
  blocking collectives: 13.8 us -> 0 us
    psum x1 -> x0, waiting for transfers between devices: 119 us -> none  [local(): lax.psum(conv_weights(first_down, padded_in, fine_shape), ('space', 'filt'))]
    pallas_call x0 -> x10, Pallas kernels: none -> 22.5 us  [the longest x1 3.27 us: local(): call(grad_kernel, (shaped((planes, channels, fine_cells), BF16), shaped((...]
    unnamed x237 -> x67, local copies, waits for them, and re-layouts: 25.8 us -> 8.8 us
    dot_general x64 -> x0, matrix products: 14.6 us -> none  [the longest x27 6.28 us: conv_transpose(): jnp.dot(matrices, stacked, preferred_element_type=jnp.float32)]
    all_gather x1 -> x0, blocking collectives: 13.8 us -> none  [local(): whole_weight = lax.all_gather(second_weight, 'filt', axis=1, tiled=True)]
    reshape x70 -> x13, local copies, waits for them, and re-layouts: 23.6 us -> 10.9 us  [the longest x2 1.69 us: local(): volume_grad.reshape(planes, channels, brick_y, depth)]
    ppermute x16 -> x24, starting transfers between devices: 46.6 us -> 35.3 us  [the longest x3 11.1 us: swap_b(): return lax.ppermute(piece, 'space', table_b)]
    slice x10 -> x0, local copies, waits for them, and re-layouts: 10.8 us -> none  [the longest x2 5.82 us: window(): lax.slice(padded, (0, offset_x, offset_y, offset_z), (padded.shape[0], of...]
  transfers between devices with their start and end apart: 19 -> 24, of which waited for: 6 -> 5; matrix products, arithmetic and copies ran while one was open for 27% -> 15% of each run, Pallas kernels for 0% -> 7%
where the time goes in v1:
time: 94.6 us; the launch traced here: 93.9 us
  starting transfers between devices  35.3 us (37%)
  local copies, waits for them, and re-layouts  23 us (24%)
  Pallas kernels  22.5 us (24%)
  waiting for transfers between devices  12.1 us (13%)
  between operations  0.97 us (1%)
    ppermute x3, starting transfers between devices, swap_b(): return lax.ppermute(piece, 'space', table_b)  11.1 us
    unnamed x67, local copies, waits for them, and re-layouts  8.8 us
    ppermute x5, starting transfers between devices, across(): return lax.ppermute(piece, ('space', 'filt'), both(table, slot))  7.98 us
    ppermute x3, waiting for transfers between devices, local(): got = [lax.ppermute(sends[k - 1], 'space', near[k]) for k in range(1, 4)]  5.4 us
    ppermute x3, waiting for transfers between devices, local(): lax.ppermute(sends[k - 1], 'space', far[k])  4.72 us
    ppermute x3, starting transfers between devices, local(): lax.ppermute(sends[k - 1], 'space', far[k])  4.39 us
    ppermute x3, starting transfers between devices, local(): lax.ppermute(final_chunk, 'space', far[k])  3.55 us
    pallas_call x1, Pallas kernels, local(): call(grad_kernel, (shaped((planes, channels, fine_cells), BF16), shaped((...  3.27 us
  transfers between devices with their start and end apart: 24, of which 5 were waited for; matrix products, arithmetic and copies ran while one was open for 15% of the time, Pallas kernels for 7%

profile of v1, /device:TPU:1, one launch (start us, length us, event | category | flops | bytes accessed | tf_op | source)
XLA Modules:
  0.0 93.9 jit_solution(14466395769200910778)
XLA Ops:
  1.7 2.1 %collective-permute-start = (bf16[2,64,512]{2,1,0:T(8,128)(2,1)S(1)}, bf16[2,64,512]{2,1,0:T(8,128)(2,1)S(1)}, u32[]{:S(2)}, u32[]{:S(2)}) collective-permute-start(bf16[2,64,512]{2,1,0:T(8,128)(2,1)S(1)} %copy.22.refs_0_), channel_id=1, source_target_pairs={{0,1},{1,0},{2,3},{3,2},{4,5},{5,4},{6,7},{7,6},{8,9},{9,8},{10,11... | collective-permute-start | bytes 393224 | tf_op jit(solution)/shard_map/ppermute | solution.py:179
  5.2 3.5 %collective-permute-start.3 = (bf16[64,512]{1,0:T(8,128)(2,1)S(1)}, bf16[64,512]{1,0:T(8,128)(2,1)S(1)}, u32[]{:S(2)}, u32[]{:S(2)}) collective-permute-start(bf16[64,512]{1,0:T(8,128)(2,1)S(1)} %bitcast.46), channel_id=1, source_target_pairs={{0,0},{1,1},{2,4},{3,5},{4,2},{5,3},{6,8},{7,9},{8,6},{9,7},{10,12... | collective-permute-start | bytes 196616 | tf_op jit(solution)/shard_map/ppermute | solution.py:179
  8.7 1.2 %collective-permute-start.4 = (bf16[64,512]{1,0:T(8,128)(2,1)S(1)}, bf16[64,512]{1,0:T(8,128)(2,1)S(1)}, u32[]{:S(2)}, u32[]{:S(2)}) collective-permute-start(bf16[64,512]{1,0:T(8,128)(2,1)S(1)} %bitcast.47), channel_id=1, source_target_pairs={{0,1},{1,0},{2,5},{3,4},{4,3},{5,2},{6,9},{7,8},{8,7},{9,6},{10,13... | collective-permute-start | bytes 196616 | tf_op jit(solution)/shard_map/ppermute | solution.py:179
  11.4 2.0 %collective-permute-done.4.refs_5_ = bf16[64,512]{1,0:T(8,128)(2,1)S(1)} collective-permute-done((bf16[64,512]{1,0:T(8,128)(2,1)S(1)}, bf16[64,512]{1,0:T(8,128)(2,1)S(1)}, u32[]{:S(2)}, u32[]{:S(2)}) %collective-permute-start.4) | collective-permute-done | bytes 65568 | tf_op jit(solution)/shard_map/ppermute | solution.py:179
  14.6 3.2 %first_conv.1 = (bf16[64,256]{1,0:T(8,128)(2,1)}, f32[2,64,1024]{2,1,0:T(8,128)}, bf16[4,64,1024]{2,1,0:T(8,128)(2,1)}) custom-call(bf16[2,64,512]{2,1,0:T(8,128)(2,1)} %copy-done.2, bf16[2,64,512]{2,1,0:T(8,128)(2,1)} %copy-done.4, bf16[64,512]{1,0:T(8,128)(2,1)} %copy-done.15, bf16[64,512]{1,0:T(8,128)(2,1)} %copy-done.16, bf16[64,512]{1,0:T(8,128)(2,1)} %copy-done.17, ...), custom_call_target="tpu_custom_call" | custom-call | tf_op jit(solution)/shard_map/first_conv/pallas_call | solution.py:240
  17.8 4.4 %collective-permute-start.6 = (bf16[64,256]{1,0:T(8,128)(2,1)}, bf16[64,256]{1,0:T(8,128)(2,1)S(1)}, u32[]{:S(2)}, u32[]{:S(2)}) collective-permute-start(bf16[64,256]{1,0:T(8,128)(2,1)} %get-tuple-element.22.own_ref), channel_id=1, source_target_pairs={{0,0},{2,4},{4,2},{6,8},{8,6},{10,12},{12,10},{14,16},{16,14},{18,... | collective-permute-start | bytes 98312 | tf_op jit(solution)/shard_map/ppermute | solution.py:173
  25.0 1.9 %second_conv.1 = (bf16[64,256]{1,0:T(8,128)(2,1)}, bf16[64,256]{1,0:T(8,128)(2,1)}) custom-call(bf16[64,256]{1,0:T(8,128)(2,1)} %get-tuple-element.22.own_ref, bf16[64,256]{1,0:T(8,128)(2,1)} %copy-done.5, bf16[64,256]{1,0:T(8,128)(2,1)} %copy-done.6, bf16[576,192]{1,0:T(8,128)(2,1)} %reshape.50.matrices, bf16[64,256]{1,0:T(8,128)(2,1)} %bitcast.43), custom_call_target="tpu_custom_call" | custom-call | tf_op jit(solution)/shard_map/second_conv/pallas_call | solution.py:259
  26.9 4.2 %collective-permute-start.8 = (bf16[64,256]{1,0:T(8,128)(2,1)}, bf16[64,256]{1,0:T(8,128)(2,1)S(1)}, u32[]{:S(2)}, u32[]{:S(2)}) collective-permute-start(bf16[64,256]{1,0:T(8,128)(2,1)} %get-tuple-element.24.own_ref.down_ref), channel_id=1, source_target_pairs={{0,0},{2,4},{4,2},{6,8},{8,6},{10,12},{12,10},{14,16},{16,14},{18,... | collective-permute-start | bytes 98312 | tf_op jit(solution)/shard_map/ppermute | solution.py:173
  31.1 1.2 %copy.18 = bf16[9,3,64,64]{2,1,3,0:T(4,128)(2,1)S(1)} copy(bf16[9,3,64,64]{3,2,1,0:T(8,128)(2,1)S(1)} %bitcast.35) | data formatting | bytes 442368 | tf_op jit(solution)/shard_map/reshape | solution.py:196
  32.4 1.6 %rev.6 = bf16[9,3,64,64]{2,1,3,0:T(4,128)(2,1)S(1)} reverse(bf16[9,3,64,64]{2,1,3,0:T(4,128)(2,1)S(1)} %copy.18), dimensions={0,1} | reverse | bytes 442368 | tf_op jit(solution)/shard_map/rev | solution.py:198
  36.3 1.9 %group_part.1.refs_0_ = bf16[64,256]{1,0:T(8,128)(2,1)} custom-call(bf16[64,256]{1,0:T(8,128)(2,1)} %get-tuple-element.24.own_ref.down_ref, bf16[64,256]{1,0:T(8,128)(2,1)} %copy-done.22, bf16[64,256]{1,0:T(8,128)(2,1)} %copy-done.23, bf16[576,192]{1,0:T(8,128)(2,1)} %reshape.53.matrices), custom_call_target="tpu_custom_call" | custom-call | tf_op jit(solution)/shard_map/group_part/pallas_call | solution.py:295
  38.3 1.2 %collective-permute-start.9 = (bf16[64,256]{1,0:T(8,128)(2,1)}, bf16[64,256]{1,0:T(8,128)(2,1)S(1)}, u32[]{:S(2)}, u32[]{:S(2)}) collective-permute-start(bf16[64,256]{1,0:T(8,128)(2,1)} %group_part.1.refs_0_), channel_id=1, source_target_pairs={{0,1},{1,0},{2,3},{3,2},{4,5},{5,4},{6,7},{7,6},{8,9},{9,8},{10,11... | collective-permute-start | bytes 98312 | tf_op jit(solution)/shard_map/ppermute | solution.py:299
  39.5 2.0 %second_weight.1.refs_4_ = f32[864,128]{1,0:T(8,128)} custom-call(bf16[64,256]{1,0:T(8,128)(2,1)} %get-tuple-element.24.own_ref.down_ref, bf16[64,256]{1,0:T(8,128)(2,1)} %get-tuple-element.22.own_ref, bf16[64,256]{1,0:T(8,128)(2,1)} %copy-done.5, bf16[64,256]{1,0:T(8,128)(2,1)} %copy-done.6), custom_call_target="tpu_custom_call" | custom-call | tf_op jit(solution)/shard_map/second_weight/pallas_call | solution.py:282
  42.1 3.3 %first_weight.1 = (bf16[2,64,1024]{2,1,0:T(8,128)(2,1)}, bf16[64,1024]{1,0:T(8,128)(2,1)}, bf16[64,1024]{1,0:T(8,128)(2,1)}, f32[448,128]{1,0:T(8,128)}, bf16[44...) custom-call(bf16[64,256]{1,0:T(8,128)(2,1)} %group_part.1.refs_0_, ...), custom_call_target="tpu_custom_call" | custom-call | tf_op jit(solution)/shard_map/first_weight/pallas_call | solution.py:342
  46.4 1.1 %collective-permute-start.14 = (bf16[448,128]{1,0:T(8,128)(2,1)}, bf16[448,128]{1,0:T(8,128)(2,1)S(1)}, u32[]{:S(2)}, u32[]{:S(2)}) collective-permute-start(bf16[448,128]{1,0:T(8,128)(2,1)} %get-tuple-element.33), channel_id=1, source_target_pairs={{0,6},{2,4},{4,2},{6,0},{8,14},{10,12},{12,10},{14,8},{16,22},{18,... | collective-permute-start | bytes 344072 | tf_op jit(solution)/shard_map/ppermute | solution.py:360
  47.5 2.3 %collective-permute-done.13.refs_1_ = bf16[448,128]{1,0:T(8,128)(2,1)S(1)} collective-permute-done((bf16[448,128]{1,0:T(8,128)(2,1)}, bf16[448,128]{1,0:T(8,128)(2,1)S(1)}, u32[]{:S(2)}, u32[]{:S(2)}) %collective-permute-start.13) | collective-permute-done | bytes 114720 | tf_op jit(solution)/shard_map/ppermute | solution.py:360
  49.8 3.1 %collective-permute-done.14.refs_2_ = bf16[448,128]{1,0:T(8,128)(2,1)S(1)} collective-permute-done((bf16[448,128]{1,0:T(8,128)(2,1)}, bf16[448,128]{1,0:T(8,128)(2,1)S(1)}, u32[]{:S(2)}, u32[]{:S(2)}) %collective-permute-start.14) | collective-permute-done | bytes 114720 | tf_op jit(solution)/shard_map/ppermute | solution.py:360
  53.6 1.9 %fold_near.1 = (f32[112,128]{1,0:T(8,128)}, bf16[112,128]{1,0:T(8,128)(2,1)}, bf16[112,128]{1,0:T(8,128)(2,1)}, bf16[112,128]{1,0:T(8,128)(2,1)}) custom-call(f32[448,128]{1,0:T(8,128)} %get-tuple-element.30.own_ref, bf16[448,128]{1,0:T(8,128)(2,1)} %copy-done.12, bf16[448,128]{1,0:T(8,128)(2,1)} %copy-done.13, bf16[448,128]{1,0:T(8,128)(2,1)} %copy-done.14), custom_call_target="tpu_custom_call" | custom-call | tf_op jit(solution)/shard_map/fold_near/pallas_call | solution.py:375
  55.5 2.1 %collective-permute-start.15 = (bf16[112,128]{1,0:T(8,128)(2,1)}, bf16[112,128]{1,0:T(8,128)(2,1)S(1)}, u32[]{:S(2)}, u32[]{:S(2)}) collective-permute-start(bf16[112,128]{1,0:T(8,128)(2,1)} %get-tuple-element.35), channel_id=1, source_target_pairs={{0,8},{2,10},{4,12},{6,14},{8,0},{10,2},{12,4},{14,6},{16,24},{18,... | collective-permute-start | bytes 86024 | tf_op jit(solution)/shard_map/ppermute | solution.py:381
  57.5 2.3 %collective-permute-start.16 = (bf16[112,128]{1,0:T(8,128)(2,1)}, bf16[112,128]{1,0:T(8,128)(2,1)S(1)}, u32[]{:S(2)}, u32[]{:S(2)}) collective-permute-start(bf16[112,128]{1,0:T(8,128)(2,1)} %get-tuple-element.36), channel_id=1, source_target_pairs={{0,16},{2,18},{4,20},{6,22},{8,24},{10,26},{12,28},{14,30},{16,0},... | collective-permute-start | bytes 86024 | tf_op jit(solution)/shard_map/ppermute | solution.py:381
  59.9 1.8 %collective-permute-done.16.refs_1_ = bf16[112,128]{1,0:T(8,128)(2,1)S(1)} collective-permute-done((bf16[112,128]{1,0:T(8,128)(2,1)}, bf16[112,128]{1,0:T(8,128)(2,1)S(1)}, u32[]{:S(2)}, u32[]{:S(2)}) %collective-permute-start.16) | collective-permute-done | bytes 28704 | tf_op jit(solution)/shard_map/ppermute | solution.py:381
  61.7 2.9 %collective-permute-done.17.refs_2_ = bf16[112,128]{1,0:T(8,128)(2,1)S(1)} collective-permute-done((bf16[112,128]{1,0:T(8,128)(2,1)}, bf16[112,128]{1,0:T(8,128)(2,1)S(1)}, u32[]{:S(2)}, u32[]{:S(2)}) %collective-permute-start.17) | collective-permute-done | bytes 28704 | tf_op jit(solution)/shard_map/ppermute | solution.py:381
  65.2 1.5 %fold_far.1.refs_0_ = bf16[112,128]{1,0:T(8,128)(2,1)} custom-call(f32[112,128]{1,0:T(8,128)} %get-tuple-element.34.own_ref, bf16[112,128]{1,0:T(8,128)(2,1)} %copy-done.27, bf16[112,128]{1,0:T(8,128)(2,1)} %copy-done.28, bf16[112,128]{1,0:T(8,128)(2,1)} %copy-done.29), custom_call_target="tpu_custom_call" | custom-call | tf_op jit(solution)/shard_map/fold_far/pallas_call | solution.py:412
  67.3 2.9 %collective-permute-start.20 = (bf16[112,128]{1,0:T(8,128)(2,1)}, bf16[112,128]{1,0:T(8,128)(2,1)S(1)}, u32[]{:S(2)}, u32[]{:S(2)}) collective-permute-start(bf16[112,128]{1,0:T(8,128)(2,1)} %fold_far.1.refs_0_), channel_id=1, source_target_pairs={{0,24},{2,26},{4,28},{6,30},{8,16},{10,18},{12,20},{14,22},{16,8},... | collective-permute-start | bytes 86024 | tf_op jit(solution)/shard_map/ppermute | solution.py:414
  70.2 2.8 %collective-permute-start.10 = (bf16[64,1024]{1,0:T(8,128)(2,1)S(1)}, bf16[64,1024]{1,0:T(8,128)(2,1)S(1)}, u32[]{:S(2)}, u32[]{:S(2)}) collective-permute-start(bf16[64,1024]{1,0:T(8,128)(2,1)S(1)} %copy-done.31), channel_id=1, source_target_pairs={{0,2},{2,0},{4,6},{6,4},{8,10},{10,8},{12,14},{14,12},{16,18},{18,... | collective-permute-start | bytes 393224 | tf_op jit(solution)/shard_map/ppermute | solution.py:170
  73.0 2.4 %collective-permute-start.11 = (bf16[64,1024]{1,0:T(8,128)(2,1)S(1)}, bf16[64,1024]{1,0:T(8,128)(2,1)S(1)}, u32[]{:S(2)}, u32[]{:S(2)}) collective-permute-start(bf16[64,1024]{1,0:T(8,128)(2,1)S(1)} %copy-done.30), channel_id=1, source_target_pairs={{0,0},{2,4},{4,2},{6,8},{8,6},{10,12},{12,10},{14,16},{16,14},{18,... | collective-permute-start | bytes 393224 | tf_op jit(solution)/shard_map/ppermute | solution.py:173
  76.7 1.5 %join_far.1.refs_0_ = bf16[448,128]{1,0:T(8,128)(2,1)} custom-call(bf16[112,128]{1,0:T(8,128)(2,1)} %fold_far.1.refs_0_, bf16[112,128]{1,0:T(8,128)(2,1)} %copy-done.24, bf16[112,128]{1,0:T(8,128)(2,1)} %copy-done.25, bf16[112,128]{1,0:T(8,128)(2,1)} %copy-done.26), custom_call_target="tpu_custom_call" | custom-call | tf_op jit(solution)/shard_map/join_far/pallas_call | solution.py:422
  78.1 1.3 %collective-permute-start.22 = (bf16[448,128]{1,0:T(8,128)(2,1)}, bf16[448,128]{1,0:T(8,128)(2,1)S(1)}, u32[]{:S(2)}, u32[]{:S(2)}) collective-permute-start(bf16[448,128]{1,0:T(8,128)(2,1)} %join_far.1.refs_0_), channel_id=1, source_target_pairs={{0,4},{2,6},{4,0},{6,2},{8,12},{10,14},{12,8},{14,10},{16,20},{18,... | collective-permute-start | bytes 344072 | tf_op jit(solution)/shard_map/ppermute | solution.py:423
  80.3 1.2 %copy.19 = bf16[9,3,64,64]{2,1,3,0:T(4,128)(2,1)S(1)} copy(bf16[9,3,64,64]{3,2,1,0:T(8,128)(2,1)S(1)} %bitcast.37) | data formatting | bytes 442368 | tf_op jit(solution)/shard_map/reshape | solution.py:191
  81.5 1.6 %rev.7 = bf16[9,3,64,64]{2,1,3,0:T(4,128)(2,1)S(1)} reverse(bf16[9,3,64,64]{2,1,3,0:T(4,128)(2,1)S(1)} %copy.19), dimensions={0,1} | reverse | bytes 442368 | tf_op jit(solution)/shard_map/rev | solution.py:193
  85.6 2.8 %volume_grad.1 = bf16[2,64,512]{2,1,0:T(8,128)(2,1)} custom-call(bf16[2,64,1024]{2,1,0:T(8,128)(2,1)} %get-tuple-element.27.own_ref, bf16[64,1024]{1,0:T(8,128)(2,1)} %copy-done.7, bf16[64,1024]{1,0:T(8,128)(2,1)} %copy-done.8, bf16[576,192]{1,0:T(8,128)(2,1)} %reshape.54.matrices), custom_call_target="tpu_custom_call" | custom-call | tf_op jit(solution)/shard_map/volume_grad/pallas_call | solution.py:396
  91.4 2.6 %join_near.1 = (f32[27,64,64]{2,1,0:T(8,128)}, f32[27,64,64]{2,1,0:T(8,128)}) custom-call(bf16[448,128]{1,0:T(8,128)(2,1)} %join_far.1.refs_0_, bf16[448,128]{1,0:T(8,128)(2,1)} %copy-done.9, bf16[448,128]{1,0:T(8,128)(2,1)} %copy-done.10, bf16[448,128]{1,0:T(8,128)(2,1)} %copy-done.11), custom_call_target="tpu_custom_call" | custom-call | tf_op jit(solution)/shard_map/join_near/pallas_call | solution.py:435
  (109 shorter events, 21.2 us)
Async XLA Ops:
  0.6 3.2 %copy-start.3 = (bf16[64,2,2,256]{3,2,1,0:T(2,128)(2,1)S(1)}, bf16[64,2,2,256]{3,2,1,0:T(2,128)(2,1)}, u32[]{:S(2)}) copy-start(bf16[64,2,2,256]{3,2,1,0:T(2,128)(2,1)} %param.4) | copy-start | bytes 393220
  1.7 8.2 %copy-start.1 = (bf16[27,64,64]{2,1,0:T(8,128)(2,1)S(1)}, bf16[27,64,64]{2,1,0:T(8,128)(2,1)}, u32[]{:S(2)}) copy-start(bf16[27,64,64]{2,1,0:T(8,128)(2,1)} %param.5) | copy-start | bytes 663556
  1.7 11.6 %collective-permute-start = (bf16[2,64,512]{2,1,0:T(8,128)(2,1)S(1)}, bf16[2,64,512]{2,1,0:T(8,128)(2,1)S(1)}, u32[]{:S(2)}, u32[]{:S(2)}) collective-permute-start(bf16[2,64,512]{2,1,0:T(8,128)(2,1)S(1)} %copy.22.refs_0_), channel_id=1, source_target_pairs={{0,1},{1,0},{2,3},{3,2},{4,5},{5,4},{6,7},{7,6},{8,9},{9,8},{10,11... | collective-permute-start | bytes 393224 | tf_op jit(solution)/shard_map/ppermute | solution.py:179
  4.0 7.4 %collective-permute-start.1 = (bf16[64,512]{1,0:T(8,128)(2,1)S(1)}, bf16[64,512]{1,0:T(8,128)(2,1)S(1)}, u32[]{:S(2)}, u32[]{:S(2)}) collective-permute-start(bf16[64,512]{1,0:T(8,128)(2,1)S(1)} %bitcast.44), channel_id=1, source_target_pairs={{0,2},{1,3},{2,0},{3,1},{4,6},{5,7},{6,4},{7,5},{8,10},{9,11},{10,... | collective-permute-start | bytes 196616 | tf_op jit(solution)/shard_map/ppermute | solution.py:179
  5.0 6.4 %collective-permute-start.2 = (bf16[64,512]{1,0:T(8,128)(2,1)S(1)}, bf16[64,512]{1,0:T(8,128)(2,1)S(1)}, u32[]{:S(2)}, u32[]{:S(2)}) collective-permute-start(bf16[64,512]{1,0:T(8,128)(2,1)S(1)} %bitcast.45), channel_id=1, source_target_pairs={{0,3},{1,2},{2,1},{3,0},{4,7},{5,6},{6,5},{7,4},{8,11},{9,10},{10,... | collective-permute-start | bytes 196616 | tf_op jit(solution)/shard_map/ppermute | solution.py:179
  5.2 6.2 %collective-permute-start.3 = (bf16[64,512]{1,0:T(8,128)(2,1)S(1)}, bf16[64,512]{1,0:T(8,128)(2,1)S(1)}, u32[]{:S(2)}, u32[]{:S(2)}) collective-permute-start(bf16[64,512]{1,0:T(8,128)(2,1)S(1)} %bitcast.46), channel_id=1, source_target_pairs={{0,0},{1,1},{2,4},{3,5},{4,2},{5,3},{6,8},{7,9},{8,6},{9,7},{10,12... | collective-permute-start | bytes 196616 | tf_op jit(solution)/shard_map/ppermute | solution.py:179
  8.7 4.7 %collective-permute-start.4 = (bf16[64,512]{1,0:T(8,128)(2,1)S(1)}, bf16[64,512]{1,0:T(8,128)(2,1)S(1)}, u32[]{:S(2)}, u32[]{:S(2)}) collective-permute-start(bf16[64,512]{1,0:T(8,128)(2,1)S(1)} %bitcast.47), channel_id=1, source_target_pairs={{0,1},{1,0},{2,5},{3,4},{4,3},{5,2},{6,9},{7,8},{8,7},{9,6},{10,13... | collective-permute-start | bytes 196616 | tf_op jit(solution)/shard_map/ppermute | solution.py:179
  11.4 10.9 %copy-start = (bf16[27,64,64]{2,1,0:T(8,128)(2,1)S(1)}, bf16[27,64,64]{2,1,0:T(8,128)(2,1)}, u32[]{:S(2)}) copy-start(bf16[27,64,64]{2,1,0:T(8,128)(2,1)} %param.6) | copy-start | bytes 663556
  17.8 6.5 %collective-permute-start.5 = (bf16[64,256]{1,0:T(8,128)(2,1)}, bf16[64,256]{1,0:T(8,128)(2,1)S(1)}, u32[]{:S(2)}, u32[]{:S(2)}) collective-permute-start(bf16[64,256]{1,0:T(8,128)(2,1)} %get-tuple-element.22.own_ref), channel_id=1, source_target_pairs={{0,2},{2,0},{4,6},{6,4},{8,10},{10,8},{12,14},{14,12},{16,18},{18,... | collective-permute-start | bytes 98312 | tf_op jit(solution)/shard_map/ppermute | solution.py:170
  17.8 6.6 %collective-permute-start.6 = (bf16[64,256]{1,0:T(8,128)(2,1)}, bf16[64,256]{1,0:T(8,128)(2,1)S(1)}, u32[]{:S(2)}, u32[]{:S(2)}) collective-permute-start(bf16[64,256]{1,0:T(8,128)(2,1)} %get-tuple-element.22.own_ref), channel_id=1, source_target_pairs={{0,0},{2,4},{4,2},{6,8},{8,6},{10,12},{12,10},{14,16},{16,14},{18,... | collective-permute-start | bytes 98312 | tf_op jit(solution)/shard_map/ppermute | solution.py:173
  26.9 8.2 %collective-permute-start.7 = (bf16[64,256]{1,0:T(8,128)(2,1)}, bf16[64,256]{1,0:T(8,128)(2,1)S(1)}, u32[]{:S(2)}, u32[]{:S(2)}) collective-permute-start(bf16[64,256]{1,0:T(8,128)(2,1)} %get-tuple-element.24.own_ref.down_ref), channel_id=1, source_target_pairs={{0,2},{2,0},{4,6},{6,4},{8,10},{10,8},{12,14},{14,12},{16,18},{18,... | collective-permute-start | bytes 98312 | tf_op jit(solution)/shard_map/ppermute | solution.py:170
  26.9 8.2 %collective-permute-start.8 = (bf16[64,256]{1,0:T(8,128)(2,1)}, bf16[64,256]{1,0:T(8,128)(2,1)S(1)}, u32[]{:S(2)}, u32[]{:S(2)}) collective-permute-start(bf16[64,256]{1,0:T(8,128)(2,1)} %get-tuple-element.24.own_ref.down_ref), channel_id=1, source_target_pairs={{0,0},{2,4},{4,2},{6,8},{8,6},{10,12},{12,10},{14,16},{16,14},{18,... | collective-permute-start | bytes 98312 | tf_op jit(solution)/shard_map/ppermute | solution.py:173
  38.3 3.2 %collective-permute-start.9 = (bf16[64,256]{1,0:T(8,128)(2,1)}, bf16[64,256]{1,0:T(8,128)(2,1)S(1)}, u32[]{:S(2)}, u32[]{:S(2)}) collective-permute-start(bf16[64,256]{1,0:T(8,128)(2,1)} %group_part.1.refs_0_), channel_id=1, source_target_pairs={{0,1},{1,0},{2,3},{3,2},{4,5},{5,4},{6,7},{7,6},{8,9},{9,8},{10,11... | collective-permute-start | bytes 98312 | tf_op jit(solution)/shard_map/ppermute | solution.py:299
  45.4 2.1 %collective-permute-start.12 = (bf16[448,128]{1,0:T(8,128)(2,1)}, bf16[448,128]{1,0:T(8,128)(2,1)S(1)}, u32[]{:S(2)}, u32[]{:S(2)}) collective-permute-start(bf16[448,128]{1,0:T(8,128)(2,1)} %get-tuple-element.31), channel_id=1, source_target_pairs={{0,2},{2,0},{4,6},{6,4},{8,10},{10,8},{12,14},{14,12},{16,18},{18,... | collective-permute-start | bytes 344072 | tf_op jit(solution)/shard_map/ppermute | solution.py:360
  45.4 4.4 %collective-permute-start.13 = (bf16[448,128]{1,0:T(8,128)(2,1)}, bf16[448,128]{1,0:T(8,128)(2,1)S(1)}, u32[]{:S(2)}, u32[]{:S(2)}) collective-permute-start(bf16[448,128]{1,0:T(8,128)(2,1)} %get-tuple-element.32), channel_id=1, source_target_pairs={{0,4},{2,6},{4,0},{6,2},{8,12},{10,14},{12,8},{14,10},{16,20},{18,... | collective-permute-start | bytes 344072 | tf_op jit(solution)/shard_map/ppermute | solution.py:360
  46.4 6.5 %collective-permute-start.14 = (bf16[448,128]{1,0:T(8,128)(2,1)}, bf16[448,128]{1,0:T(8,128)(2,1)S(1)}, u32[]{:S(2)}, u32[]{:S(2)}) collective-permute-start(bf16[448,128]{1,0:T(8,128)(2,1)} %get-tuple-element.33), channel_id=1, source_target_pairs={{0,6},{2,4},{4,2},{6,0},{8,14},{10,12},{12,10},{14,8},{16,22},{18,... | collective-permute-start | bytes 344072 | tf_op jit(solution)/shard_map/ppermute | solution.py:360
  47.5 5.4 %copy-start.12 = (bf16[448,128]{1,0:T(8,128)(2,1)}, bf16[448,128]{1,0:T(8,128)(2,1)S(1)}, u32[]{:S(2)}) copy-start(bf16[448,128]{1,0:T(8,128)(2,1)S(1)} %collective-permute-done.12.refs_0_) | copy-start | bytes 344068
  49.8 3.1 %copy-start.13 = (bf16[448,128]{1,0:T(8,128)(2,1)}, bf16[448,128]{1,0:T(8,128)(2,1)S(1)}, u32[]{:S(2)}) copy-start(bf16[448,128]{1,0:T(8,128)(2,1)S(1)} %collective-permute-done.13.refs_1_) | copy-start | bytes 344068
  53.6 16.6 %copy-start.31 = (bf16[64,1024]{1,0:T(8,128)(2,1)S(1)}, bf16[64,1024]{1,0:T(8,128)(2,1)}, u32[]{:S(2)}) copy-start(bf16[64,1024]{1,0:T(8,128)(2,1)} %get-tuple-element.28) | copy-start | bytes 393220
  55.5 17.5 %copy-start.30 = (bf16[64,1024]{1,0:T(8,128)(2,1)S(1)}, bf16[64,1024]{1,0:T(8,128)(2,1)}, u32[]{:S(2)}) copy-start(bf16[64,1024]{1,0:T(8,128)(2,1)} %get-tuple-element.29) | copy-start | bytes 393220
  55.5 4.4 %collective-permute-start.15 = (bf16[112,128]{1,0:T(8,128)(2,1)}, bf16[112,128]{1,0:T(8,128)(2,1)S(1)}, u32[]{:S(2)}, u32[]{:S(2)}) collective-permute-start(bf16[112,128]{1,0:T(8,128)(2,1)} %get-tuple-element.35), channel_id=1, source_target_pairs={{0,8},{2,10},{4,12},{6,14},{8,0},{10,2},{12,4},{14,6},{16,24},{18,... | collective-permute-start | bytes 86024 | tf_op jit(solution)/shard_map/ppermute | solution.py:381
  57.5 4.1 %collective-permute-start.16 = (bf16[112,128]{1,0:T(8,128)(2,1)}, bf16[112,128]{1,0:T(8,128)(2,1)S(1)}, u32[]{:S(2)}, u32[]{:S(2)}) collective-permute-start(bf16[112,128]{1,0:T(8,128)(2,1)} %get-tuple-element.36), channel_id=1, source_target_pairs={{0,16},{2,18},{4,20},{6,22},{8,24},{10,26},{12,28},{14,30},{16,0},... | collective-permute-start | bytes 86024 | tf_op jit(solution)/shard_map/ppermute | solution.py:381
  59.9 4.7 %collective-permute-start.17 = (bf16[112,128]{1,0:T(8,128)(2,1)}, bf16[112,128]{1,0:T(8,128)(2,1)S(1)}, u32[]{:S(2)}, u32[]{:S(2)}) collective-permute-start(bf16[112,128]{1,0:T(8,128)(2,1)} %get-tuple-element.37), channel_id=1, source_target_pairs={{0,24},{2,26},{4,28},{6,30},{8,16},{10,18},{12,20},{14,22},{16,8},... | collective-permute-start | bytes 86024 | tf_op jit(solution)/shard_map/ppermute | solution.py:381
  59.9 4.7 %copy-start.27 = (bf16[112,128]{1,0:T(8,128)(2,1)}, bf16[112,128]{1,0:T(8,128)(2,1)S(1)}, u32[]{:S(2)}) copy-start(bf16[112,128]{1,0:T(8,128)(2,1)S(1)} %collective-permute-done.15.refs_0_) | copy-start | bytes 86020
  66.7 8.8 %collective-permute-start.18 = (bf16[112,128]{1,0:T(8,128)(2,1)}, bf16[112,128]{1,0:T(8,128)(2,1)S(1)}, u32[]{:S(2)}, u32[]{:S(2)}) collective-permute-start(bf16[112,128]{1,0:T(8,128)(2,1)} %fold_far.1.refs_0_), channel_id=1, source_target_pairs={{0,8},{2,10},{4,12},{6,14},{8,0},{10,2},{12,4},{14,6},{16,24},{18,... | collective-permute-start | bytes 86024 | tf_op jit(solution)/shard_map/ppermute | solution.py:414
  66.7 8.8 %collective-permute-start.19 = (bf16[112,128]{1,0:T(8,128)(2,1)}, bf16[112,128]{1,0:T(8,128)(2,1)S(1)}, u32[]{:S(2)}, u32[]{:S(2)}) collective-permute-start(bf16[112,128]{1,0:T(8,128)(2,1)} %fold_far.1.refs_0_), channel_id=1, source_target_pairs={{0,16},{2,18},{4,20},{6,22},{8,24},{10,26},{12,28},{14,30},{16,0},... | collective-permute-start | bytes 86024 | tf_op jit(solution)/shard_map/ppermute | solution.py:414
  67.3 8.1 %collective-permute-start.20 = (bf16[112,128]{1,0:T(8,128)(2,1)}, bf16[112,128]{1,0:T(8,128)(2,1)S(1)}, u32[]{:S(2)}, u32[]{:S(2)}) collective-permute-start(bf16[112,128]{1,0:T(8,128)(2,1)} %fold_far.1.refs_0_), channel_id=1, source_target_pairs={{0,24},{2,26},{4,28},{6,30},{8,16},{10,18},{12,20},{14,22},{16,8},... | collective-permute-start | bytes 86024 | tf_op jit(solution)/shard_map/ppermute | solution.py:414
  70.2 14.7 %collective-permute-start.10 = (bf16[64,1024]{1,0:T(8,128)(2,1)S(1)}, bf16[64,1024]{1,0:T(8,128)(2,1)S(1)}, u32[]{:S(2)}, u32[]{:S(2)}) collective-permute-start(bf16[64,1024]{1,0:T(8,128)(2,1)S(1)} %copy-done.31), channel_id=1, source_target_pairs={{0,2},{2,0},{4,6},{6,4},{8,10},{10,8},{12,14},{14,12},{16,18},{18,... | collective-permute-start | bytes 393224 | tf_op jit(solution)/shard_map/ppermute | solution.py:170
  73.0 11.9 %collective-permute-start.11 = (bf16[64,1024]{1,0:T(8,128)(2,1)S(1)}, bf16[64,1024]{1,0:T(8,128)(2,1)S(1)}, u32[]{:S(2)}, u32[]{:S(2)}) collective-permute-start(bf16[64,1024]{1,0:T(8,128)(2,1)S(1)} %copy-done.30), channel_id=1, source_target_pairs={{0,0},{2,4},{4,2},{6,8},{8,6},{10,12},{12,10},{14,16},{16,14},{18,... | collective-permute-start | bytes 393224 | tf_op jit(solution)/shard_map/ppermute | solution.py:173
  78.1 11.9 %collective-permute-start.21 = (bf16[448,128]{1,0:T(8,128)(2,1)}, bf16[448,128]{1,0:T(8,128)(2,1)S(1)}, u32[]{:S(2)}, u32[]{:S(2)}) collective-permute-start(bf16[448,128]{1,0:T(8,128)(2,1)} %join_far.1.refs_0_), channel_id=1, source_target_pairs={{0,2},{2,0},{4,6},{6,4},{8,10},{10,8},{12,14},{14,12},{16,18},{18,... | collective-permute-start | bytes 344072 | tf_op jit(solution)/shard_map/ppermute | solution.py:423
  78.1 11.9 %collective-permute-start.22 = (bf16[448,128]{1,0:T(8,128)(2,1)}, bf16[448,128]{1,0:T(8,128)(2,1)S(1)}, u32[]{:S(2)}, u32[]{:S(2)}) collective-permute-start(bf16[448,128]{1,0:T(8,128)(2,1)} %join_far.1.refs_0_), channel_id=1, source_target_pairs={{0,4},{2,6},{4,0},{6,2},{8,12},{10,14},{12,8},{14,10},{16,20},{18,... | collective-permute-start | bytes 344072 | tf_op jit(solution)/shard_map/ppermute | solution.py:423
  79.5 10.6 %collective-permute-start.23 = (bf16[448,128]{1,0:T(8,128)(2,1)}, bf16[448,128]{1,0:T(8,128)(2,1)S(1)}, u32[]{:S(2)}, u32[]{:S(2)}) collective-permute-start(bf16[448,128]{1,0:T(8,128)(2,1)} %join_far.1.refs_0_), channel_id=1, source_target_pairs={{0,6},{2,4},{4,2},{6,0},{8,14},{10,12},{12,10},{14,8},{16,22},{18,... | collective-permute-start | bytes 344072 | tf_op jit(solution)/shard_map/ppermute | solution.py:423
  (24 other events, 24.0 us)

commit v2 on v1

--- a/solution.py
+++ b/solution.py
@@ -13,17 +13,23 @@
 
 
 def call(body, outs, scratch=(), name=None):
-    return pl.pallas_call(
-        body,
-        out_shape=outs,
-        scratch_shapes=scratch,
-        name=name,
-        compiler_params=pltpu.CompilerParams(vmem_limit_bytes=VMEM_LIMIT),
-    )
+    def run(*args):
+        kernel = pl.pallas_call(
+            body,
+            out_shape=outs,
+            in_specs=[pl.BlockSpec(memory_space=pltpu.VMEM)] * len(args),
+            out_specs=jax.tree.map(lambda _: pl.BlockSpec(memory_space=pltpu.VMEM), outs),
+            scratch_shapes=scratch,
+            name=name,
+            compiler_params=pltpu.CompilerParams(vmem_limit_bytes=VMEM_LIMIT),
+        )
+        return kernel(*[pltpu.with_memory_space_constraint(arg, pltpu.VMEM) for arg in args])
+
+    return run
 
 
 def shaped(shape, dtype):
-    return jax.ShapeDtypeStruct(shape, dtype)
+    return pltpu.VMEM(shape, dtype)
 
 
 def dot(lhs, rhs):

time: 94.6 us -> 69.8 us (0.74)
  Pallas kernels: 22.5 us -> 4.81 us
  local copies, waits for them, and re-layouts: 23 us -> 12.7 us
  waiting for transfers between devices: 12.1 us -> 14.9 us
    pallas_call x10, Pallas kernels: 22.5 us -> 4.81 us  [run(): kernel(*[pltpu.with_memory_space_constraint(arg, pltpu.VMEM) for arg in a...]
    unnamed x67 -> x15, local copies, waits for them, and re-layouts: 8.8 us -> 2.28 us
    ppermute x1, waiting for transfers between devices: 0.01 us -> 1.11 us  [local(): lax.ppermute(part, 'filt', [(f, f ^ slot) for f in range(filt)])]
  transfers between devices with their start and end apart: 24 -> 24, of which waited for: 5 -> 8; matrix products, arithmetic and copies ran while one was open for 15% -> 14% of each run, Pallas kernels for 7% -> 2%
where the time goes in v2:
time: 69.8 us; the launch traced here: 69.6 us
  starting transfers between devices  36.1 us (52%)
  waiting for transfers between devices  14.9 us (21%)
  local copies, waits for them, and re-layouts  12.7 us (18%)
  Pallas kernels  4.81 us (7%)
  between operations  0.96 us (1%)
    ppermute x3, starting transfers between devices, swap_b(): return lax.ppermute(piece, 'space', table_b)  11.4 us
    ppermute x5, starting transfers between devices, across(): return lax.ppermute(piece, ('space', 'filt'), both(table, slot))  7.98 us
    ppermute x3, waiting for transfers between devices, local(): got = [lax.ppermute(sends[k - 1], 'space', near[k]) for k in range(1, 4)]  5.26 us
    pallas_call x10, Pallas kernels, run(): kernel(*[pltpu.with_memory_space_constraint(arg, pltpu.VMEM) for arg in a...  4.81 us
    ppermute x3, starting transfers between devices, local(): lax.ppermute(sends[k - 1], 'space', far[k])  4.66 us
    ppermute x3, waiting for transfers between devices, local(): lax.ppermute(sends[k - 1], 'space', far[k])  4.51 us
    ppermute x3, starting transfers between devices, local(): lax.ppermute(final_chunk, 'space', far[k])  3.6 us
    ppermute x3, starting transfers between devices, swap_a(): return lax.ppermute(piece, 'space', table_a)  2.84 us
  transfers between devices with their start and end apart: 24, of which 8 were waited for; matrix products, arithmetic and copies ran while one was open for 14% of the time, Pallas kernels for 2%

profile of v2, /device:TPU:1, one launch (start us, length us, event | category | flops | bytes accessed | tf_op | source)
XLA Modules:
  0.0 69.6 jit_solution(15326274588314529747)
XLA Ops:
  0.6 1.1 %reshape.56 = bf16[2,64,512]{2,0,1:T(2,128)(2,1)S(1)} reshape(bf16[2,64,2,256]{3,2,0,1:T(2,128)(2,1)} %bitcast.39) | data formatting | bytes 262144 | tf_op jit(solution)/shard_map/reshape | solution.py:189
  1.7 2.1 %collective-permute-start = (bf16[2,64,512]{2,1,0:T(8,128)(2,1)S(1)}, bf16[2,64,512]{2,1,0:T(8,128)(2,1)S(1)}, u32[]{:S(2)}, u32[]{:S(2)}) collective-permute-start(bf16[2,64,512]{2,1,0:T(8,128)(2,1)S(1)} %copy.22.refs_0_), channel_id=1, source_target_pairs={{0,1},{1,0},{2,3},{3,2},{4,5},{5,4},{6,7},{7,6},{8,9},{9,8},{10,11... | collective-permute-start | bytes 393224 | tf_op jit(solution)/shard_map/ppermute | solution.py:185
  4.0 1.0 %collective-permute-start.1 = (bf16[64,512]{1,0:T(8,128)(2,1)S(1)}, bf16[64,512]{1,0:T(8,128)(2,1)S(1)}, u32[]{:S(2)}, u32[]{:S(2)}) collective-permute-start(bf16[64,512]{1,0:T(8,128)(2,1)S(1)} %bitcast.44), channel_id=1, source_target_pairs={{0,2},{1,3},{2,0},{3,1},{4,6},{5,7},{6,4},{7,5},{8,10},{9,11},{10,... | collective-permute-start | bytes 196616 | tf_op jit(solution)/shard_map/ppermute | solution.py:185
  5.0 3.7 %collective-permute-start.3 = (bf16[64,512]{1,0:T(8,128)(2,1)S(1)}, bf16[64,512]{1,0:T(8,128)(2,1)S(1)}, u32[]{:S(2)}, u32[]{:S(2)}) collective-permute-start(bf16[64,512]{1,0:T(8,128)(2,1)S(1)} %bitcast.46), channel_id=1, source_target_pairs={{0,0},{1,1},{2,4},{3,5},{4,2},{5,3},{6,8},{7,9},{8,6},{9,7},{10,12... | collective-permute-start | bytes 196616 | tf_op jit(solution)/shard_map/ppermute | solution.py:185
  8.7 1.2 %collective-permute-start.4 = (bf16[64,512]{1,0:T(8,128)(2,1)S(1)}, bf16[64,512]{1,0:T(8,128)(2,1)S(1)}, u32[]{:S(2)}, u32[]{:S(2)}) collective-permute-start(bf16[64,512]{1,0:T(8,128)(2,1)S(1)} %bitcast.47), channel_id=1, source_target_pairs={{0,1},{1,0},{2,5},{3,4},{4,3},{5,2},{6,9},{7,8},{8,7},{9,6},{10,13... | collective-permute-start | bytes 196616 | tf_op jit(solution)/shard_map/ppermute | solution.py:185
  10.7 2.7 %collective-permute-done.4.refs_5_ = bf16[64,512]{1,0:T(8,128)(2,1)S(1)} collective-permute-done((bf16[64,512]{1,0:T(8,128)(2,1)S(1)}, bf16[64,512]{1,0:T(8,128)(2,1)S(1)}, u32[]{:S(2)}, u32[]{:S(2)}) %collective-permute-start.4) | collective-permute-done | bytes 65568 | tf_op jit(solution)/shard_map/ppermute | solution.py:185
  13.3 1.2 %first_conv.1 = (bf16[64,256]{1,0:T(8,128)(2,1)S(1)}, f32[2,64,1024]{2,1,0:T(8,128)S(1)}, bf16[4,64,1024]{2,1,0:T(8,128)(2,1)S(1)}) custom-call(bf16[2,64,512]{2,1,0:T(8,128)(2,1)S(1)} %copy.22.refs_0_, bf16[2,64,512]{2,1,0:T(8,128)(2,1)S(1)} %collective-permute-done.refs_1_, bf16[64,512]{1,0:T(8,128)(2,1)S(1)} %collective-permute-done.1.refs_2_, ...), custom_call_target="tpu_custom_call" | custom-call | tf_op jit(solution)/shard_map/first_conv/pallas_call | solution.py:26
  14.6 4.4 %collective-permute-start.6 = (bf16[64,256]{1,0:T(8,128)(2,1)S(1)}, bf16[64,256]{1,0:T(8,128)(2,1)S(1)}, u32[]{:S(2)}, u32[]{:S(2)}) collective-permute-start(bf16[64,256]{1,0:T(8,128)(2,1)S(1)} %get-tuple-element.22.own_ref), channel_id=1, source_target_pairs={{0,0},{2,4},{4,2},{6,8},{8,6},{10,12},{12,10},{14,16},{16,14},{18,... | collective-permute-start | bytes 98312 | tf_op jit(solution)/shard_map/ppermute | solution.py:179
  21.0 4.5 %collective-permute-start.8 = (bf16[64,256]{1,0:T(8,128)(2,1)S(1)}, bf16[64,256]{1,0:T(8,128)(2,1)S(1)}, u32[]{:S(2)}, u32[]{:S(2)}) collective-permute-start(bf16[64,256]{1,0:T(8,128)(2,1)S(1)} %get-tuple-element.24.own_ref.down_ref), channel_id=1, source_target_pairs={{0,0},{2,4},{4,2},{6,8},{8,6},{10,12},{12,10},{14,16},{16,14},{18,... | collective-permute-start | bytes 98312 | tf_op jit(solution)/shard_map/ppermute | solution.py:179
  25.6 1.2 %copy.18 = bf16[9,3,64,64]{2,1,3,0:T(4,128)(2,1)S(1)} copy(bf16[9,3,64,64]{3,2,1,0:T(8,128)(2,1)S(1)} %bitcast.36) | data formatting | bytes 442368 | tf_op jit(solution)/shard_map/reshape | solution.py:202
  26.8 1.6 %rev.6 = bf16[9,3,64,64]{2,1,3,0:T(4,128)(2,1)S(1)} reverse(bf16[9,3,64,64]{2,1,3,0:T(4,128)(2,1)S(1)} %copy.18), dimensions={0,1} | reverse | bytes 442368 | tf_op jit(solution)/shard_map/rev | solution.py:204
  29.1 1.3 %collective-permute-start.9 = (bf16[64,256]{1,0:T(8,128)(2,1)S(1)}, bf16[64,256]{1,0:T(8,128)(2,1)S(1)}, u32[]{:S(2)}, u32[]{:S(2)}) collective-permute-start(bf16[64,256]{1,0:T(8,128)(2,1)S(1)} %group_part.1.refs_0_), channel_id=1, source_target_pairs={{0,1},{1,0},{2,3},{3,2},{4,5},{5,4},{6,7},{7,6},{8,9},{9,8},{10,11... | collective-permute-start | bytes 98312 | tf_op jit(solution)/shard_map/ppermute | solution.py:305
  30.9 1.1 %collective-permute-done.9.refs_1_ = bf16[64,256]{1,0:T(8,128)(2,1)S(1)} collective-permute-done((bf16[64,256]{1,0:T(8,128)(2,1)S(1)}, bf16[64,256]{1,0:T(8,128)(2,1)S(1)}, u32[]{:S(2)}, u32[]{:S(2)}) %collective-permute-start.9) | collective-permute-done | bytes 32800 | tf_op jit(solution)/shard_map/ppermute | solution.py:305
  32.0 1.1 %first_weight.1 = (bf16[2,64,1024]{2,1,0:T(8,128)(2,1)S(1)}, bf16[64,1024]{1,0:T(8,128)(2,1)S(1)}, bf16[64,1024]{1,0:T(8,128)(2,1)S(1)}, f32[448,128]{1,0:T(8,12...) custom-call(bf16[64,256]{1,0:T(8,128)(2,1)S(1)} %group_part.1.refs_0_, ...), custom_call_target="tpu_custom_call" | custom-call | tf_op jit(solution)/shard_map/first_weight/pallas_call | solution.py:26
  33.2 1.3 %collective-permute-start.13 = (bf16[448,128]{1,0:T(8,128)(2,1)S(1)}, bf16[448,128]{1,0:T(8,128)(2,1)S(1)}, u32[]{:S(2)}, u32[]{:S(2)}) collective-permute-start(bf16[448,128]{1,0:T(8,128)(2,1)S(1)} %get-tuple-element.32), channel_id=1, source_target_pairs={{0,4},{2,6},{4,0},{6,2},{8,12},{10,14},{12,8},{14,10},{16,20},{18,... | collective-permute-start | bytes 344072 | tf_op jit(solution)/shard_map/ppermute | solution.py:366
  34.5 0.8 %collective-permute-start.14 = (bf16[448,128]{1,0:T(8,128)(2,1)S(1)}, bf16[448,128]{1,0:T(8,128)(2,1)S(1)}, u32[]{:S(2)}, u32[]{:S(2)}) collective-permute-start(bf16[448,128]{1,0:T(8,128)(2,1)S(1)} %get-tuple-element.33), channel_id=1, source_target_pairs={{0,6},{2,4},{4,2},{6,0},{8,14},{10,12},{12,10},{14,8},{16,22},{18,... | collective-permute-start | bytes 344072 | tf_op jit(solution)/shard_map/ppermute | solution.py:366
  35.3 2.2 %collective-permute-done.13.refs_1_ = bf16[448,128]{1,0:T(8,128)(2,1)S(1)} collective-permute-done((bf16[448,128]{1,0:T(8,128)(2,1)S(1)}, bf16[448,128]{1,0:T(8,128)(2,1)S(1)}, u32[]{:S(2)}, u32[]{:S(2)}) %collective-permute-start.13) | collective-permute-done | bytes 114720 | tf_op jit(solution)/shard_map/ppermute | solution.py:366
  37.5 3.1 %collective-permute-done.14.refs_2_ = bf16[448,128]{1,0:T(8,128)(2,1)S(1)} collective-permute-done((bf16[448,128]{1,0:T(8,128)(2,1)S(1)}, bf16[448,128]{1,0:T(8,128)(2,1)S(1)}, u32[]{:S(2)}, u32[]{:S(2)}) %collective-permute-start.14) | collective-permute-done | bytes 114720 | tf_op jit(solution)/shard_map/ppermute | solution.py:366
  40.7 2.3 %collective-permute-start.15 = (bf16[112,128]{1,0:T(8,128)(2,1)S(1)}, bf16[112,128]{1,0:T(8,128)(2,1)S(1)}, u32[]{:S(2)}, u32[]{:S(2)}) collective-permute-start(bf16[112,128]{1,0:T(8,128)(2,1)S(1)} %get-tuple-element.35), channel_id=1, source_target_pairs={{0,8},{2,10},{4,12},{6,14},{8,0},{10,2},{12,4},{14,6},{16,24},{18,... | collective-permute-start | bytes 86024 | tf_op jit(solution)/shard_map/ppermute | solution.py:387
  43.0 2.3 %collective-permute-start.16 = (bf16[112,128]{1,0:T(8,128)(2,1)S(1)}, bf16[112,128]{1,0:T(8,128)(2,1)S(1)}, u32[]{:S(2)}, u32[]{:S(2)}) collective-permute-start(bf16[112,128]{1,0:T(8,128)(2,1)S(1)} %get-tuple-element.36), channel_id=1, source_target_pairs={{0,16},{2,18},{4,20},{6,22},{8,24},{10,26},{12,28},{14,30},{16,0},... | collective-permute-start | bytes 86024 | tf_op jit(solution)/shard_map/ppermute | solution.py:387
  45.3 1.6 %collective-permute-done.16.refs_1_ = bf16[112,128]{1,0:T(8,128)(2,1)S(1)} collective-permute-done((bf16[112,128]{1,0:T(8,128)(2,1)S(1)}, bf16[112,128]{1,0:T(8,128)(2,1)S(1)}, u32[]{:S(2)}, u32[]{:S(2)}) %collective-permute-start.16) | collective-permute-done | bytes 28704 | tf_op jit(solution)/shard_map/ppermute | solution.py:387
  47.0 2.9 %collective-permute-done.17.refs_2_ = bf16[112,128]{1,0:T(8,128)(2,1)S(1)} collective-permute-done((bf16[112,128]{1,0:T(8,128)(2,1)S(1)}, bf16[112,128]{1,0:T(8,128)(2,1)S(1)}, u32[]{:S(2)}, u32[]{:S(2)}) %collective-permute-start.17) | collective-permute-done | bytes 28704 | tf_op jit(solution)/shard_map/ppermute | solution.py:387
  50.6 2.9 %collective-permute-start.20 = (bf16[112,128]{1,0:T(8,128)(2,1)S(1)}, bf16[112,128]{1,0:T(8,128)(2,1)S(1)}, u32[]{:S(2)}, u32[]{:S(2)}) collective-permute-start(bf16[112,128]{1,0:T(8,128)(2,1)S(1)} %fold_far.1.refs_0_), channel_id=1, source_target_pairs={{0,24},{2,26},{4,28},{6,30},{8,16},{10,18},{12,20},{14,22},{16,8},... | collective-permute-start | bytes 86024 | tf_op jit(solution)/shard_map/ppermute | solution.py:420
  53.5 2.7 %collective-permute-start.10 = (bf16[64,1024]{1,0:T(8,128)(2,1)S(1)}, bf16[64,1024]{1,0:T(8,128)(2,1)S(1)}, u32[]{:S(2)}, u32[]{:S(2)}) collective-permute-start(bf16[64,1024]{1,0:T(8,128)(2,1)S(1)} %get-tuple-element.28), channel_id=1, source_target_pairs={{0,2},{2,0},{4,6},{6,4},{8,10},{10,8},{12,14},{14,12},{16,18},{18,... | collective-permute-start | bytes 393224 | tf_op jit(solution)/shard_map/ppermute | solution.py:176
  56.2 2.4 %collective-permute-start.11 = (bf16[64,1024]{1,0:T(8,128)(2,1)S(1)}, bf16[64,1024]{1,0:T(8,128)(2,1)S(1)}, u32[]{:S(2)}, u32[]{:S(2)}) collective-permute-start(bf16[64,1024]{1,0:T(8,128)(2,1)S(1)} %get-tuple-element.29), channel_id=1, source_target_pairs={{0,0},{2,4},{4,2},{6,8},{8,6},{10,12},{12,10},{14,16},{16,14},{18,... | collective-permute-start | bytes 393224 | tf_op jit(solution)/shard_map/ppermute | solution.py:179
  58.7 1.4 %collective-permute-start.22 = (bf16[448,128]{1,0:T(8,128)(2,1)S(1)}, bf16[448,128]{1,0:T(8,128)(2,1)S(1)}, u32[]{:S(2)}, u32[]{:S(2)}) collective-permute-start(bf16[448,128]{1,0:T(8,128)(2,1)S(1)} %join_far.1.refs_0_), channel_id=1, source_target_pairs={{0,4},{2,6},{4,0},{6,2},{8,12},{10,14},{12,8},{14,10},{16,20},{18,... | collective-permute-start | bytes 344072 | tf_op jit(solution)/shard_map/ppermute | solution.py:429
  60.9 1.2 %copy.19 = bf16[9,3,64,64]{2,1,3,0:T(4,128)(2,1)S(1)} copy(bf16[9,3,64,64]{3,2,1,0:T(8,128)(2,1)S(1)} %bitcast.38) | data formatting | bytes 442368 | tf_op jit(solution)/shard_map/reshape | solution.py:197
  62.1 1.6 %rev.7 = bf16[9,3,64,64]{2,1,3,0:T(4,128)(2,1)S(1)} reverse(bf16[9,3,64,64]{2,1,3,0:T(4,128)(2,1)S(1)} %copy.19), dimensions={0,1} | reverse | bytes 442368 | tf_op jit(solution)/shard_map/rev | solution.py:199
  64.7 0.9 %volume_grad.1 = bf16[2,64,512]{2,1,0:T(8,128)(2,1)S(1)} custom-call(bf16[2,64,1024]{2,1,0:T(8,128)(2,1)S(1)} %get-tuple-element.27.own_ref, bf16[64,1024]{1,0:T(8,128)(2,1)S(1)} %collective-permute-done.10.a_ref, bf16[64,1024]{1,0:T(8,128)(2,1)S(1)} %collective-permute-done.11.b_ref, bf16[576,192]{1,0:T(8,128)(2,1)S(1)} %reshape.54.matrices), custom_call_target="tpu_custom_call" | custom-call | tf_op jit(solution)/shard_map/volume_grad/pallas_call | solution.py:26
  66.5 0.9 %collective-permute-done.23.refs_3_ = bf16[448,128]{1,0:T(8,128)(2,1)S(1)} collective-permute-done((bf16[448,128]{1,0:T(8,128)(2,1)S(1)}, bf16[448,128]{1,0:T(8,128)(2,1)S(1)}, u32[]{:S(2)}, u32[]{:S(2)}) %collective-permute-start.23) | collective-permute-done | bytes 114720 | tf_op jit(solution)/shard_map/ppermute | solution.py:429
  67.7 0.9 %copy.34 = f32[27,64,64]{2,1,0:T(8,128)} copy(f32[27,64,64]{2,1,0:T(8,128)S(1)} %get-tuple-element.52) | data formatting | bytes 884736
  68.7 0.9 %copy.35 = f32[27,64,64]{2,1,0:T(8,128)} copy(f32[27,64,64]{2,1,0:T(8,128)S(1)} %get-tuple-element.53) | data formatting | bytes 884736
  (57 shorter events, 8.0 us)
Async XLA Ops:
  0.6 3.2 %copy-start.3 = (bf16[64,2,2,256]{3,2,1,0:T(2,128)(2,1)S(1)}, bf16[64,2,2,256]{3,2,1,0:T(2,128)(2,1)}, u32[]{:S(2)}) copy-start(bf16[64,2,2,256]{3,2,1,0:T(2,128)(2,1)} %param.4) | copy-start | bytes 393220
  1.7 8.2 %copy-start.1 = (bf16[27,64,64]{2,1,0:T(8,128)(2,1)S(1)}, bf16[27,64,64]{2,1,0:T(8,128)(2,1)}, u32[]{:S(2)}) copy-start(bf16[27,64,64]{2,1,0:T(8,128)(2,1)} %param.5) | copy-start | bytes 663556
  1.7 11.6 %collective-permute-start = (bf16[2,64,512]{2,1,0:T(8,128)(2,1)S(1)}, bf16[2,64,512]{2,1,0:T(8,128)(2,1)S(1)}, u32[]{:S(2)}, u32[]{:S(2)}) collective-permute-start(bf16[2,64,512]{2,1,0:T(8,128)(2,1)S(1)} %copy.22.refs_0_), channel_id=1, source_target_pairs={{0,1},{1,0},{2,3},{3,2},{4,5},{5,4},{6,7},{7,6},{8,9},{9,8},{10,11... | collective-permute-start | bytes 393224 | tf_op jit(solution)/shard_map/ppermute | solution.py:185
  4.0 6.7 %collective-permute-start.1 = (bf16[64,512]{1,0:T(8,128)(2,1)S(1)}, bf16[64,512]{1,0:T(8,128)(2,1)S(1)}, u32[]{:S(2)}, u32[]{:S(2)}) collective-permute-start(bf16[64,512]{1,0:T(8,128)(2,1)S(1)} %bitcast.44), channel_id=1, source_target_pairs={{0,2},{1,3},{2,0},{3,1},{4,6},{5,7},{6,4},{7,5},{8,10},{9,11},{10,... | collective-permute-start | bytes 196616 | tf_op jit(solution)/shard_map/ppermute | solution.py:185
  5.0 5.7 %collective-permute-start.2 = (bf16[64,512]{1,0:T(8,128)(2,1)S(1)}, bf16[64,512]{1,0:T(8,128)(2,1)S(1)}, u32[]{:S(2)}, u32[]{:S(2)}) collective-permute-start(bf16[64,512]{1,0:T(8,128)(2,1)S(1)} %bitcast.45), channel_id=1, source_target_pairs={{0,3},{1,2},{2,1},{3,0},{4,7},{5,6},{6,5},{7,4},{8,11},{9,10},{10,... | collective-permute-start | bytes 196616 | tf_op jit(solution)/shard_map/ppermute | solution.py:185
  5.0 5.6 %collective-permute-start.3 = (bf16[64,512]{1,0:T(8,128)(2,1)S(1)}, bf16[64,512]{1,0:T(8,128)(2,1)S(1)}, u32[]{:S(2)}, u32[]{:S(2)}) collective-permute-start(bf16[64,512]{1,0:T(8,128)(2,1)S(1)} %bitcast.46), channel_id=1, source_target_pairs={{0,0},{1,1},{2,4},{3,5},{4,2},{5,3},{6,8},{7,9},{8,6},{9,7},{10,12... | collective-permute-start | bytes 196616 | tf_op jit(solution)/shard_map/ppermute | solution.py:185
  8.7 4.7 %collective-permute-start.4 = (bf16[64,512]{1,0:T(8,128)(2,1)S(1)}, bf16[64,512]{1,0:T(8,128)(2,1)S(1)}, u32[]{:S(2)}, u32[]{:S(2)}) collective-permute-start(bf16[64,512]{1,0:T(8,128)(2,1)S(1)} %bitcast.47), channel_id=1, source_target_pairs={{0,1},{1,0},{2,5},{3,4},{4,3},{5,2},{6,9},{7,8},{8,7},{9,6},{10,13... | collective-permute-start | bytes 196616 | tf_op jit(solution)/shard_map/ppermute | solution.py:185
  10.6 8.4 %copy-start = (bf16[27,64,64]{2,1,0:T(8,128)(2,1)S(1)}, bf16[27,64,64]{2,1,0:T(8,128)(2,1)}, u32[]{:S(2)}) copy-start(bf16[27,64,64]{2,1,0:T(8,128)(2,1)} %param.6) | copy-start | bytes 663556
  14.5 5.7 %collective-permute-start.5 = (bf16[64,256]{1,0:T(8,128)(2,1)S(1)}, bf16[64,256]{1,0:T(8,128)(2,1)S(1)}, u32[]{:S(2)}, u32[]{:S(2)}) collective-permute-start(bf16[64,256]{1,0:T(8,128)(2,1)S(1)} %get-tuple-element.22.own_ref), channel_id=1, source_target_pairs={{0,2},{2,0},{4,6},{6,4},{8,10},{10,8},{12,14},{14,12},{16,18},{18,... | collective-permute-start | bytes 98312 | tf_op jit(solution)/shard_map/ppermute | solution.py:176
  14.6 6.0 %collective-permute-start.6 = (bf16[64,256]{1,0:T(8,128)(2,1)S(1)}, bf16[64,256]{1,0:T(8,128)(2,1)S(1)}, u32[]{:S(2)}, u32[]{:S(2)}) collective-permute-start(bf16[64,256]{1,0:T(8,128)(2,1)S(1)} %get-tuple-element.22.own_ref), channel_id=1, source_target_pairs={{0,0},{2,4},{4,2},{6,8},{8,6},{10,12},{12,10},{14,16},{16,14},{18,... | collective-permute-start | bytes 98312 | tf_op jit(solution)/shard_map/ppermute | solution.py:179
  19.4 0.8 %copy-start.4 = (bf16[64,1,2,128]{3,2,1,0:T(2,128)(2,1)S(1)}, bf16[64,1,2,128]{3,2,1,0:T(2,128)(2,1)}, u32[]{:S(2)}) copy-start(bf16[64,1,2,128]{3,2,1,0:T(2,128)(2,1)} %param.7) | copy-start | bytes 98308
  20.9 7.9 %collective-permute-start.7 = (bf16[64,256]{1,0:T(8,128)(2,1)S(1)}, bf16[64,256]{1,0:T(8,128)(2,1)S(1)}, u32[]{:S(2)}, u32[]{:S(2)}) collective-permute-start(bf16[64,256]{1,0:T(8,128)(2,1)S(1)} %get-tuple-element.24.own_ref.down_ref), channel_id=1, source_target_pairs={{0,2},{2,0},{4,6},{6,4},{8,10},{10,8},{12,14},{14,12},{16,18},{18,... | collective-permute-start | bytes 98312 | tf_op jit(solution)/shard_map/ppermute | solution.py:176
  21.0 7.8 %collective-permute-start.8 = (bf16[64,256]{1,0:T(8,128)(2,1)S(1)}, bf16[64,256]{1,0:T(8,128)(2,1)S(1)}, u32[]{:S(2)}, u32[]{:S(2)}) collective-permute-start(bf16[64,256]{1,0:T(8,128)(2,1)S(1)} %get-tuple-element.24.own_ref.down_ref), channel_id=1, source_target_pairs={{0,0},{2,4},{4,2},{6,8},{8,6},{10,12},{12,10},{14,16},{16,14},{18,... | collective-permute-start | bytes 98312 | tf_op jit(solution)/shard_map/ppermute | solution.py:179
  29.1 2.8 %collective-permute-start.9 = (bf16[64,256]{1,0:T(8,128)(2,1)S(1)}, bf16[64,256]{1,0:T(8,128)(2,1)S(1)}, u32[]{:S(2)}, u32[]{:S(2)}) collective-permute-start(bf16[64,256]{1,0:T(8,128)(2,1)S(1)} %group_part.1.refs_0_), channel_id=1, source_target_pairs={{0,1},{1,0},{2,3},{3,2},{4,5},{5,4},{6,7},{7,6},{8,9},{9,8},{10,11... | collective-permute-start | bytes 98312 | tf_op jit(solution)/shard_map/ppermute | solution.py:305
  33.1 2.2 %collective-permute-start.12 = (bf16[448,128]{1,0:T(8,128)(2,1)S(1)}, bf16[448,128]{1,0:T(8,128)(2,1)S(1)}, u32[]{:S(2)}, u32[]{:S(2)}) collective-permute-start(bf16[448,128]{1,0:T(8,128)(2,1)S(1)} %get-tuple-element.31), channel_id=1, source_target_pairs={{0,2},{2,0},{4,6},{6,4},{8,10},{10,8},{12,14},{14,12},{16,18},{18,... | collective-permute-start | bytes 344072 | tf_op jit(solution)/shard_map/ppermute | solution.py:366
  33.2 4.3 %collective-permute-start.13 = (bf16[448,128]{1,0:T(8,128)(2,1)S(1)}, bf16[448,128]{1,0:T(8,128)(2,1)S(1)}, u32[]{:S(2)}, u32[]{:S(2)}) collective-permute-start(bf16[448,128]{1,0:T(8,128)(2,1)S(1)} %get-tuple-element.32), channel_id=1, source_target_pairs={{0,4},{2,6},{4,0},{6,2},{8,12},{10,14},{12,8},{14,10},{16,20},{18,... | collective-permute-start | bytes 344072 | tf_op jit(solution)/shard_map/ppermute | solution.py:366
  34.5 6.1 %collective-permute-start.14 = (bf16[448,128]{1,0:T(8,128)(2,1)S(1)}, bf16[448,128]{1,0:T(8,128)(2,1)S(1)}, u32[]{:S(2)}, u32[]{:S(2)}) collective-permute-start(bf16[448,128]{1,0:T(8,128)(2,1)S(1)} %get-tuple-element.33), channel_id=1, source_target_pairs={{0,6},{2,4},{4,2},{6,0},{8,14},{10,12},{12,10},{14,8},{16,22},{18,... | collective-permute-start | bytes 344072 | tf_op jit(solution)/shard_map/ppermute | solution.py:366
  40.6 20.3 %copy-start.2 = (bf16[27,64,64]{2,1,0:T(8,128)(2,1)S(1)}, bf16[27,64,64]{2,1,0:T(8,128)(2,1)}, u32[]{:S(2)}) copy-start(bf16[27,64,64]{2,1,0:T(8,128)(2,1)} %param.5) | copy-start | bytes 663556
  40.7 4.7 %collective-permute-start.15 = (bf16[112,128]{1,0:T(8,128)(2,1)S(1)}, bf16[112,128]{1,0:T(8,128)(2,1)S(1)}, u32[]{:S(2)}, u32[]{:S(2)}) collective-permute-start(bf16[112,128]{1,0:T(8,128)(2,1)S(1)} %get-tuple-element.35), channel_id=1, source_target_pairs={{0,8},{2,10},{4,12},{6,14},{8,0},{10,2},{12,4},{14,6},{16,24},{18,... | collective-permute-start | bytes 86024 | tf_op jit(solution)/shard_map/ppermute | solution.py:387
  43.0 3.9 %collective-permute-start.16 = (bf16[112,128]{1,0:T(8,128)(2,1)S(1)}, bf16[112,128]{1,0:T(8,128)(2,1)S(1)}, u32[]{:S(2)}, u32[]{:S(2)}) collective-permute-start(bf16[112,128]{1,0:T(8,128)(2,1)S(1)} %get-tuple-element.36), channel_id=1, source_target_pairs={{0,16},{2,18},{4,20},{6,22},{8,24},{10,26},{12,28},{14,30},{16,0},... | collective-permute-start | bytes 86024 | tf_op jit(solution)/shard_map/ppermute | solution.py:387
  45.3 4.5 %collective-permute-start.17 = (bf16[112,128]{1,0:T(8,128)(2,1)S(1)}, bf16[112,128]{1,0:T(8,128)(2,1)S(1)}, u32[]{:S(2)}, u32[]{:S(2)}) collective-permute-start(bf16[112,128]{1,0:T(8,128)(2,1)S(1)} %get-tuple-element.37), channel_id=1, source_target_pairs={{0,24},{2,26},{4,28},{6,30},{8,16},{10,18},{12,20},{14,22},{16,8},... | collective-permute-start | bytes 86024 | tf_op jit(solution)/shard_map/ppermute | solution.py:387
  49.9 8.7 %collective-permute-start.18 = (bf16[112,128]{1,0:T(8,128)(2,1)S(1)}, bf16[112,128]{1,0:T(8,128)(2,1)S(1)}, u32[]{:S(2)}, u32[]{:S(2)}) collective-permute-start(bf16[112,128]{1,0:T(8,128)(2,1)S(1)} %fold_far.1.refs_0_), channel_id=1, source_target_pairs={{0,8},{2,10},{4,12},{6,14},{8,0},{10,2},{12,4},{14,6},{16,24},{18,... | collective-permute-start | bytes 86024 | tf_op jit(solution)/shard_map/ppermute | solution.py:420
  50.0 8.6 %collective-permute-start.19 = (bf16[112,128]{1,0:T(8,128)(2,1)S(1)}, bf16[112,128]{1,0:T(8,128)(2,1)S(1)}, u32[]{:S(2)}, u32[]{:S(2)}) collective-permute-start(bf16[112,128]{1,0:T(8,128)(2,1)S(1)} %fold_far.1.refs_0_), channel_id=1, source_target_pairs={{0,16},{2,18},{4,20},{6,22},{8,24},{10,26},{12,28},{14,30},{16,0},... | collective-permute-start | bytes 86024 | tf_op jit(solution)/shard_map/ppermute | solution.py:420
  50.6 8.0 %collective-permute-start.20 = (bf16[112,128]{1,0:T(8,128)(2,1)S(1)}, bf16[112,128]{1,0:T(8,128)(2,1)S(1)}, u32[]{:S(2)}, u32[]{:S(2)}) collective-permute-start(bf16[112,128]{1,0:T(8,128)(2,1)S(1)} %fold_far.1.refs_0_), channel_id=1, source_target_pairs={{0,24},{2,26},{4,28},{6,30},{8,16},{10,18},{12,20},{14,22},{16,8},... | collective-permute-start | bytes 86024 | tf_op jit(solution)/shard_map/ppermute | solution.py:420
  53.5 11.2 %collective-permute-start.10 = (bf16[64,1024]{1,0:T(8,128)(2,1)S(1)}, bf16[64,1024]{1,0:T(8,128)(2,1)S(1)}, u32[]{:S(2)}, u32[]{:S(2)}) collective-permute-start(bf16[64,1024]{1,0:T(8,128)(2,1)S(1)} %get-tuple-element.28), channel_id=1, source_target_pairs={{0,2},{2,0},{4,6},{6,4},{8,10},{10,8},{12,14},{14,12},{16,18},{18,... | collective-permute-start | bytes 393224 | tf_op jit(solution)/shard_map/ppermute | solution.py:176
  56.2 8.5 %collective-permute-start.11 = (bf16[64,1024]{1,0:T(8,128)(2,1)S(1)}, bf16[64,1024]{1,0:T(8,128)(2,1)S(1)}, u32[]{:S(2)}, u32[]{:S(2)}) collective-permute-start(bf16[64,1024]{1,0:T(8,128)(2,1)S(1)} %get-tuple-element.29), channel_id=1, source_target_pairs={{0,0},{2,4},{4,2},{6,8},{8,6},{10,12},{12,10},{14,16},{16,14},{18,... | collective-permute-start | bytes 393224 | tf_op jit(solution)/shard_map/ppermute | solution.py:179
  58.7 7.8 %collective-permute-start.21 = (bf16[448,128]{1,0:T(8,128)(2,1)S(1)}, bf16[448,128]{1,0:T(8,128)(2,1)S(1)}, u32[]{:S(2)}, u32[]{:S(2)}) collective-permute-start(bf16[448,128]{1,0:T(8,128)(2,1)S(1)} %join_far.1.refs_0_), channel_id=1, source_target_pairs={{0,2},{2,0},{4,6},{6,4},{8,10},{10,8},{12,14},{14,12},{16,18},{18,... | collective-permute-start | bytes 344072 | tf_op jit(solution)/shard_map/ppermute | solution.py:429
  58.7 7.7 %collective-permute-start.22 = (bf16[448,128]{1,0:T(8,128)(2,1)S(1)}, bf16[448,128]{1,0:T(8,128)(2,1)S(1)}, u32[]{:S(2)}, u32[]{:S(2)}) collective-permute-start(bf16[448,128]{1,0:T(8,128)(2,1)S(1)} %join_far.1.refs_0_), channel_id=1, source_target_pairs={{0,4},{2,6},{4,0},{6,2},{8,12},{10,14},{12,8},{14,10},{16,20},{18,... | collective-permute-start | bytes 344072 | tf_op jit(solution)/shard_map/ppermute | solution.py:429
  60.1 7.3 %collective-permute-start.23 = (bf16[448,128]{1,0:T(8,128)(2,1)S(1)}, bf16[448,128]{1,0:T(8,128)(2,1)S(1)}, u32[]{:S(2)}, u32[]{:S(2)}) collective-permute-start(bf16[448,128]{1,0:T(8,128)(2,1)S(1)} %join_far.1.refs_0_), channel_id=1, source_target_pairs={{0,6},{2,4},{4,2},{6,0},{8,14},{10,12},{12,10},{14,8},{16,22},{18,... | collective-permute-start | bytes 344072 | tf_op jit(solution)/shard_map/ppermute | solution.py:429

commit v3 on v2

v3 whole, which is shorter than its diff:
```python
import jax
import jax.numpy as jnp
from jax import lax
from jax.experimental import pallas as pl
from jax.experimental.pallas import tpu as pltpu
from jax.sharding import PartitionSpec as P


F32 = jnp.float32
BF16 = jnp.bfloat16
VMEM_LIMIT = 32 * 1024 * 1024


def call(body, outs, scratch=()):
    def run(*args):
        return pl.pallas_call(
            body,
            out_shape=outs,
            in_specs=[pl.BlockSpec(memory_space=pltpu.VMEM)] * len(args),
            scratch_shapes=scratch,
            compiler_params=pltpu.CompilerParams(vmem_limit_bytes=VMEM_LIMIT),
        )(*[pltpu.with_memory_space_constraint(arg, pltpu.VMEM) for arg in args])

    return run


def shaped(shape, dtype):
    return pltpu.VMEM(shape, dtype)


def dot(lhs, rhs):
    return jnp.dot(lhs, rhs, preferred_element_type=F32)


def dot_cells(lhs, rhs):
    return lax.dot_general(lhs, rhs, (((1,), (1,)), ((), ())), preferred_element_type=F32)


def silu_slope(values):
    part = 1.0 / (1.0 + jnp.exp(-values))
    return part * (1.0 + values * (1.0 - part))


def silu(values):
    return values / (1.0 + jnp.exp(-values))


def stack3(cells, depth):
    count = cells.shape[1]
    lane = lax.broadcasted_iota(jnp.int32, cells.shape, 1) % depth
    wide = cells.astype(F32)
    below = jnp.where(lane == 0, 0.0, pltpu.roll(wide, 1, 1)).astype(BF16)
    above = jnp.where(lane == depth - 1, 0.0, pltpu.roll(wide, count - 1, 1)).astype(BF16)
    return jnp.concatenate([below, cells, above], axis=0)


def shifted_rows(cells, offset, depth):
    if offset == 0:
        return cells
    blank = jnp.zeros((cells.shape[0], depth), cells.dtype)
    if cells.shape[1] == depth:
        return blank
    if offset > 0:
        return jnp.concatenate([cells[:, depth:], blank], axis=1)
    return jnp.concatenate([blank, cells[:, :-depth]], axis=1)


def conv_planes(matrices, stacks, planes, outputs, depth):
    results = [None] * planes
    for place in range(planes + 2):
        first = max(0, place - planes + 1)
        last = min(2, place)
        rows = matrices[first * 3 * outputs : (last + 1) * 3 * outputs, :]
        terms = dot(rows, stacks[place])
        for tap_x in range(first, last + 1):
            for tap_y in range(3):
                begin = ((tap_x - first) * 3 + tap_y) * outputs
                term = shifted_rows(terms[begin : begin + outputs], tap_y - 1, depth)
                target = place - tap_x
                results[target] = term if results[target] is None else results[target] + term
    return results


def weight_planes(acc, grads, stacks, depth):
    planes = len(grads)
    outputs = grads[0].shape[0]
    rows = [
        jnp.concatenate([shifted_rows(grad, 1 - tap_y, depth) for tap_y in range(3)], axis=0)
        for grad in grads
    ]
    for tap_x in range(3):
        total = None
        for plane in range(planes):
            term = dot_cells(rows[plane], stacks[plane + tap_x])
            total = term if total is None else total + term
        acc[tap_x * 3 * outputs : (tap_x + 1) * 3 * outputs, :] = total


def pack(acc, target, base, rows):
    half = rows // 2
    target[base : base + rows, :] = acc[:, :128]
    target[base + rows : base + rows + half, :] = jnp.concatenate(
        [acc[:half, 128:], acc[half:, 128:]], axis=1
    )


def unpack(source, base, rows, out, scale):
    half = rows // 2
    outputs = rows // 9
    for pair in range(9):
        main = source[base + pair * outputs : base + (pair + 1) * outputs, :].astype(F32) * scale
        out[3 * pair] = main[:, :64]
        out[3 * pair + 1] = main[:, 64:]
    for piece in range(0, 9 * outputs, 8):
        row = piece if piece < half else piece - half
        tail = source[base + rows + row : base + rows + row + 8, :].astype(F32) * scale
        side = tail[:, :64] if piece < half else tail[:, 64:]
        out[3 * (piece // outputs) + 2, piece % outputs : piece % outputs + 8, :] = side


def forward_matrix(taps, target, outputs):
    for pair in range(9):
        target[pair * outputs : (pair + 1) * outputs, :] = jnp.concatenate(
            [taps[3 * pair + tap_z] for tap_z in range(3)], axis=1
        )


def backward_matrix(taps):
    rows = [
        jnp.concatenate([taps[26 - 3 * pair - tap_z] for pair in range(9)], axis=1)
        for tap_z in range(3)
    ]
    return jnp.concatenate(rows, axis=0).T


def pick(flag, one, other):
    return jnp.where(flag, one, other)


def swap_tables(count):
    ends = [(0, 0), (count - 1, count - 1)]
    table_b = ends + [(i, i + 1) for i in range(1, count - 1, 2)]
    table_b += [(i + 1, i) for i in range(1, count - 1, 2)]
    low = [i for i in range(count - 2) if i % 4 >= 2]
    table_d = [(i, i + 2) for i in low] + [(i + 2, i) for i in low]
    table_d += [(0, 0), (1, 1), (count - 2, count - 2), (count - 1, count - 1)]
    return table_b, table_d


def join_rows(target, place, pieces, brick):
    index = lax.axis_index("filt")
    for slot, piece in enumerate(pieces):
        start = pl.multiple_of((index ^ slot) * brick, brick)
        target[place, :, pl.ds(start, brick)] = piece


def local(space, filt, volume, first_weight, second_weight, cotangent):
    channels, planes, brick_y, depth = volume.shape
    filters = second_weight.shape[1]
    fine_y = brick_y * filt
    low_y = fine_y // 2
    low_depth = depth // 2
    fine_cells = fine_y * depth
    low_cells = low_y * low_depth
    brick = brick_y * depth
    fine_scale = 1.0 / (planes * space * fine_cells) ** 0.5
    low_scale = 1.0 / (planes // 2 * space * low_cells) ** 0.5
    blocks = channels // filters
    extra = low_cells // blocks
    table_b, table_d = swap_tables(space)

    def mirror(mask):
        return [(i, i ^ mask) for i in range(space)]

    def along(piece, table):
        return lax.ppermute(piece, "space", table)

    def across(piece, table, slot):
        pairs = [(i * filt + f, j * filt + (f ^ slot)) for i, j in table for f in range(filt)]
        return lax.ppermute(piece, ("space", "filt"), pairs)

    place = lax.axis_index("space")
    bricks = jnp.transpose(volume, (1, 0, 2, 3)).reshape(planes, channels, brick)
    cot = cotangent.reshape(filters, blocks, extra)
    cot = jnp.transpose(cot, (1, 0, 2)).reshape(channels, extra)
    edge = jnp.where(place % 2 == 1, bricks[planes - 1], bricks[0])
    own_message = jnp.concatenate([bricks[p] for p in range(planes)] + [cot], axis=1)
    edge_message = jnp.concatenate([edge, cot], axis=1)
    own = [own_message] + [across(own_message, mirror(0), slot) for slot in range(1, filt)]
    side_b = [across(edge_message, table_b, slot) for slot in range(filt)]
    side_a = [along(message, mirror(1)) for message in own]

    narrow = jnp.concatenate([second_weight[:14], second_weight[13:]], axis=2)
    narrows = [narrow] + [across(narrow, mirror(0), slot) for slot in range(1, filt)]

    def first_kernel(*refs):
        own_refs, a_refs, b_refs = refs[:filt], refs[filt : 2 * filt], refs[2 * filt : 3 * filt]
        taps, pooled_ref, slope_ref, whole_ref, matrices = refs[3 * filt :]
        index = lax.axis_index("space")
        odd = index % 2 == 1
        inside = jnp.logical_and(index > 0, index < space - 1)
        forward_matrix(taps, matrices, channels)
        for plane in range(planes):
            pieces = [ref[:, plane * brick : (plane + 1) * brick] for ref in own_refs]
            join_rows(whole_ref, 1 + plane, pieces, brick)
        lefts, rights = [], []
        for a_ref, b_ref in zip(a_refs, b_refs):
            got_a = pick(odd, a_ref[:, (planes - 1) * brick : planes * brick], a_ref[:, :brick])
            got_b = b_ref[:, :brick]
            got_b = pick(inside, got_b, jnp.zeros_like(got_b))
            lefts.append(pick(odd, got_a, got_b))
            rights.append(pick(odd, got_b, got_a))
        join_rows(whole_ref, 0, lefts, brick)
        join_rows(whole_ref, planes + 1, rights, brick)
        stacks = [stack3(whole_ref[p], depth) for p in range(planes + 2)]
        pre = conv_planes(matrices, stacks, planes, channels, depth)
        hidden = [silu(value).astype(BF16) for value in pre]
        for plane in range(planes):
            slope_ref[plane] = silu_slope(pre[plane])
        pairs = (
            lax.broadcasted_iota(jnp.int32, (depth, low_depth), 0) // 2
            == lax.broadcasted_iota(jnp.int32, (depth, low_depth), 1)
        ).astype(BF16)
        for row in range(low_y):
            rows = jnp.concatenate(
                [
                    hidden[x][:, (2 * row + y) * depth : (2 * row + y + 1) * depth]
                    for x in range(2)
                    for y in range(2)
                ],
                axis=0,
            )
            sums = dot(rows, pairs)
            total = sums[:channels]
            for piece in range(1, 4):
                total = total + sums[piece * channels : (piece + 1) * channels]
            pooled_ref[:, row * low_depth : (row + 1) * low_depth] = (0.125 * total).astype(BF16)

    pooled, slope, whole = call(
        first_kernel,
        (
            shaped((channels, low_cells), BF16),
            shaped((planes, channels, fine_cells), F32),
            shaped((planes + 2, channels, fine_cells), BF16),
        ),
        (pltpu.VMEM((9 * channels, 3 * channels), BF16),),
    )(*own, *side_a, *side_b, first_weight)

    pool_d = along(pooled, table_d)
    pool_x = along(pooled, mirror(2))
    pool_a = along(pooled, mirror(1))
    pool_ax = along(pool_x, mirror(1))
    pool_ad = along(pool_d, mirror(1))

    def matrix_kernel(*refs):
        narrow_refs, taps = refs[:filt], refs[filt]
        forward_ref, back_ref, first_ref = refs[filt + 1 :]
        for slot, ref in enumerate(narrow_refs):
            values = [ref[t, :, :64] if t < 14 else ref[t - 13, :, 64:] for t in range(27)]
            forward_matrix(values, forward_ref.at[slot], filters)
            back_ref[slot] = backward_matrix(values)
        first_ref[...] = backward_matrix([taps[t] for t in range(27)])

    second_forward, second_back, first_back = call(
        matrix_kernel,
        (
            shaped((filt, 9 * filters, 3 * channels), BF16),
            shaped((filt, 9 * channels, 3 * filters), BF16),
            shaped((9 * channels, 3 * channels), BF16),
        ),
    )(*narrows, first_weight)

    first_rows, second_rows = 9 * channels, 9 * filters
    packed_first, packed_second = first_rows * 3 // 2, second_rows * 3 // 2
    far_side = space // 4
    unit = 8 * space
    total_rows = -(-(packed_first + packed_second) // unit) * unit
    half = total_rows // 2
    chunk = half // far_side

    def middle_kernel(*refs):
        own_refs, a_refs, b_refs = refs[:filt], refs[filt : 2 * filt], refs[2 * filt : 3 * filt]
        pool_ref, pa_ref, px_ref, pd_ref, pax_ref, pad_ref = refs[3 * filt : 3 * filt + 6]
        forward_ref, back_ref, slope_ref, whole_ref = refs[3 * filt + 6 : 3 * filt + 10]
        features_ref, down_ref, edge_a_ref, edge_b_ref, keep_ref, send_ref = refs[
            3 * filt + 10 : 3 * filt + 16
        ]
        first_acc, second_acc, rows_ref, parts_ref = refs[3 * filt + 16 :]
        index = lax.axis_index("space")
        odd = index % 2 == 1
        up = (index // 2) % 2 == 1
        inside = jnp.logical_and(index > 0, index < space - 1)
        inside_two = jnp.logical_and(index > 1, index < space - 2)
        blank = jnp.zeros((channels, low_cells), BF16)
        got_d = pick(inside_two, pd_ref[...], blank)
        got_ad = pick(inside_two, pad_ref[...], blank)
        got_a, got_x, got_ax = pa_ref[...], px_ref[...], pax_ref[...]
        other = pick(odd == up, got_ad, got_ax)
        pools = [
            pick(up, got_x, got_d),
            pick(odd, got_a, other),
            pool_ref[...],
            pick(odd, other, got_a),
            pick(up, got_d, got_x),
        ]
        stacks = [stack3(value, low_depth) for value in pools]

        def cot_of(packed):
            return jnp.concatenate(
                [packed[k * filters : (k + 1) * filters] for k in range(blocks)], axis=1
            ).astype(F32)

        for slot in range(filt):
            pre = conv_planes(forward_ref.at[slot], stacks, 3, filters, low_depth)
            cot_own = cot_of(own_refs[slot][:, planes * brick :])
            cot_a = cot_of(a_refs[slot][:, planes * brick :])
            cot_b = cot_of(b_refs[slot][:, brick:])
            cot_b = pick(inside, cot_b, jnp.zeros_like(cot_b))
            cots = [pick(odd, cot_a, cot_b), cot_own, pick(odd, cot_b, cot_a)]
            downs = [
                (value * silu_slope(pre[plane])).astype(BF16) for plane, value in enumerate(cots)
            ]
            if slot == 0:
                features_ref[...] = silu(pre[1]).astype(BF16)
                weight_planes(second_acc, [downs[1]], stacks[1:4], low_depth)
            down_stacks = [stack3(value, low_depth) for value in downs]
            (part,) = conv_planes(back_ref.at[slot], down_stacks, 1, channels, low_depth)
            parts_ref[lax.axis_index("filt") ^ slot] = part.astype(BF16)

        spread = (
            lax.broadcasted_iota(jnp.int32, (low_depth, depth), 0)
            == lax.broadcasted_iota(jnp.int32, (low_depth, depth), 1) // 2
        ).astype(BF16)
        columns = []
        for row in range(low_y):
            wide = None
            for group in range(filt):
                cells = parts_ref[group, :, row * low_depth : (row + 1) * low_depth]
                term = dot(cells, spread)
                wide = term if wide is None else wide + term
            columns += [0.125 * wide] * 2
        hidden_grad = jnp.concatenate(columns, axis=1)
        grads = [(hidden_grad * slope_ref[p]).astype(BF16) for p in range(planes)]
        for plane in range(planes):
            down_ref[plane] = grads[plane]
        edge_a_ref[...] = pick(odd, grads[0], grads[planes - 1])
        edge_b_ref[...] = pick(odd, grads[planes - 1], grads[0])
        fine_stacks = [stack3(whole_ref[p], depth) for p in range(planes + 2)]
        weight_planes(first_acc, grads, fine_stacks, depth)
        pack(first_acc, rows_ref, 0, first_rows)
        pack(second_acc, rows_ref, packed_first, second_rows)
        if total_rows > packed_first + packed_second:
            rows_ref[packed_first + packed_second :, :] = jnp.zeros(
                (total_rows - packed_first - packed_second, 128), F32
            )
        core = index % 2
        keep_ref[...] = rows_ref[pl.ds(pl.multiple_of(core * half, 16), half), :]
        send_ref[...] = rows_ref[pl.ds(pl.multiple_of((1 - core) * half, 16), half), :].astype(
            BF16
        )

    features, first_down, edge_a, edge_b, keep, send = call(
        middle_kernel,
        (
            shaped((filters, low_cells), BF16),
            shaped((planes, channels, fine_cells), BF16),
            shaped((channels, fine_cells), BF16),
            shaped((channels, fine_cells), BF16),
            shaped((half, 128), F32),
            shaped((half, 128), BF16),
        ),
        (
            pltpu.VMEM((first_rows, 3 * channels), F32),
            pltpu.VMEM((second_rows, 3 * channels), F32),
            pltpu.VMEM((total_rows, 128), F32),
            pltpu.VMEM((filt, channels, low_cells), BF16),
        ),
    )(
        *own,
        *side_a,
        *side_b,
        pooled,
        pool_a,
        pool_x,
        pool_d,
        pool_ax,
        pool_ad,
        second_forward,
        second_back,
        slope,
        whole,
    )
    features = features.reshape(filters, 1, low_y, low_depth)

    got = along(send, mirror(1))

    def split_kernel(keep_ref, got_ref, *refs):
        out_refs, rows_ref = refs[:-1], refs[-1]
        rows_ref[...] = keep_ref[...] + got_ref[...].astype(F32)
        high = lax.axis_index("space") // 4
        out_refs[0][...] = rows_ref[pl.ds(pl.multiple_of(high * chunk, 16), chunk), :]
        for k in range(1, far_side):
            start = pl.multiple_of((high ^ k) * chunk, 16)
            out_refs[k][...] = rows_ref[pl.ds(start, chunk), :].astype(BF16)

    own_chunk, *sends = call(
        split_kernel,
        (shaped((chunk, 128), F32),) + (shaped((chunk, 128), BF16),) * (far_side - 1),
        (pltpu.VMEM((half, 128), F32),),
    )(keep, got)
    got = [along(sends[k - 1], mirror(4 * k)) for k in range(1, far_side)]
    halo_a, halo_b = along(edge_a, mirror(1)), along(edge_b, table_b)

    def sum_kernel(own_ref, *refs):
        total = own_ref[...].astype(F32)
        for ref in refs[:-1]:
            total = total + ref[...].astype(F32)
        refs[-1][...] = total.astype(BF16)

    summed = call(sum_kernel, shaped((chunk, 128), BF16))(own_chunk, *got)
    other = along(summed, mirror(2))

    def volume_kernel(own_ref, a_ref, b_ref, matrices, out_ref, rows_ref):
        index = lax.axis_index("space")
        odd = index % 2 == 1
        inside = jnp.logical_and(index > 0, index < space - 1)
        got_a, got_b = a_ref[...], b_ref[...]
        got_b = pick(inside, got_b, jnp.zeros_like(got_b))
        values = [pick(odd, got_a, got_b)] + [own_ref[p] for p in range(planes)]
        values.append(pick(odd, got_b, got_a))
        blank = jnp.zeros((channels, depth), BF16)
        begin = pl.multiple_of(lax.axis_index("filt") * brick, brick)
        stacks = []
        for position, value in enumerate(values):
            rows_ref[position] = jnp.concatenate([blank, value, blank], axis=1)
            stacks.append(stack3(rows_ref[position, :, pl.ds(begin, brick + 2 * depth)], depth))
        results = conv_planes(matrices, stacks, planes, channels, depth)
        for plane in range(planes):
            out_ref[plane] = results[plane][:, depth : depth + brick].astype(BF16)

    volume_grad = call(
        volume_kernel,
        shaped((planes, channels, brick), BF16),
        (pltpu.VMEM((planes + 2, channels, fine_cells + 2 * depth), BF16),),
    )(first_down, halo_a, halo_b, first_back)
    volume_grad = jnp.transpose(volume_grad.reshape(planes, channels, brick_y, depth), (1, 0, 2, 3))

    final_chunk = call(sum_kernel, shaped((chunk, 128), BF16))(summed, other)
    pieces = [final_chunk] + [along(final_chunk, mirror(4 * k)) for k in range(1, far_side)]

    def join_kernel(*refs):
        high = lax.axis_index("space") // 4
        for k, ref in enumerate(refs[:-1]):
            refs[-1][pl.ds(pl.multiple_of((high ^ k) * chunk, 16), chunk), :] = ref[...]

    group = call(join_kernel, shaped((half, 128), BF16))(*pieces)
    partner = along(group, mirror(1))

    def final_kernel(own_ref, got_ref, first_ref, second_ref, rows_ref):
        core = lax.axis_index("space") % 2
        rows_ref[pl.ds(pl.multiple_of(core * half, 16), half), :] = own_ref[...].astype(F32)
        rows_ref[pl.ds(pl.multiple_of((1 - core) * half, 16), half), :] = got_ref[...].astype(F32)
        unpack(rows_ref, 0, first_rows, first_ref, fine_scale)
        unpack(rows_ref, packed_first, second_rows, second_ref, low_scale)

    first_grad, second_grad = call(
        final_kernel,
        (
            jax.ShapeDtypeStruct((27, channels, channels), F32),
            jax.ShapeDtypeStruct((27, filters, channels), F32),
        ),
        (pltpu.VMEM((total_rows, 128), F32),),
    )(group, partner)
    return (features, volume_grad, first_grad, second_grad)


def solution(mesh):
    def whole_program(*args):
        return local(mesh.shape["space"], mesh.shape["filt"], *args)

    placed = (
        P(None, "space", "filt", None),
        P(),
        P(None, "filt", None),
        P("filt", "space", None, None),
    )
    return jax.shard_map(
        whole_program,
        mesh=mesh,
        in_specs=placed,
        out_specs=(
            P("filt", "space", None, None),
            P(None, "space", "filt", None),
            P(),
            P(None, "filt", None),
        ),
        check_vma=False,
    )
```

time: 69.8 us -> 66.7 us (0.956)
  local copies, waits for them, and re-layouts: 12.7 us -> 3.26 us
  waiting for transfers between devices: 14.9 us -> 22.7 us
  starting transfers between devices: 36.1 us -> 32 us
  Pallas kernels: 4.81 us -> 7.18 us
    ppermute x24 -> x22, waiting for transfers between devices: 14.9 us -> 22.7 us  [the longest x18 15.1 us: along(): return lax.ppermute(piece, 'space', table)]
    reshape x10 -> x0, local copies, waits for them, and re-layouts: 5.69 us -> none  [the longest x2 1.62 us: local(): second_taps = second_weight.reshape(9, 3, filters, channels)]
    ppermute x24 -> x22, starting transfers between devices: 36.1 us -> 32 us  [the longest x18 24.1 us: along(): return lax.ppermute(piece, 'space', table)]
    rev x2 -> x0, local copies, waits for them, and re-layouts: 3.28 us -> none  [the longest x1 1.64 us: local(): second_taps[::-1, ::-1]]
    pallas_call x10 -> x9, Pallas kernels: 4.81 us -> 7.18 us  [run(): pl.pallas_call(body, out_shape=outs, in_specs=[pl.BlockSpec(memory_space=...]
    unnamed x15 -> x10, local copies, waits for them, and re-layouts: 2.28 us -> 0.78 us
    slice x0 -> x2, local copies, waits for them, and re-layouts: none -> 1.05 us  [the longest x1 1.02 us: local(): bricks[p]]
  transfers between devices with their start and end apart: 24 -> 22, of which waited for: 8 -> 12; matrix products, arithmetic and copies ran while one was open for 14% -> 2% of each run, Pallas kernels for 2% -> 4%
where the time goes in v3:
time: 66.7 us; the launch traced here: 66.1 us
  starting transfers between devices  32 us (48%)
  waiting for transfers between devices  22.7 us (34%)
  Pallas kernels  7.18 us (11%)
  local copies, waits for them, and re-layouts  3.26 us (5%)
  between operations  0.84 us (1%)
    ppermute x18, starting transfers between devices, along(): return lax.ppermute(piece, 'space', table)  24.1 us
    ppermute x18, waiting for transfers between devices, along(): return lax.ppermute(piece, 'space', table)  15.1 us
    ppermute x4, starting transfers between devices, across(): return lax.ppermute(piece, ('space', 'filt'), pairs)  7.92 us
    ppermute x4, waiting for transfers between devices, across(): return lax.ppermute(piece, ('space', 'filt'), pairs)  7.61 us
    pallas_call x9, Pallas kernels, run(): pl.pallas_call(body, out_shape=outs, in_specs=[pl.BlockSpec(memory_space=...  7.18 us
  transfers between devices with their start and end apart: 22, of which 12 were waited for; matrix products, arithmetic and copies ran while one was open for 2% of the time, Pallas kernels for 4%

profile of v3, /device:TPU:1, one launch (start us, length us, event | category | flops | bytes accessed | tf_op | source)
XLA Modules:
  0.0 66.1 jit_solution(3782930940972735981)
XLA Ops:
  0.7 1.0 %fusion.1 = (bf16[1,64,2,256]{3,2,0,1:T(2,128)(2,1)S(1)}, bf16[1,64,2,256]{3,2,0,1:T(2,128)(2,1)S(1)}) fusion(bf16[2,64,2,256]{3,2,0,1:T(2,128)(2,1)} %bitcast.25), kind=kLoop, calls=%fused_computation.9 | loop fusion | bytes 262144 | tf_op jit(solution)/shard_map/slice | solution.py:187
  1.8 0.7 %copy-done.2 = bf16[64,1,2,128]{3,2,1,0:T(2,128)(2,1)S(1)} copy-done((bf16[64,1,2,128]{3,2,1,0:T(2,128)(2,1)S(1)}, bf16[64,1,2,128]{3,2,1,0:T(2,128)(2,1)}, u32[]{:S(2)}) %copy-start.2) | copy-done | bytes 32792
  2.5 2.7 %collective-permute-start = (bf16[64,1280]{1,0:T(8,128)(2,1)S(1)}, bf16[64,1280]{1,0:T(8,128)(2,1)S(1)}, u32[]{:S(2)}, u32[]{:S(2)}) collective-permute-start(bf16[64,1280]{1,0:T(8,128)(2,1)S(1)} %constant_dynamic-update-slice_fusion.refs_0_), channel_id=1, source_target_pairs={{0,1},{1,0},{2,3},{3,2},{4,5},{5,4},{6,7},{7,6},{8,9},{9,8},{10,11... | collective-permute-start | bytes 491528 | tf_op jit(solution)/shard_map/ppermute | solution.py:180
  5.5 4.2 %collective-permute-done.refs_1_ = bf16[64,1280]{1,0:T(8,128)(2,1)S(1)} collective-permute-done((bf16[64,1280]{1,0:T(8,128)(2,1)S(1)}, bf16[64,1280]{1,0:T(8,128)(2,1)S(1)}, u32[]{:S(2)}, u32[]{:S(2)}) %collective-permute-start) | collective-permute-done | bytes 163872 | tf_op jit(solution)/shard_map/ppermute | solution.py:180
  9.7 0.9 %collective-permute-start.2 = (bf16[64,1280]{1,0:T(8,128)(2,1)S(1)}, bf16[64,1280]{1,0:T(8,128)(2,1)S(1)}, u32[]{:S(2)}, u32[]{:S(2)}) collective-permute-start(bf16[64,1280]{1,0:T(8,128)(2,1)S(1)} %collective-permute-done.refs_1_), channel_id=1, source_target_pairs={{0,2},{2,0},{4,6},{6,4},{8,10},{10,8},{12,14},{14,12},{16,18},{18,... | collective-permute-start | bytes 491528 | tf_op jit(solution)/shard_map/ppermute | solution.py:176
  10.6 2.7 %collective-permute-start.4 = (bf16[64,768]{1,0:T(8,128)(2,1)S(1)}, bf16[64,768]{1,0:T(8,128)(2,1)S(1)}, u32[]{:S(2)}, u32[]{:S(2)}) collective-permute-start(bf16[64,768]{1,0:T(8,128)(2,1)S(1)} %pad_maximum_fusion.1), channel_id=1, source_target_pairs={{0,1},{1,0},{30,31},{31,30},{2,5},{3,4},{6,9},{7,8},{10,13},{11,12... | collective-permute-start | bytes 294920 | tf_op jit(solution)/shard_map/ppermute | solution.py:180
  13.3 2.5 %collective-permute-start.3 = (bf16[64,768]{1,0:T(8,128)(2,1)S(1)}, bf16[64,768]{1,0:T(8,128)(2,1)S(1)}, u32[]{:S(2)}, u32[]{:S(2)}) collective-permute-start(bf16[64,768]{1,0:T(8,128)(2,1)S(1)} %pad_maximum_fusion.1), channel_id=1, source_target_pairs={{0,0},{1,1},{30,30},{31,31},{2,4},{3,5},{6,8},{7,9},{10,12},{11,13... | collective-permute-start | bytes 294920 | tf_op jit(solution)/shard_map/ppermute | solution.py:180
  15.8 1.1 %collective-permute-done.4.refs_5_ = bf16[64,768]{1,0:T(8,128)(2,1)S(1)} collective-permute-done((bf16[64,768]{1,0:T(8,128)(2,1)S(1)}, bf16[64,768]{1,0:T(8,128)(2,1)S(1)}, u32[]{:S(2)}, u32[]{:S(2)}) %collective-permute-start.4) | collective-permute-done | bytes 98336 | tf_op jit(solution)/shard_map/ppermute | solution.py:180
  16.8 2.4 %collective-permute-done.3.refs_4_ = bf16[64,768]{1,0:T(8,128)(2,1)S(1)} collective-permute-done((bf16[64,768]{1,0:T(8,128)(2,1)S(1)}, bf16[64,768]{1,0:T(8,128)(2,1)S(1)}, u32[]{:S(2)}, u32[]{:S(2)}) %collective-permute-start.3) | collective-permute-done | bytes 98336 | tf_op jit(solution)/shard_map/ppermute | solution.py:180
  19.2 1.2 %shard_map.75 = (bf16[64,256]{1,0:T(8,128)(2,1)S(1)}, f32[2,64,1024]{2,1,0:T(8,128)S(1)}, bf16[4,64,1024]{2,1,0:T(8,128)(2,1)S(1)}) custom-call(bf16[64,1280]{1,0:T(8,128)(2,1)S(1)} %constant_dynamic-update-slice_fusion.refs_0_, bf16[64,1280]{1,0:T(8,128)(2,1)S(1)} %collective-permute-done.refs_1_, bf16[64,1280]{1,0:T(8,128)(2,1)S(1)} %collective-permute-done.1.refs_2_, ...), custom_call_target="tpu_custom_call" | custom-call | tf_op jit(solution)/shard_map/pallas_call | solution.py:16
  20.4 0.7 %collective-permute-start.7 = (bf16[64,256]{1,0:T(8,128)(2,1)S(1)}, bf16[64,256]{1,0:T(8,128)(2,1)S(1)}, u32[]{:S(2)}, u32[]{:S(2)}) collective-permute-start(bf16[64,256]{1,0:T(8,128)(2,1)S(1)} %get-tuple-element.22.refs_6_), channel_id=1, source_target_pairs={{4,8},{6,10},{12,16},{14,18},{20,24},{22,26},{8,4},{10,6},{16,12},... | collective-permute-start | bytes 98312 | tf_op jit(solution)/shard_map/ppermute | solution.py:176
  21.1 4.8 %collective-permute-start.6 = (bf16[64,256]{1,0:T(8,128)(2,1)S(1)}, bf16[64,256]{1,0:T(8,128)(2,1)S(1)}, u32[]{:S(2)}, u32[]{:S(2)}) collective-permute-start(bf16[64,256]{1,0:T(8,128)(2,1)S(1)} %get-tuple-element.22.refs_6_), channel_id=1, source_target_pairs={{0,4},{2,6},{4,0},{6,2},{8,12},{10,14},{12,8},{14,10},{16,20},{18,... | collective-permute-start | bytes 98312 | tf_op jit(solution)/shard_map/ppermute | solution.py:176
  25.9 0.9 %collective-permute-start.5 = (bf16[64,256]{1,0:T(8,128)(2,1)S(1)}, bf16[64,256]{1,0:T(8,128)(2,1)S(1)}, u32[]{:S(2)}, u32[]{:S(2)}) collective-permute-start(bf16[64,256]{1,0:T(8,128)(2,1)S(1)} %get-tuple-element.22.refs_6_), channel_id=1, source_target_pairs={{0,2},{2,0},{4,6},{6,4},{8,10},{10,8},{12,14},{14,12},{16,18},{18,... | collective-permute-start | bytes 98312 | tf_op jit(solution)/shard_map/ppermute | solution.py:176
  27.2 1.5 %collective-permute-start.8 = (bf16[64,256]{1,0:T(8,128)(2,1)S(1)}, bf16[64,256]{1,0:T(8,128)(2,1)S(1)}, u32[]{:S(2)}, u32[]{:S(2)}) collective-permute-start(bf16[64,256]{1,0:T(8,128)(2,1)S(1)} %collective-permute-done.6.refs_8_), channel_id=1, source_target_pairs={{0,2},{2,0},{4,6},{6,4},{8,10},{10,8},{12,14},{14,12},{16,18},{18,... | collective-permute-start | bytes 98312 | tf_op jit(solution)/shard_map/ppermute | solution.py:176
  29.5 2.8 %shard_map.77 = (bf16[64,256]{1,0:T(8,128)(2,1)S(1)}, bf16[2,64,1024]{2,1,0:T(8,128)(2,1)S(1)}, bf16[64,1024]{1,0:T(8,128)(2,1)S(1)}, bf16[64,1024]{1,0:T(8,128)...) custom-call(bf16[64,1280]{1,0:T(8,128)(2,1)S(1)} %constant_dynamic-update-slice_fusion.refs_0_, ...), custom_call_target="tpu_custom_call" | custom-call | tf_op jit(solution)/shard_map/pallas_call | solution.py:16
  32.8 1.1 %collective-permute-done.13.got_ref = bf16[896,128]{1,0:T(8,128)(2,1)S(1)} collective-permute-done((bf16[896,128]{1,0:T(8,128)(2,1)S(1)}, bf16[896,128]{1,0:T(8,128)(2,1)S(1)}, u32[]{:S(2)}, u32[]{:S(2)}) %collective-permute-start.13) | collective-permute-done | bytes 229408 | tf_op jit(solution)/shard_map/ppermute | solution.py:176
  34.0 1.5 %collective-permute-start.14 = (bf16[224,128]{1,0:T(8,128)(2,1)S(1)}, bf16[224,128]{1,0:T(8,128)(2,1)S(1)}, u32[]{:S(2)}, u32[]{:S(2)}) collective-permute-start(bf16[224,128]{1,0:T(8,128)(2,1)S(1)} %get-tuple-element.35), channel_id=1, source_target_pairs={{0,8},{2,10},{4,12},{6,14},{8,0},{10,2},{12,4},{14,6},{16,24},{18,... | collective-permute-start | bytes 172040 | tf_op jit(solution)/shard_map/ppermute | solution.py:176
  35.5 2.6 %collective-permute-start.15 = (bf16[224,128]{1,0:T(8,128)(2,1)S(1)}, bf16[224,128]{1,0:T(8,128)(2,1)S(1)}, u32[]{:S(2)}, u32[]{:S(2)}) collective-permute-start(bf16[224,128]{1,0:T(8,128)(2,1)S(1)} %get-tuple-element.36), channel_id=1, source_target_pairs={{0,16},{2,18},{4,20},{6,22},{8,24},{10,26},{12,28},{14,30},{16,0},... | collective-permute-start | bytes 172040 | tf_op jit(solution)/shard_map/ppermute | solution.py:176
  38.2 1.6 %collective-permute-done.15.refs_1_ = bf16[224,128]{1,0:T(8,128)(2,1)S(1)} collective-permute-done((bf16[224,128]{1,0:T(8,128)(2,1)S(1)}, bf16[224,128]{1,0:T(8,128)(2,1)S(1)}, u32[]{:S(2)}, u32[]{:S(2)}) %collective-permute-start.15) | collective-permute-done | bytes 57376 | tf_op jit(solution)/shard_map/ppermute | solution.py:176
  39.7 3.4 %collective-permute-done.16.refs_2_ = bf16[224,128]{1,0:T(8,128)(2,1)S(1)} collective-permute-done((bf16[224,128]{1,0:T(8,128)(2,1)S(1)}, bf16[224,128]{1,0:T(8,128)(2,1)S(1)}, u32[]{:S(2)}, u32[]{:S(2)}) %collective-permute-start.16) | collective-permute-done | bytes 57376 | tf_op jit(solution)/shard_map/ppermute | solution.py:176
  43.7 2.5 %collective-permute-done.17.refs_0_ = bf16[224,128]{1,0:T(8,128)(2,1)S(1)} collective-permute-done((bf16[224,128]{1,0:T(8,128)(2,1)S(1)}, bf16[224,128]{1,0:T(8,128)(2,1)S(1)}, u32[]{:S(2)}, u32[]{:S(2)}) %collective-permute-start.17) | collective-permute-done | bytes 57376 | tf_op jit(solution)/shard_map/ppermute | solution.py:176
  46.2 2.1 %collective-permute-start.20 = (bf16[224,128]{1,0:T(8,128)(2,1)S(1)}, bf16[224,128]{1,0:T(8,128)(2,1)S(1)}, u32[]{:S(2)}, u32[]{:S(2)}) collective-permute-start(bf16[224,128]{1,0:T(8,128)(2,1)S(1)} %shard_map.81.refs_0_), channel_id=1, source_target_pairs={{0,24},{2,26},{4,28},{6,30},{8,16},{10,18},{12,20},{14,22},{16,8},... | collective-permute-start | bytes 172040 | tf_op jit(solution)/shard_map/ppermute | solution.py:176
  48.7 1.1 %collective-permute-start.18 = (bf16[224,128]{1,0:T(8,128)(2,1)S(1)}, bf16[224,128]{1,0:T(8,128)(2,1)S(1)}, u32[]{:S(2)}, u32[]{:S(2)}) collective-permute-start(bf16[224,128]{1,0:T(8,128)(2,1)S(1)} %shard_map.81.refs_0_), channel_id=1, source_target_pairs={{0,8},{2,10},{4,12},{6,14},{8,0},{10,2},{12,4},{14,6},{16,24},{18,... | collective-permute-start | bytes 172040 | tf_op jit(solution)/shard_map/ppermute | solution.py:176
  49.9 1.3 %collective-permute-done.20.refs_3_ = bf16[224,128]{1,0:T(8,128)(2,1)S(1)} collective-permute-done((bf16[224,128]{1,0:T(8,128)(2,1)S(1)}, bf16[224,128]{1,0:T(8,128)(2,1)S(1)}, u32[]{:S(2)}, u32[]{:S(2)}) %collective-permute-start.20) | collective-permute-done | bytes 57376 | tf_op jit(solution)/shard_map/ppermute | solution.py:176
  51.1 2.3 %collective-permute-done.19.refs_2_ = bf16[224,128]{1,0:T(8,128)(2,1)S(1)} collective-permute-done((bf16[224,128]{1,0:T(8,128)(2,1)S(1)}, bf16[224,128]{1,0:T(8,128)(2,1)S(1)}, u32[]{:S(2)}, u32[]{:S(2)}) %collective-permute-start.19) | collective-permute-done | bytes 57376 | tf_op jit(solution)/shard_map/ppermute | solution.py:176
  53.5 3.0 %collective-permute-start.21 = (bf16[896,128]{1,0:T(8,128)(2,1)S(1)}, bf16[896,128]{1,0:T(8,128)(2,1)S(1)}, u32[]{:S(2)}, u32[]{:S(2)}) collective-permute-start(bf16[896,128]{1,0:T(8,128)(2,1)S(1)} %shard_map.82.own_ref), channel_id=1, source_target_pairs={{0,2},{2,0},{4,6},{6,4},{8,10},{10,8},{12,14},{14,12},{16,18},{18,... | collective-permute-start | bytes 688136 | tf_op jit(solution)/shard_map/ppermute | solution.py:176
  56.6 3.3 %collective-permute-start.12 = (bf16[64,1024]{1,0:T(8,128)(2,1)S(1)}, bf16[64,1024]{1,0:T(8,128)(2,1)S(1)}, u32[]{:S(2)}, u32[]{:S(2)}) collective-permute-start(bf16[64,1024]{1,0:T(8,128)(2,1)S(1)} %get-tuple-element.30), channel_id=1, source_target_pairs={{0,0},{30,30},{2,4},{6,8},{10,12},{14,16},{18,20},{22,24},{26,28},... | collective-permute-start | bytes 393224 | tf_op jit(solution)/shard_map/ppermute | solution.py:176
  60.0 0.6 reshape.19
  60.6 2.3 %collective-permute-done.12.b_ref = bf16[64,1024]{1,0:T(8,128)(2,1)S(1)} collective-permute-done((bf16[64,1024]{1,0:T(8,128)(2,1)S(1)}, bf16[64,1024]{1,0:T(8,128)(2,1)S(1)}, u32[]{:S(2)}, u32[]{:S(2)}) %collective-permute-start.12) | collective-permute-done | bytes 131104 | tf_op jit(solution)/shard_map/ppermute | solution.py:176
  62.9 0.9 %shard_map.78 = bf16[2,64,512]{2,1,0:T(8,128)(2,1)S(1)} custom-call(bf16[2,64,1024]{2,1,0:T(8,128)(2,1)S(1)} %get-tuple-element.28.own_ref, bf16[64,1024]{1,0:T(8,128)(2,1)S(1)} %collective-permute-done.11.a_ref, bf16[64,1024]{1,0:T(8,128)(2,1)S(1)} %collective-permute-done.12.b_ref, bf16[576,192]{1,0:T(8,128)(2,1)S(1)} %get-tuple-element.31.matrices), custom_call_target="tpu_custom_call" | custom-call | tf_op jit(solution)/shard_map/pallas_call | solution.py:16
  63.9 0.7 %copy.17 = bf16[2,64,2,256]{3,2,0,1:T(2,128)(2,1)} copy(bf16[2,64,2,256]{3,2,1,0:T(2,128)(2,1)S(1)} %reshape.20) | data formatting | bytes 262144 | tf_op jit(solution)/shard_map/reshape | solution.py:446
  64.6 1.5 %shard_map.83 = (f32[27,64,64]{2,1,0:T(8,128)}, f32[27,64,64]{2,1,0:T(8,128)}) custom-call(bf16[896,128]{1,0:T(8,128)(2,1)S(1)} %shard_map.82.own_ref, bf16[896,128]{1,0:T(8,128)(2,1)S(1)} %collective-permute-done.21.got_ref), custom_call_target="tpu_custom_call" | custom-call | tf_op jit(solution)/shard_map/pallas_call | solution.py:16
  (40 shorter events, 3.3 us)
Async XLA Ops:
  0.6 4.6 %copy-start.1 = (bf16[27,64,64]{2,1,0:T(8,128)(2,1)S(1)}, bf16[27,64,64]{2,1,0:T(8,128)(2,1)}, u32[]{:S(2)}) copy-start(bf16[27,64,64]{2,1,0:T(8,128)(2,1)} %param.6) | copy-start | bytes 663556
  1.7 0.8 %copy-start.2 = (bf16[64,1,2,128]{3,2,1,0:T(2,128)(2,1)S(1)}, bf16[64,1,2,128]{3,2,1,0:T(2,128)(2,1)}, u32[]{:S(2)}) copy-start(bf16[64,1,2,128]{3,2,1,0:T(2,128)(2,1)} %param.7) | copy-start | bytes 98308
  2.5 16.7 %collective-permute-start.1 = (bf16[64,1280]{1,0:T(8,128)(2,1)S(1)}, bf16[64,1280]{1,0:T(8,128)(2,1)S(1)}, u32[]{:S(2)}, u32[]{:S(2)}) collective-permute-start(bf16[64,1280]{1,0:T(8,128)(2,1)S(1)} %constant_dynamic-update-slice_fusion.refs_0_), channel_id=1, source_target_pairs={{0,2},{2,0},{4,6},{6,4},{8,10},{10,8},{12,14},{14,12},{16,18},{18,... | collective-permute-start | bytes 491528 | tf_op jit(solution)/shard_map/ppermute | solution.py:176
  2.5 7.2 %collective-permute-start = (bf16[64,1280]{1,0:T(8,128)(2,1)S(1)}, bf16[64,1280]{1,0:T(8,128)(2,1)S(1)}, u32[]{:S(2)}, u32[]{:S(2)}) collective-permute-start(bf16[64,1280]{1,0:T(8,128)(2,1)S(1)} %constant_dynamic-update-slice_fusion.refs_0_), channel_id=1, source_target_pairs={{0,1},{1,0},{2,3},{3,2},{4,5},{5,4},{6,7},{7,6},{8,9},{9,8},{10,11... | collective-permute-start | bytes 491528 | tf_op jit(solution)/shard_map/ppermute | solution.py:180
  5.3 14.0 %copy-start = (bf16[27,64,64]{2,1,0:T(8,128)(2,1)S(1)}, bf16[27,64,64]{2,1,0:T(8,128)(2,1)}, u32[]{:S(2)}) copy-start(bf16[27,64,64]{2,1,0:T(8,128)(2,1)} %refs_2_.1) | copy-start | bytes 663556
  5.4 23.3 %collective-permute-start.10 = (bf16[14,64,128]{2,1,0:T(8,128)(2,1)S(1)}, bf16[14,64,128]{2,1,0:T(8,128)(2,1)S(1)}, u32[]{:S(2)}, u32[]{:S(2)}) collective-permute-start(bf16[14,64,128]{2,1,0:T(8,128)(2,1)S(1)} %pad_maximum_fusion.refs_0_), channel_id=1, source_target_pairs={{0,1},{1,0},{2,3},{3,2},{4,5},{5,4},{6,7},{7,6},{8,9},{9,8},{10,11... | collective-permute-start | bytes 688136 | tf_op jit(solution)/shard_map/ppermute | solution.py:180
  9.7 9.5 %collective-permute-start.2 = (bf16[64,1280]{1,0:T(8,128)(2,1)S(1)}, bf16[64,1280]{1,0:T(8,128)(2,1)S(1)}, u32[]{:S(2)}, u32[]{:S(2)}) collective-permute-start(bf16[64,1280]{1,0:T(8,128)(2,1)S(1)} %collective-permute-done.refs_1_), channel_id=1, source_target_pairs={{0,2},{2,0},{4,6},{6,4},{8,10},{10,8},{12,14},{14,12},{16,18},{18,... | collective-permute-start | bytes 491528 | tf_op jit(solution)/shard_map/ppermute | solution.py:176
  10.6 6.2 %collective-permute-start.4 = (bf16[64,768]{1,0:T(8,128)(2,1)S(1)}, bf16[64,768]{1,0:T(8,128)(2,1)S(1)}, u32[]{:S(2)}, u32[]{:S(2)}) collective-permute-start(bf16[64,768]{1,0:T(8,128)(2,1)S(1)} %pad_maximum_fusion.1), channel_id=1, source_target_pairs={{0,1},{1,0},{30,31},{31,30},{2,5},{3,4},{6,9},{7,8},{10,13},{11,12... | collective-permute-start | bytes 294920 | tf_op jit(solution)/shard_map/ppermute | solution.py:180
  13.3 5.9 %collective-permute-start.3 = (bf16[64,768]{1,0:T(8,128)(2,1)S(1)}, bf16[64,768]{1,0:T(8,128)(2,1)S(1)}, u32[]{:S(2)}, u32[]{:S(2)}) collective-permute-start(bf16[64,768]{1,0:T(8,128)(2,1)S(1)} %pad_maximum_fusion.1), channel_id=1, source_target_pairs={{0,0},{1,1},{30,30},{31,31},{2,4},{3,5},{6,8},{7,9},{10,12},{11,13... | collective-permute-start | bytes 294920 | tf_op jit(solution)/shard_map/ppermute | solution.py:180
  20.4 6.4 %collective-permute-start.7 = (bf16[64,256]{1,0:T(8,128)(2,1)S(1)}, bf16[64,256]{1,0:T(8,128)(2,1)S(1)}, u32[]{:S(2)}, u32[]{:S(2)}) collective-permute-start(bf16[64,256]{1,0:T(8,128)(2,1)S(1)} %get-tuple-element.22.refs_6_), channel_id=1, source_target_pairs={{4,8},{6,10},{12,16},{14,18},{20,24},{22,26},{8,4},{10,6},{16,12},... | collective-permute-start | bytes 98312 | tf_op jit(solution)/shard_map/ppermute | solution.py:176
  21.1 6.1 %collective-permute-start.6 = (bf16[64,256]{1,0:T(8,128)(2,1)S(1)}, bf16[64,256]{1,0:T(8,128)(2,1)S(1)}, u32[]{:S(2)}, u32[]{:S(2)}) collective-permute-start(bf16[64,256]{1,0:T(8,128)(2,1)S(1)} %get-tuple-element.22.refs_6_), channel_id=1, source_target_pairs={{0,4},{2,6},{4,0},{6,2},{8,12},{10,14},{12,8},{14,10},{16,20},{18,... | collective-permute-start | bytes 98312 | tf_op jit(solution)/shard_map/ppermute | solution.py:176
  25.9 3.4 %collective-permute-start.5 = (bf16[64,256]{1,0:T(8,128)(2,1)S(1)}, bf16[64,256]{1,0:T(8,128)(2,1)S(1)}, u32[]{:S(2)}, u32[]{:S(2)}) collective-permute-start(bf16[64,256]{1,0:T(8,128)(2,1)S(1)} %get-tuple-element.22.refs_6_), channel_id=1, source_target_pairs={{0,2},{2,0},{4,6},{6,4},{8,10},{10,8},{12,14},{14,12},{16,18},{18,... | collective-permute-start | bytes 98312 | tf_op jit(solution)/shard_map/ppermute | solution.py:176
  26.8 2.5 %collective-permute-start.9 = (bf16[64,256]{1,0:T(8,128)(2,1)S(1)}, bf16[64,256]{1,0:T(8,128)(2,1)S(1)}, u32[]{:S(2)}, u32[]{:S(2)}) collective-permute-start(bf16[64,256]{1,0:T(8,128)(2,1)S(1)} %collective-permute-done.7.refs_9_), channel_id=1, source_target_pairs={{0,2},{2,0},{4,6},{6,4},{8,10},{10,8},{12,14},{14,12},{16,18},{18,... | collective-permute-start | bytes 98312 | tf_op jit(solution)/shard_map/ppermute | solution.py:176
  27.2 2.3 %collective-permute-start.8 = (bf16[64,256]{1,0:T(8,128)(2,1)S(1)}, bf16[64,256]{1,0:T(8,128)(2,1)S(1)}, u32[]{:S(2)}, u32[]{:S(2)}) collective-permute-start(bf16[64,256]{1,0:T(8,128)(2,1)S(1)} %collective-permute-done.6.refs_8_), channel_id=1, source_target_pairs={{0,2},{2,0},{4,6},{6,4},{8,10},{10,8},{12,14},{14,12},{16,18},{18,... | collective-permute-start | bytes 98312 | tf_op jit(solution)/shard_map/ppermute | solution.py:176
  32.4 1.6 %collective-permute-start.13 = (bf16[896,128]{1,0:T(8,128)(2,1)S(1)}, bf16[896,128]{1,0:T(8,128)(2,1)S(1)}, u32[]{:S(2)}, u32[]{:S(2)}) collective-permute-start(bf16[896,128]{1,0:T(8,128)(2,1)S(1)} %get-tuple-element.33), channel_id=1, source_target_pairs={{0,2},{2,0},{4,6},{6,4},{8,10},{10,8},{12,14},{14,12},{16,18},{18,... | collective-permute-start | bytes 688136 | tf_op jit(solution)/shard_map/ppermute | solution.py:176
  34.0 4.2 %collective-permute-start.14 = (bf16[224,128]{1,0:T(8,128)(2,1)S(1)}, bf16[224,128]{1,0:T(8,128)(2,1)S(1)}, u32[]{:S(2)}, u32[]{:S(2)}) collective-permute-start(bf16[224,128]{1,0:T(8,128)(2,1)S(1)} %get-tuple-element.35), channel_id=1, source_target_pairs={{0,8},{2,10},{4,12},{6,14},{8,0},{10,2},{12,4},{14,6},{16,24},{18,... | collective-permute-start | bytes 172040 | tf_op jit(solution)/shard_map/ppermute | solution.py:176
  35.5 4.2 %collective-permute-start.15 = (bf16[224,128]{1,0:T(8,128)(2,1)S(1)}, bf16[224,128]{1,0:T(8,128)(2,1)S(1)}, u32[]{:S(2)}, u32[]{:S(2)}) collective-permute-start(bf16[224,128]{1,0:T(8,128)(2,1)S(1)} %get-tuple-element.36), channel_id=1, source_target_pairs={{0,16},{2,18},{4,20},{6,22},{8,24},{10,26},{12,28},{14,30},{16,0},... | collective-permute-start | bytes 172040 | tf_op jit(solution)/shard_map/ppermute | solution.py:176
  38.2 4.9 %collective-permute-start.16 = (bf16[224,128]{1,0:T(8,128)(2,1)S(1)}, bf16[224,128]{1,0:T(8,128)(2,1)S(1)}, u32[]{:S(2)}, u32[]{:S(2)}) collective-permute-start(bf16[224,128]{1,0:T(8,128)(2,1)S(1)} %get-tuple-element.37), channel_id=1, source_target_pairs={{0,24},{2,26},{4,28},{6,30},{8,16},{10,18},{12,20},{14,22},{16,8},... | collective-permute-start | bytes 172040 | tf_op jit(solution)/shard_map/ppermute | solution.py:176
  43.1 3.1 %collective-permute-start.17 = (bf16[224,128]{1,0:T(8,128)(2,1)S(1)}, bf16[224,128]{1,0:T(8,128)(2,1)S(1)}, u32[]{:S(2)}, u32[]{:S(2)}) collective-permute-start(bf16[224,128]{1,0:T(8,128)(2,1)S(1)} %shard_map.80.own_ref), channel_id=1, source_target_pairs={{0,4},{2,6},{4,0},{6,2},{8,12},{10,14},{12,8},{14,10},{16,20},{18,... | collective-permute-start | bytes 172040 | tf_op jit(solution)/shard_map/ppermute | solution.py:176
  46.2 4.9 %collective-permute-start.20 = (bf16[224,128]{1,0:T(8,128)(2,1)S(1)}, bf16[224,128]{1,0:T(8,128)(2,1)S(1)}, u32[]{:S(2)}, u32[]{:S(2)}) collective-permute-start(bf16[224,128]{1,0:T(8,128)(2,1)S(1)} %shard_map.81.refs_0_), channel_id=1, source_target_pairs={{0,24},{2,26},{4,28},{6,30},{8,16},{10,18},{12,20},{14,22},{16,8},... | collective-permute-start | bytes 172040 | tf_op jit(solution)/shard_map/ppermute | solution.py:176
  48.3 5.1 %collective-permute-start.19 = (bf16[224,128]{1,0:T(8,128)(2,1)S(1)}, bf16[224,128]{1,0:T(8,128)(2,1)S(1)}, u32[]{:S(2)}, u32[]{:S(2)}) collective-permute-start(bf16[224,128]{1,0:T(8,128)(2,1)S(1)} %shard_map.81.refs_0_), channel_id=1, source_target_pairs={{0,16},{2,18},{4,20},{6,22},{8,24},{10,26},{12,28},{14,30},{16,0},... | collective-permute-start | bytes 172040 | tf_op jit(solution)/shard_map/ppermute | solution.py:176
  48.7 4.7 %collective-permute-start.18 = (bf16[224,128]{1,0:T(8,128)(2,1)S(1)}, bf16[224,128]{1,0:T(8,128)(2,1)S(1)}, u32[]{:S(2)}, u32[]{:S(2)}) collective-permute-start(bf16[224,128]{1,0:T(8,128)(2,1)S(1)} %shard_map.81.refs_0_), channel_id=1, source_target_pairs={{0,8},{2,10},{4,12},{6,14},{8,0},{10,2},{12,4},{14,6},{16,24},{18,... | collective-permute-start | bytes 172040 | tf_op jit(solution)/shard_map/ppermute | solution.py:176
  53.5 11.1 %collective-permute-start.21 = (bf16[896,128]{1,0:T(8,128)(2,1)S(1)}, bf16[896,128]{1,0:T(8,128)(2,1)S(1)}, u32[]{:S(2)}, u32[]{:S(2)}) collective-permute-start(bf16[896,128]{1,0:T(8,128)(2,1)S(1)} %shard_map.82.own_ref), channel_id=1, source_target_pairs={{0,2},{2,0},{4,6},{6,4},{8,10},{10,8},{12,14},{14,12},{16,18},{18,... | collective-permute-start | bytes 688136 | tf_op jit(solution)/shard_map/ppermute | solution.py:176
  56.5 4.1 %collective-permute-start.11 = (bf16[64,1024]{1,0:T(8,128)(2,1)S(1)}, bf16[64,1024]{1,0:T(8,128)(2,1)S(1)}, u32[]{:S(2)}, u32[]{:S(2)}) collective-permute-start(bf16[64,1024]{1,0:T(8,128)(2,1)S(1)} %get-tuple-element.29), channel_id=1, source_target_pairs={{0,2},{2,0},{4,6},{6,4},{8,10},{10,8},{12,14},{14,12},{16,18},{18,... | collective-permute-start | bytes 393224 | tf_op jit(solution)/shard_map/ppermute | solution.py:176
  56.6 6.3 %collective-permute-start.12 = (bf16[64,1024]{1,0:T(8,128)(2,1)S(1)}, bf16[64,1024]{1,0:T(8,128)(2,1)S(1)}, u32[]{:S(2)}, u32[]{:S(2)}) collective-permute-start(bf16[64,1024]{1,0:T(8,128)(2,1)S(1)} %get-tuple-element.30), channel_id=1, source_target_pairs={{0,0},{30,30},{2,4},{6,8},{10,12},{14,16},{18,20},{22,24},{26,28},... | collective-permute-start | bytes 393224 | tf_op jit(solution)/shard_map/ppermute | solution.py:176

commit v4 on v3

--- a/solution.py
+++ b/solution.py
@@ -11,15 +11,27 @@
 VMEM_LIMIT = 32 * 1024 * 1024
 
 
-def call(body, outs, scratch=()):
+def call(body, outs, scratch=(), far=(), aliases=None, out_far=False):
     def run(*args):
-        return pl.pallas_call(
+        kernel = pl.pallas_call(
             body,
             out_shape=outs,
-            in_specs=[pl.BlockSpec(memory_space=pltpu.VMEM)] * len(args),
+            in_specs=[
+                pl.BlockSpec(memory_space=pltpu.HBM if k in far else pltpu.VMEM)
+                for k in range(len(args))
+            ],
+            out_specs=jax.tree.map(
+                lambda _: pl.BlockSpec(memory_space=pltpu.HBM if out_far else pltpu.VMEM), outs
+            ),
             scratch_shapes=scratch,
+            input_output_aliases=aliases or {},
             compiler_params=pltpu.CompilerParams(vmem_limit_bytes=VMEM_LIMIT),
-        )(*[pltpu.with_memory_space_constraint(arg, pltpu.VMEM) for arg in args])
+        )
+        near = [
+            pltpu.with_memory_space_constraint(arg, pltpu.HBM if k in far else pltpu.VMEM)
+            for k, arg in enumerate(args)
+        ]
+        return kernel(*near)
 
     return run
 
@@ -65,13 +77,13 @@
     return jnp.concatenate([blank, cells[:, :-depth]], axis=1)
 
 
-def conv_planes(matrices, stacks, planes, outputs, depth):
-    results = [None] * planes
-    for place in range(planes + 2):
+def conv_planes(matrices, stacks, planes, outputs, depth, results=None):
+    results = list(results) if results else [None] * planes
+    for place, stack in stacks.items():
         first = max(0, place - planes + 1)
         last = min(2, place)
         rows = matrices[first * 3 * outputs : (last + 1) * 3 * outputs, :]
-        terms = dot(rows, stacks[place])
+        terms = dot(rows, stack)
         for tap_x in range(first, last + 1):
             for tap_y in range(3):
                 begin = ((tap_x - first) * 3 + tap_y) * outputs
@@ -81,27 +93,30 @@
     return results
 
 
-def weight_planes(acc, grads, stacks, depth):
+def weight_planes(grads, stacks, depth):
     planes = len(grads)
-    outputs = grads[0].shape[0]
     rows = [
         jnp.concatenate([shifted_rows(grad, 1 - tap_y, depth) for tap_y in range(3)], axis=0)
         for grad in grads
     ]
+    sums = []
     for tap_x in range(3):
         total = None
         for plane in range(planes):
             term = dot_cells(rows[plane], stacks[plane + tap_x])
             total = term if total is None else total + term
-        acc[tap_x * 3 * outputs : (tap_x + 1) * 3 * outputs, :] = total
-
-
-def pack(acc, target, base, rows):
-    half = rows // 2
-    target[base : base + rows, :] = acc[:, :128]
-    target[base + rows : base + rows + half, :] = jnp.concatenate(
-        [acc[:half, 128:], acc[half:, 128:]], axis=1
-    )
+        sums.append(total)
+    return sums
+
+
+def packed(sums, count):
+    acc = jnp.concatenate(sums, axis=0)
+    rows = acc.shape[0]
+    tail = jnp.concatenate([acc[: rows // 2, 128:], acc[rows // 2 :, 128:]], axis=1)
+    pieces = [acc[:, :128], tail]
+    if count > rows * 3 // 2:
+        pieces.append(jnp.zeros((count - rows * 3 // 2, 128), F32))
+    return jnp.concatenate(pieces, axis=0)
 
 
 def unpack(source, base, rows, out, scale):
@@ -179,30 +194,92 @@
         pairs = [(i * filt + f, j * filt + (f ^ slot)) for i, j in table for f in range(filt)]
         return lax.ppermute(piece, ("space", "filt"), pairs)
 
-    place = lax.axis_index("space")
-    bricks = jnp.transpose(volume, (1, 0, 2, 3)).reshape(planes, channels, brick)
-    cot = cotangent.reshape(filters, blocks, extra)
-    cot = jnp.transpose(cot, (1, 0, 2)).reshape(channels, extra)
-    edge = jnp.where(place % 2 == 1, bricks[planes - 1], bricks[0])
-    own_message = jnp.concatenate([bricks[p] for p in range(planes)] + [cot], axis=1)
-    edge_message = jnp.concatenate([edge, cot], axis=1)
+
+    def message_kernel(*refs):
+        far_refs, own_ref, edge_ref, narrow_ref, first_ref = refs[:4], *refs[4:8]
+        cells_ref, cot_ref, second_ref, sems = refs[8:]
+        odd = lax.axis_index("space") % 2 == 1
+        copies = [
+            pltpu.make_async_copy(source, target, sems.at[k])
+            for k, (source, target) in enumerate(
+                zip(far_refs, (cells_ref, cot_ref, second_ref, first_ref))
+            )
+        ]
+        for copy in copies:
+            copy.start()
+        copies[0].wait()
+        for plane in range(planes):
+            for row in range(brick_y):
+                start = (plane * brick_y + row) * depth
+                own_ref[:, start : start + depth] = cells_ref[:, plane, row, :]
+        copies[1].wait()
+        width = low_y // blocks
+        for row in range(low_y):
+            block, start = row // width, (row % width) * low_depth
+            piece = cot_ref[:, 0, row, :]
+            own_ref[
+                block * filters : (block + 1) * filters,
+                planes * brick + start : planes * brick + start + low_depth,
+            ] = piece
+        edge_ref[:, :brick] = pick(
+            odd, own_ref[:, (planes - 1) * brick : planes * brick], own_ref[:, :brick]
+        )
+        edge_ref[:, brick:] = own_ref[:, planes * brick :]
+
+        copies[2].wait()
+        for tap in range(14):
+            narrow_ref[tap] = jnp.concatenate([second_ref[tap], second_ref[tap + 13]], axis=1)
+        copies[3].wait()
+
+    own_message, edge_message, narrow, first_taps = call(
+        message_kernel,
+        (
+            shaped((channels, planes * brick + extra), BF16),
+            shaped((channels, brick + extra), BF16),
+            shaped((14, filters, 128), BF16),
+            shaped(first_weight.shape, BF16),
+        ),
+        (
+            pltpu.VMEM(volume.shape, BF16),
+            pltpu.VMEM(cotangent.shape, BF16),
+            pltpu.VMEM(second_weight.shape, BF16),
+            pltpu.SemaphoreType.DMA((4,)),
+        ),
+        far=(0, 1, 2, 3),
+    )(volume, cotangent, second_weight, first_weight)
     own = [own_message] + [across(own_message, mirror(0), slot) for slot in range(1, filt)]
     side_b = [across(edge_message, table_b, slot) for slot in range(filt)]
     side_a = [along(message, mirror(1)) for message in own]
 
-    narrow = jnp.concatenate([second_weight[:14], second_weight[13:]], axis=2)
     narrows = [narrow] + [across(narrow, mirror(0), slot) for slot in range(1, filt)]
 
+    def own_kernel(*refs):
+        own_refs, taps = refs[:filt], refs[filt]
+        whole_ref, sums_ref, matrices = refs[filt + 1 :]
+        forward_matrix(taps, matrices, channels)
+        for plane in range(planes):
+            pieces = [ref[:, plane * brick : (plane + 1) * brick] for ref in own_refs]
+            join_rows(whole_ref, plane, pieces, brick)
+        stacks = {1 + plane: stack3(whole_ref[plane], depth) for plane in range(planes)}
+        sums = conv_planes(matrices, stacks, planes, channels, depth)
+        for plane in range(planes):
+            sums_ref[plane] = sums[plane]
+
+    whole, own_sums, first_forward = call(
+        own_kernel,
+        (
+            shaped((planes, channels, fine_cells), BF16),
+            shaped((planes, channels, fine_cells), F32),
+            shaped((9 * channels, 3 * channels), BF16),
+        ),
+    )(*own, first_taps)
+
     def first_kernel(*refs):
-        own_refs, a_refs, b_refs = refs[:filt], refs[filt : 2 * filt], refs[2 * filt : 3 * filt]
-        taps, pooled_ref, slope_ref, whole_ref, matrices = refs[3 * filt :]
+        a_refs, b_refs = refs[:filt], refs[filt : 2 * filt]
+        sums_ref, matrices, pooled_ref, slope_ref, sides_ref = refs[2 * filt :]
         index = lax.axis_index("space")
         odd = index % 2 == 1
         inside = jnp.logical_and(index > 0, index < space - 1)
-        forward_matrix(taps, matrices, channels)
-        for plane in range(planes):
-            pieces = [ref[:, plane * brick : (plane + 1) * brick] for ref in own_refs]
-            join_rows(whole_ref, 1 + plane, pieces, brick)
         lefts, rights = [], []
         for a_ref, b_ref in zip(a_refs, b_refs):
             got_a = pick(odd, a_ref[:, (planes - 1) * brick : planes * brick], a_ref[:, :brick])
@@ -210,10 +287,11 @@
             got_b = pick(inside, got_b, jnp.zeros_like(got_b))
             lefts.append(pick(odd, got_a, got_b))
             rights.append(pick(odd, got_b, got_a))
-        join_rows(whole_ref, 0, lefts, brick)
-        join_rows(whole_ref, planes + 1, rights, brick)
-        stacks = [stack3(whole_ref[p], depth) for p in range(planes + 2)]
-        pre = conv_planes(matrices, stacks, planes, channels, depth)
+        join_rows(sides_ref, 0, lefts, brick)
+        join_rows(sides_ref, 1, rights, brick)
+        stacks = {0: stack3(sides_ref[0], depth), planes + 1: stack3(sides_ref[1], depth)}
+        sums = [sums_ref[plane] for plane in range(planes)]
+        pre = conv_planes(matrices, stacks, planes, channels, depth, sums)
         hidden = [silu(value).astype(BF16) for value in pre]
         for plane in range(planes):
             slope_ref[plane] = silu_slope(pre[plane])
@@ -236,15 +314,14 @@
                 total = total + sums[piece * channels : (piece + 1) * channels]
             pooled_ref[:, row * low_depth : (row + 1) * low_depth] = (0.125 * total).astype(BF16)
 
-    pooled, slope, whole = call(
+    pooled, slope, sides = call(
         first_kernel,
         (
             shaped((channels, low_cells), BF16),
             shaped((planes, channels, fine_cells), F32),
-            shaped((planes + 2, channels, fine_cells), BF16),
-        ),
-        (pltpu.VMEM((9 * channels, 3 * channels), BF16),),
-    )(*own, *side_a, *side_b, first_weight)
+            shaped((2, channels, fine_cells), BF16),
+        ),
+    )(*side_a, *side_b, own_sums, first_forward)
 
     pool_d = along(pooled, table_d)
     pool_x = along(pooled, mirror(2))
@@ -253,39 +330,43 @@
     pool_ad = along(pool_d, mirror(1))
 
     def matrix_kernel(*refs):
-        narrow_refs, taps = refs[:filt], refs[filt]
-        forward_ref, back_ref, first_ref = refs[filt + 1 :]
+        narrow_refs, taps, whole_ref, sides_ref = refs[:filt], refs[filt], refs[filt + 1], refs[filt + 2]
+        forward_ref, back_ref, first_ref, fine_ref = refs[filt + 3 :]
         for slot, ref in enumerate(narrow_refs):
             values = [ref[t, :, :64] if t < 14 else ref[t - 13, :, 64:] for t in range(27)]
             forward_matrix(values, forward_ref.at[slot], filters)
             back_ref[slot] = backward_matrix(values)
         first_ref[...] = backward_matrix([taps[t] for t in range(27)])
-
-    second_forward, second_back, first_back = call(
+        fine_ref[0] = stack3(sides_ref[0], depth)
+        fine_ref[planes + 1] = stack3(sides_ref[1], depth)
+        for plane in range(planes):
+            fine_ref[1 + plane] = stack3(whole_ref[plane], depth)
+
+    second_forward, second_back, first_back, fine_stacks = call(
         matrix_kernel,
         (
             shaped((filt, 9 * filters, 3 * channels), BF16),
             shaped((filt, 9 * channels, 3 * filters), BF16),
             shaped((9 * channels, 3 * channels), BF16),
-        ),
-    )(*narrows, first_weight)
+            shaped((planes + 2, 3 * channels, fine_cells), BF16),
+        ),
+    )(*narrows, first_taps, whole, sides)
 
     first_rows, second_rows = 9 * channels, 9 * filters
     packed_first, packed_second = first_rows * 3 // 2, second_rows * 3 // 2
     far_side = space // 4
-    unit = 8 * space
-    total_rows = -(-(packed_first + packed_second) // unit) * unit
-    half = total_rows // 2
+    unit = 16 * far_side
+    half = -(-max(packed_first, packed_second) // unit) * unit
     chunk = half // far_side
 
     def middle_kernel(*refs):
         own_refs, a_refs, b_refs = refs[:filt], refs[filt : 2 * filt], refs[2 * filt : 3 * filt]
         pool_ref, pa_ref, px_ref, pd_ref, pax_ref, pad_ref = refs[3 * filt : 3 * filt + 6]
-        forward_ref, back_ref, slope_ref, whole_ref = refs[3 * filt + 6 : 3 * filt + 10]
+        forward_ref, back_ref, slope_ref, fine_ref = refs[3 * filt + 6 : 3 * filt + 10]
         features_ref, down_ref, edge_a_ref, edge_b_ref, keep_ref, send_ref = refs[
             3 * filt + 10 : 3 * filt + 16
         ]
-        first_acc, second_acc, rows_ref, parts_ref = refs[3 * filt + 16 :]
+        parts_ref = refs[3 * filt + 16]
         index = lax.axis_index("space")
         odd = index % 2 == 1
         up = (index // 2) % 2 == 1
@@ -303,7 +384,7 @@
             pick(odd, other, got_a),
             pick(up, got_d, got_x),
         ]
-        stacks = [stack3(value, low_depth) for value in pools]
+        stacks = {k: stack3(value, low_depth) for k, value in enumerate(pools)}
 
         def cot_of(packed):
             return jnp.concatenate(
@@ -322,8 +403,8 @@
             ]
             if slot == 0:
                 features_ref[...] = silu(pre[1]).astype(BF16)
-                weight_planes(second_acc, [downs[1]], stacks[1:4], low_depth)
-            down_stacks = [stack3(value, low_depth) for value in downs]
+                second_sums = weight_planes([downs[1]], [stacks[1], stacks[2], stacks[3]], low_depth)
+            down_stacks = {k: stack3(value, low_depth) for k, value in enumerate(downs)}
             (part,) = conv_planes(back_ref.at[slot], down_stacks, 1, channels, low_depth)
             parts_ref[lax.axis_index("filt") ^ slot] = part.astype(BF16)
 
@@ -345,21 +426,13 @@
             down_ref[plane] = grads[plane]
         edge_a_ref[...] = pick(odd, grads[0], grads[planes - 1])
         edge_b_ref[...] = pick(odd, grads[planes - 1], grads[0])
-        fine_stacks = [stack3(whole_ref[p], depth) for p in range(planes + 2)]
-        weight_planes(first_acc, grads, fine_stacks, depth)
-        pack(first_acc, rows_ref, 0, first_rows)
-        pack(second_acc, rows_ref, packed_first, second_rows)
-        if total_rows > packed_first + packed_second:
-            rows_ref[packed_first + packed_second :, :] = jnp.zeros(
-                (total_rows - packed_first - packed_second, 128), F32
-            )
-        core = index % 2
-        keep_ref[...] = rows_ref[pl.ds(pl.multiple_of(core * half, 16), half), :]
-        send_ref[...] = rows_ref[pl.ds(pl.multiple_of((1 - core) * half, 16), half), :].astype(
-            BF16
-        )
-
-    features, first_down, edge_a, edge_b, keep, send = call(
+        fine_stacks = [fine_ref[p] for p in range(planes + 2)]
+        first_sums = packed(weight_planes(grads, fine_stacks, depth), half)
+        second_sums = packed(second_sums, half)
+        keep_ref[...] = pick(odd, second_sums, first_sums)
+        send_ref[...] = pick(odd, first_sums, second_sums).astype(BF16)
+
+    flat_features, first_down, edge_a, edge_b, keep, send = call(
         middle_kernel,
         (
             shaped((filters, low_cells), BF16),
@@ -370,9 +443,6 @@
             shaped((half, 128), BF16),
         ),
         (
-            pltpu.VMEM((first_rows, 3 * channels), F32),
-            pltpu.VMEM((second_rows, 3 * channels), F32),
-            pltpu.VMEM((total_rows, 128), F32),
             pltpu.VMEM((filt, channels, low_cells), BF16),
         ),
     )(
@@ -388,9 +458,8 @@
         second_forward,
         second_back,
         slope,
-        whole,
+        fine_stacks,
     )
-    features = features.reshape(filters, 1, low_y, low_depth)
 
     got = along(send, mirror(1))
 
@@ -420,7 +489,7 @@
     summed = call(sum_kernel, shaped((chunk, 128), BF16))(own_chunk, *got)
     other = along(summed, mirror(2))
 
-    def volume_kernel(own_ref, a_ref, b_ref, matrices, out_ref, rows_ref):
+    def volume_kernel(own_ref, a_ref, b_ref, matrices, flat_ref, out_ref, features_ref, rows_ref):
         index = lax.axis_index("space")
         odd = index % 2 == 1
         inside = jnp.logical_and(index > 0, index < space - 1)
@@ -430,20 +499,27 @@
         values.append(pick(odd, got_b, got_a))
         blank = jnp.zeros((channels, depth), BF16)
         begin = pl.multiple_of(lax.axis_index("filt") * brick, brick)
-        stacks = []
+        stacks = {}
         for position, value in enumerate(values):
             rows_ref[position] = jnp.concatenate([blank, value, blank], axis=1)
-            stacks.append(stack3(rows_ref[position, :, pl.ds(begin, brick + 2 * depth)], depth))
+            cells = rows_ref[position, :, pl.ds(begin, brick + 2 * depth)]
+            stacks[position] = stack3(cells, depth)
         results = conv_planes(matrices, stacks, planes, channels, depth)
         for plane in range(planes):
-            out_ref[plane] = results[plane][:, depth : depth + brick].astype(BF16)
-
-    volume_grad = call(
+            for row in range(brick_y):
+                cells = results[plane][:, (row + 1) * depth : (row + 2) * depth]
+                out_ref[:, plane, row, :] = cells.astype(BF16)
+        for row in range(low_y):
+            features_ref[:, 0, row, :] = flat_ref[:, row * low_depth : (row + 1) * low_depth]
+
+    volume_grad, features = call(
         volume_kernel,
-        shaped((planes, channels, brick), BF16),
+        (
+            jax.ShapeDtypeStruct(volume.shape, BF16),
+            jax.ShapeDtypeStruct(cotangent.shape, BF16),
+        ),
         (pltpu.VMEM((planes + 2, channels, fine_cells + 2 * depth), BF16),),
-    )(first_down, halo_a, halo_b, first_back)
-    volume_grad = jnp.transpose(volume_grad.reshape(planes, channels, brick_y, depth), (1, 0, 2, 3))
+    )(first_down, halo_a, halo_b, first_back, flat_features)
 
     final_chunk = call(sum_kernel, shaped((chunk, 128), BF16))(summed, other)
     pieces = [final_chunk] + [along(final_chunk, mirror(4 * k)) for k in range(1, far_side)]
@@ -461,7 +537,7 @@
         rows_ref[pl.ds(pl.multiple_of(core * half, 16), half), :] = own_ref[...].astype(F32)
         rows_ref[pl.ds(pl.multiple_of((1 - core) * half, 16), half), :] = got_ref[...].astype(F32)
         unpack(rows_ref, 0, first_rows, first_ref, fine_scale)
-        unpack(rows_ref, packed_first, second_rows, second_ref, low_scale)
+        unpack(rows_ref, half, second_rows, second_ref, low_scale)
 
     first_grad, second_grad = call(
         final_kernel,
@@ -469,7 +545,7 @@
             jax.ShapeDtypeStruct((27, channels, channels), F32),
             jax.ShapeDtypeStruct((27, filters, channels), F32),
         ),
-        (pltpu.VMEM((total_rows, 128), F32),),
+        (pltpu.VMEM((2 * half, 128), F32),),
     )(group, partner)
     return (features, volume_grad, first_grad, second_grad)
 

time: 66.7 us -> 66.9 us (level)
  local copies, waits for them, and re-layouts: 3.26 us -> 0 us
  Pallas kernels: 7.18 us -> 9.84 us
  waiting for transfers between devices: 22.7 us -> 23.8 us
    pallas_call x9 -> x11, Pallas kernels: 7.18 us -> 9.84 us  [run(): return kernel(*near)]
    ppermute x18, waiting for transfers between devices: 15.1 us -> 16.7 us  [along(): return lax.ppermute(piece, 'space', table)]
    reshape x3 -> x0, local copies, waits for them, and re-layouts: 1.41 us -> none  [the longest x2 0.78 us: local(): volume_grad.reshape(planes, channels, brick_y, depth)]
    ppermute x18, starting transfers between devices: 24.1 us -> 25.4 us  [along(): return lax.ppermute(piece, 'space', table)]
    slice x2 -> x0, local copies, waits for them, and re-layouts: 1.05 us -> none  [the longest x1 1.02 us: local(): bricks[p]]
    ppermute x4, starting transfers between devices: 7.92 us -> 6.98 us  [across(): return lax.ppermute(piece, ('space', 'filt'), pairs)]
    unnamed x10 -> x0, local copies, waits for them, and re-layouts: 0.78 us -> none
  transfers between devices with their start and end apart: 22 -> 22, of which waited for: 12 -> 12; matrix products, arithmetic and copies ran while one was open for 2% -> 0% of each run, Pallas kernels for 4% -> 6%
where the time goes in v4:
time: 66.9 us; the launch traced here: 66.7 us
  starting transfers between devices  32.3 us (48%)
  waiting for transfers between devices  23.8 us (36%)
  Pallas kernels  9.84 us (15%)
  between operations  0.77 us (1%)
    ppermute x18, starting transfers between devices, along(): return lax.ppermute(piece, 'space', table)  25.4 us
    ppermute x18, waiting for transfers between devices, along(): return lax.ppermute(piece, 'space', table)  16.7 us
    pallas_call x11, Pallas kernels, run(): return kernel(*near)  9.84 us
    ppermute x4, waiting for transfers between devices, across(): return lax.ppermute(piece, ('space', 'filt'), pairs)  7.11 us
    ppermute x4, starting transfers between devices, across(): return lax.ppermute(piece, ('space', 'filt'), pairs)  6.98 us
  transfers between devices with their start and end apart: 22, of which 12 were waited for; matrix products, arithmetic and copies ran while one was open for 0% of the time, Pallas kernels for 6%

profile of v4, /device:TPU:1, one launch (start us, length us, event | category | flops | bytes accessed | tf_op | source)
XLA Modules:
  0.0 66.7 jit_solution(12769604955168774345)
XLA Ops:
  0.6 1.4 %shard_map.75 = (bf16[64,1280]{1,0:T(8,128)(2,1)S(1)}, bf16[64,768]{1,0:T(8,128)(2,1)S(1)}, bf16[14,64,128]{2,1,0:T(8,128)(2,1)S(1)}, bf16[27,64,64]{2,1,0:T(8,128)(2,1)S(1)}) custom-call(bf16[64,2,2,256]{3,2,1,0:T(2,128)(2,1)} %refs_0_.1, bf16[64,1,2,128]{3,2,1,0:T(2,128)(2,1)} %refs_1_.1, bf16[27,64,64]{2,1,0:T(8,128)(2,1)} %refs_2_.1, ...), custom_call_target="tpu_custom_call" | custom-call | tf_op jit(solution)/shard_map/pallas_call | solution.py:34
  2.1 2.1 %collective-permute-start = (bf16[64,1280]{1,0:T(8,128)(2,1)S(1)}, bf16[64,1280]{1,0:T(8,128)(2,1)S(1)}, u32[]{:S(2)}, u32[]{:S(2)}) collective-permute-start(bf16[64,1280]{1,0:T(8,128)(2,1)S(1)} %get-tuple-element.32.refs_0_), channel_id=1, source_target_pairs={{0,1},{1,0},{2,3},{3,2},{4,5},{5,4},{6,7},{7,6},{8,9},{9,8},{10,11... | collective-permute-start | bytes 491528 | tf_op jit(solution)/shard_map/ppermute | solution.py:195
  4.2 1.0 %collective-permute-start.1 = (bf16[64,1280]{1,0:T(8,128)(2,1)S(1)}, bf16[64,1280]{1,0:T(8,128)(2,1)S(1)}, u32[]{:S(2)}, u32[]{:S(2)}) collective-permute-start(bf16[64,1280]{1,0:T(8,128)(2,1)S(1)} %get-tuple-element.32.refs_0_), channel_id=1, source_target_pairs={{0,2},{2,0},{4,6},{6,4},{8,10},{10,8},{12,14},{14,12},{16,18},{18,... | collective-permute-start | bytes 491528 | tf_op jit(solution)/shard_map/ppermute | solution.py:191
  5.1 2.9 %collective-permute-done.refs_1_ = bf16[64,1280]{1,0:T(8,128)(2,1)S(1)} collective-permute-done((bf16[64,1280]{1,0:T(8,128)(2,1)S(1)}, bf16[64,1280]{1,0:T(8,128)(2,1)S(1)}, u32[]{:S(2)}, u32[]{:S(2)}) %collective-permute-start) | collective-permute-done | bytes 163872 | tf_op jit(solution)/shard_map/ppermute | solution.py:195
  8.1 1.3 %collective-permute-start.2 = (bf16[64,1280]{1,0:T(8,128)(2,1)S(1)}, bf16[64,1280]{1,0:T(8,128)(2,1)S(1)}, u32[]{:S(2)}, u32[]{:S(2)}) collective-permute-start(bf16[64,1280]{1,0:T(8,128)(2,1)S(1)} %collective-permute-done.refs_1_), channel_id=1, source_target_pairs={{0,2},{2,0},{4,6},{6,4},{8,10},{10,8},{12,14},{14,12},{16,18},{18,... | collective-permute-start | bytes 491528 | tf_op jit(solution)/shard_map/ppermute | solution.py:191
  9.3 1.5 %collective-permute-start.10 = (bf16[14,64,128]{2,1,0:T(8,128)(2,1)S(1)}, bf16[14,64,128]{2,1,0:T(8,128)(2,1)S(1)}, u32[]{:S(2)}, u32[]{:S(2)}) collective-permute-start(bf16[14,64,128]{2,1,0:T(8,128)(2,1)S(1)} %get-tuple-element.38.refs_0_), channel_id=1, source_target_pairs={{0,1},{1,0},{2,3},{3,2},{4,5},{5,4},{6,7},{7,6},{8,9},{9,8},{10,11... | collective-permute-start | bytes 688136 | tf_op jit(solution)/shard_map/ppermute | solution.py:195
  10.8 3.3 %collective-permute-start.3 = (bf16[64,768]{1,0:T(8,128)(2,1)S(1)}, bf16[64,768]{1,0:T(8,128)(2,1)S(1)}, u32[]{:S(2)}, u32[]{:S(2)}) collective-permute-start(bf16[64,768]{1,0:T(8,128)(2,1)S(1)} %get-tuple-element.33), channel_id=1, source_target_pairs={{0,0},{1,1},{30,30},{31,31},{2,4},{3,5},{6,8},{7,9},{10,12},{11,13... | collective-permute-start | bytes 294920 | tf_op jit(solution)/shard_map/ppermute | solution.py:195
  14.2 0.7 %shard_map.76 = (bf16[2,64,1024]{2,1,0:T(8,128)(2,1)S(1)}, f32[2,64,1024]{2,1,0:T(8,128)S(1)}, bf16[576,192]{1,0:T(8,128)(2,1)S(1)}) custom-call(bf16[64,1280]{1,0:T(8,128)(2,1)S(1)} %get-tuple-element.32.refs_0_, bf16[64,1280]{1,0:T(8,128)(2,1)S(1)} %collective-permute-done.refs_1_, bf16[27,64,64]{2,1,0:T(8,128)(2,1)S(1)} %get-tuple-element.34.refs_2_), custom_call_target="tpu_custom_call" | custom-call | tf_op jit(solution)/shard_map/pallas_call | solution.py:34
  14.9 2.1 %collective-permute-done.3.refs_2_.refs_4_ = bf16[64,768]{1,0:T(8,128)(2,1)S(1)} collective-permute-done((bf16[64,768]{1,0:T(8,128)(2,1)S(1)}, bf16[64,768]{1,0:T(8,128)(2,1)S(1)}, u32[]{:S(2)}, u32[]{:S(2)}) %collective-permute-start.3) | collective-permute-done | bytes 98336 | tf_op jit(solution)/shard_map/ppermute | solution.py:195
  17.0 2.1 %collective-permute-done.4.refs_3_.refs_5_ = bf16[64,768]{1,0:T(8,128)(2,1)S(1)} collective-permute-done((bf16[64,768]{1,0:T(8,128)(2,1)S(1)}, bf16[64,768]{1,0:T(8,128)(2,1)S(1)}, u32[]{:S(2)}, u32[]{:S(2)}) %collective-permute-start.4) | collective-permute-done | bytes 98336 | tf_op jit(solution)/shard_map/ppermute | solution.py:195
  19.1 0.7 %shard_map.77 = (bf16[64,256]{1,0:T(8,128)(2,1)S(1)}, f32[2,64,1024]{2,1,0:T(8,128)S(1)}, bf16[2,64,1024]{2,1,0:T(8,128)(2,1)S(1)}) custom-call(bf16[64,1280]{1,0:T(8,128)(2,1)S(1)} %collective-permute-done.1.refs_0_.refs_2_, bf16[64,1280]{1,0:T(8,128)(2,1)S(1)} %collective-permute-done.2.refs_1_.refs_3_, ...), custom_call_target="tpu_custom_call" | custom-call | tf_op jit(solution)/shard_map/pallas_call | solution.py:34
  19.8 2.2 %collective-permute-start.6 = (bf16[64,256]{1,0:T(8,128)(2,1)S(1)}, bf16[64,256]{1,0:T(8,128)(2,1)S(1)}, u32[]{:S(2)}, u32[]{:S(2)}) collective-permute-start(bf16[64,256]{1,0:T(8,128)(2,1)S(1)} %get-tuple-element.37.refs_6_), channel_id=1, source_target_pairs={{0,4},{2,6},{4,0},{6,2},{8,12},{10,14},{12,8},{14,10},{16,20},{18,... | collective-permute-start | bytes 98312 | tf_op jit(solution)/shard_map/ppermute | solution.py:191
  22.0 0.7 collective-permute-start.7
  22.8 0.6 collective-permute-done.6.refs_8_
  23.4 1.1 %collective-permute-start.8 = (bf16[64,256]{1,0:T(8,128)(2,1)S(1)}, bf16[64,256]{1,0:T(8,128)(2,1)S(1)}, u32[]{:S(2)}, u32[]{:S(2)}) collective-permute-start(bf16[64,256]{1,0:T(8,128)(2,1)S(1)} %collective-permute-done.6.refs_8_), channel_id=1, source_target_pairs={{0,2},{2,0},{4,6},{6,4},{8,10},{10,8},{12,14},{14,12},{16,18},{18,... | collective-permute-start | bytes 98312 | tf_op jit(solution)/shard_map/ppermute | solution.py:191
  24.5 0.9 %shard_map.78 = (bf16[2,576,192]{2,1,0:T(8,128)(2,1)S(1)}, bf16[2,576,192]{2,1,0:T(8,128)(2,1)S(1)}, bf16[576,192]{1,0:T(8,128)(2,1)S(1)}, bf16[4,192,1024]{2,1,0:T(8,128)(2,1)S(1)}) custom-call(bf16[14,64,128]{2,1,0:T(8,128)(2,1)S(1)} %get-tuple-element.38.refs_0_, bf16[14,64,128]{2,1,0:T(8,128)(2,1)S(1)} %collective-permute-done.10.refs_1_, ...), custom_call_target="tpu_custom_call" | custom-call | tf_op jit(solution)/shard_map/pallas_call | solution.py:34
  25.7 2.7 %shard_map.79 = (bf16[64,256]{1,0:T(8,128)(2,1)S(1)}, bf16[2,64,1024]{2,1,0:T(8,128)(2,1)S(1)}, bf16[64,1024]{1,0:T(8,128)(2,1)S(1)}, bf16[64,1024]{1,0:T(8,128)...) custom-call(bf16[64,1280]{1,0:T(8,128)(2,1)S(1)} %get-tuple-element.32.refs_0_, ...), custom_call_target="tpu_custom_call" | custom-call | tf_op jit(solution)/shard_map/pallas_call | solution.py:34
  28.7 1.2 %collective-permute-done.13.got_ref = bf16[896,128]{1,0:T(8,128)(2,1)S(1)} collective-permute-done((bf16[896,128]{1,0:T(8,128)(2,1)S(1)}, bf16[896,128]{1,0:T(8,128)(2,1)S(1)}, u32[]{:S(2)}, u32[]{:S(2)}) %collective-permute-start.13) | collective-permute-done | bytes 229408 | tf_op jit(solution)/shard_map/ppermute | solution.py:191
  30.0 5.3 %collective-permute-start.14 = (bf16[224,128]{1,0:T(8,128)(2,1)S(1)}, bf16[224,128]{1,0:T(8,128)(2,1)S(1)}, u32[]{:S(2)}, u32[]{:S(2)}) collective-permute-start(bf16[224,128]{1,0:T(8,128)(2,1)S(1)} %get-tuple-element.55), channel_id=1, source_target_pairs={{0,8},{2,10},{4,12},{6,14},{8,0},{10,2},{12,4},{14,6},{16,24},{18,... | collective-permute-start | bytes 172040 | tf_op jit(solution)/shard_map/ppermute | solution.py:191
  35.3 2.5 %collective-permute-start.15 = (bf16[224,128]{1,0:T(8,128)(2,1)S(1)}, bf16[224,128]{1,0:T(8,128)(2,1)S(1)}, u32[]{:S(2)}, u32[]{:S(2)}) collective-permute-start(bf16[224,128]{1,0:T(8,128)(2,1)S(1)} %get-tuple-element.56), channel_id=1, source_target_pairs={{0,16},{2,18},{4,20},{6,22},{8,24},{10,26},{12,28},{14,30},{16,0},... | collective-permute-start | bytes 172040 | tf_op jit(solution)/shard_map/ppermute | solution.py:191
  37.7 2.3 %collective-permute-done.15.refs_1_ = bf16[224,128]{1,0:T(8,128)(2,1)S(1)} collective-permute-done((bf16[224,128]{1,0:T(8,128)(2,1)S(1)}, bf16[224,128]{1,0:T(8,128)(2,1)S(1)}, u32[]{:S(2)}, u32[]{:S(2)}) %collective-permute-start.15) | collective-permute-done | bytes 57376 | tf_op jit(solution)/shard_map/ppermute | solution.py:191
  40.0 2.6 %collective-permute-done.16.refs_2_ = bf16[224,128]{1,0:T(8,128)(2,1)S(1)} collective-permute-done((bf16[224,128]{1,0:T(8,128)(2,1)S(1)}, bf16[224,128]{1,0:T(8,128)(2,1)S(1)}, u32[]{:S(2)}, u32[]{:S(2)}) %collective-permute-start.16) | collective-permute-done | bytes 57376 | tf_op jit(solution)/shard_map/ppermute | solution.py:191
  42.8 3.0 %collective-permute-done.17.refs_0_ = bf16[224,128]{1,0:T(8,128)(2,1)S(1)} collective-permute-done((bf16[224,128]{1,0:T(8,128)(2,1)S(1)}, bf16[224,128]{1,0:T(8,128)(2,1)S(1)}, u32[]{:S(2)}, u32[]{:S(2)}) %collective-permute-start.17) | collective-permute-done | bytes 57376 | tf_op jit(solution)/shard_map/ppermute | solution.py:191
  46.3 1.2 %collective-permute-start.19 = (bf16[224,128]{1,0:T(8,128)(2,1)S(1)}, bf16[224,128]{1,0:T(8,128)(2,1)S(1)}, u32[]{:S(2)}, u32[]{:S(2)}) collective-permute-start(bf16[224,128]{1,0:T(8,128)(2,1)S(1)} %shard_map.83.refs_0_), channel_id=1, source_target_pairs={{0,16},{2,18},{4,20},{6,22},{8,24},{10,26},{12,28},{14,30},{16,0},... | collective-permute-start | bytes 172040 | tf_op jit(solution)/shard_map/ppermute | solution.py:191
  47.4 2.0 %collective-permute-start.20 = (bf16[224,128]{1,0:T(8,128)(2,1)S(1)}, bf16[224,128]{1,0:T(8,128)(2,1)S(1)}, u32[]{:S(2)}, u32[]{:S(2)}) collective-permute-start(bf16[224,128]{1,0:T(8,128)(2,1)S(1)} %shard_map.83.refs_0_), channel_id=1, source_target_pairs={{0,24},{2,26},{4,28},{6,30},{8,16},{10,18},{12,20},{14,22},{16,8},... | collective-permute-start | bytes 172040 | tf_op jit(solution)/shard_map/ppermute | solution.py:191
  49.4 0.8 %collective-permute-done.19.refs_2_ = bf16[224,128]{1,0:T(8,128)(2,1)S(1)} collective-permute-done((bf16[224,128]{1,0:T(8,128)(2,1)S(1)}, bf16[224,128]{1,0:T(8,128)(2,1)S(1)}, u32[]{:S(2)}, u32[]{:S(2)}) %collective-permute-start.19) | collective-permute-done | bytes 57376 | tf_op jit(solution)/shard_map/ppermute | solution.py:191
  50.2 2.1 %collective-permute-done.20.refs_3_ = bf16[224,128]{1,0:T(8,128)(2,1)S(1)} collective-permute-done((bf16[224,128]{1,0:T(8,128)(2,1)S(1)}, bf16[224,128]{1,0:T(8,128)(2,1)S(1)}, u32[]{:S(2)}, u32[]{:S(2)}) %collective-permute-start.20) | collective-permute-done | bytes 57376 | tf_op jit(solution)/shard_map/ppermute | solution.py:191
  52.3 4.8 %collective-permute-start.21 = (bf16[896,128]{1,0:T(8,128)(2,1)S(1)}, bf16[896,128]{1,0:T(8,128)(2,1)S(1)}, u32[]{:S(2)}, u32[]{:S(2)}) collective-permute-start(bf16[896,128]{1,0:T(8,128)(2,1)S(1)} %shard_map.84.own_ref), channel_id=1, source_target_pairs={{0,2},{2,0},{4,6},{6,4},{8,10},{10,8},{12,14},{14,12},{16,18},{18,... | collective-permute-start | bytes 688136 | tf_op jit(solution)/shard_map/ppermute | solution.py:191
  57.2 2.5 %collective-permute-start.12 = (bf16[64,1024]{1,0:T(8,128)(2,1)S(1)}, bf16[64,1024]{1,0:T(8,128)(2,1)S(1)}, u32[]{:S(2)}, u32[]{:S(2)}) collective-permute-start(bf16[64,1024]{1,0:T(8,128)(2,1)S(1)} %get-tuple-element.47), channel_id=1, source_target_pairs={{0,0},{30,30},{2,4},{6,8},{10,12},{14,16},{18,20},{22,24},{26,28},... | collective-permute-start | bytes 393224 | tf_op jit(solution)/shard_map/ppermute | solution.py:191
  59.7 3.8 %collective-permute-done.12.b_ref = bf16[64,1024]{1,0:T(8,128)(2,1)S(1)} collective-permute-done((bf16[64,1024]{1,0:T(8,128)(2,1)S(1)}, bf16[64,1024]{1,0:T(8,128)(2,1)S(1)}, u32[]{:S(2)}, u32[]{:S(2)}) %collective-permute-start.12) | collective-permute-done | bytes 131104 | tf_op jit(solution)/shard_map/ppermute | solution.py:191
  63.5 1.7 %shard_map.80 = (bf16[64,2,2,256]{3,2,1,0:T(2,128)(2,1)}, bf16[64,1,2,128]{3,2,1,0:T(2,128)(2,1)}) custom-call(bf16[2,64,1024]{2,1,0:T(8,128)(2,1)S(1)} %get-tuple-element.45.own_ref, bf16[64,1024]{1,0:T(8,128)(2,1)S(1)} %collective-permute-done.11.a_ref, bf16[64,1024]{1,0:T(8,128)(2,1)S(1)} %collective-permute-done.12.b_ref, ...), custom_call_target="tpu_custom_call" | custom-call | tf_op jit(solution)/shard_map/pallas_call | solution.py:34
  65.2 1.5 %shard_map.85 = (f32[27,64,64]{2,1,0:T(8,128)}, f32[27,64,64]{2,1,0:T(8,128)}) custom-call(bf16[896,128]{1,0:T(8,128)(2,1)S(1)} %shard_map.84.own_ref, bf16[896,128]{1,0:T(8,128)(2,1)S(1)} %collective-permute-done.21.got_ref), custom_call_target="tpu_custom_call" | custom-call | tf_op jit(solution)/shard_map/pallas_call | solution.py:34
  (23 shorter events, 1.6 us)
Async XLA Ops:
  2.1 6.0 %collective-permute-start = (bf16[64,1280]{1,0:T(8,128)(2,1)S(1)}, bf16[64,1280]{1,0:T(8,128)(2,1)S(1)}, u32[]{:S(2)}, u32[]{:S(2)}) collective-permute-start(bf16[64,1280]{1,0:T(8,128)(2,1)S(1)} %get-tuple-element.32.refs_0_), channel_id=1, source_target_pairs={{0,1},{1,0},{2,3},{3,2},{4,5},{5,4},{6,7},{7,6},{8,9},{9,8},{10,11... | collective-permute-start | bytes 491528 | tf_op jit(solution)/shard_map/ppermute | solution.py:195
  4.2 14.9 %collective-permute-start.1 = (bf16[64,1280]{1,0:T(8,128)(2,1)S(1)}, bf16[64,1280]{1,0:T(8,128)(2,1)S(1)}, u32[]{:S(2)}, u32[]{:S(2)}) collective-permute-start(bf16[64,1280]{1,0:T(8,128)(2,1)S(1)} %get-tuple-element.32.refs_0_), channel_id=1, source_target_pairs={{0,2},{2,0},{4,6},{6,4},{8,10},{10,8},{12,14},{14,12},{16,18},{18,... | collective-permute-start | bytes 491528 | tf_op jit(solution)/shard_map/ppermute | solution.py:191
  8.1 11.0 %collective-permute-start.2 = (bf16[64,1280]{1,0:T(8,128)(2,1)S(1)}, bf16[64,1280]{1,0:T(8,128)(2,1)S(1)}, u32[]{:S(2)}, u32[]{:S(2)}) collective-permute-start(bf16[64,1280]{1,0:T(8,128)(2,1)S(1)} %collective-permute-done.refs_1_), channel_id=1, source_target_pairs={{0,2},{2,0},{4,6},{6,4},{8,10},{10,8},{12,14},{14,12},{16,18},{18,... | collective-permute-start | bytes 491528 | tf_op jit(solution)/shard_map/ppermute | solution.py:191
  9.3 15.2 %collective-permute-start.10 = (bf16[14,64,128]{2,1,0:T(8,128)(2,1)S(1)}, bf16[14,64,128]{2,1,0:T(8,128)(2,1)S(1)}, u32[]{:S(2)}, u32[]{:S(2)}) collective-permute-start(bf16[14,64,128]{2,1,0:T(8,128)(2,1)S(1)} %get-tuple-element.38.refs_0_), channel_id=1, source_target_pairs={{0,1},{1,0},{2,3},{3,2},{4,5},{5,4},{6,7},{7,6},{8,9},{9,8},{10,11... | collective-permute-start | bytes 688136 | tf_op jit(solution)/shard_map/ppermute | solution.py:195
  10.8 6.2 %collective-permute-start.3 = (bf16[64,768]{1,0:T(8,128)(2,1)S(1)}, bf16[64,768]{1,0:T(8,128)(2,1)S(1)}, u32[]{:S(2)}, u32[]{:S(2)}) collective-permute-start(bf16[64,768]{1,0:T(8,128)(2,1)S(1)} %get-tuple-element.33), channel_id=1, source_target_pairs={{0,0},{1,1},{30,30},{31,31},{2,4},{3,5},{6,8},{7,9},{10,12},{11,13... | collective-permute-start | bytes 294920 | tf_op jit(solution)/shard_map/ppermute | solution.py:195
  14.1 5.0 %collective-permute-start.4 = (bf16[64,768]{1,0:T(8,128)(2,1)S(1)}, bf16[64,768]{1,0:T(8,128)(2,1)S(1)}, u32[]{:S(2)}, u32[]{:S(2)}) collective-permute-start(bf16[64,768]{1,0:T(8,128)(2,1)S(1)} %get-tuple-element.33), channel_id=1, source_target_pairs={{0,1},{1,0},{30,31},{31,30},{2,5},{3,4},{6,9},{7,8},{10,13},{11,12... | collective-permute-start | bytes 294920 | tf_op jit(solution)/shard_map/ppermute | solution.py:195
  19.8 3.5 %collective-permute-start.6 = (bf16[64,256]{1,0:T(8,128)(2,1)S(1)}, bf16[64,256]{1,0:T(8,128)(2,1)S(1)}, u32[]{:S(2)}, u32[]{:S(2)}) collective-permute-start(bf16[64,256]{1,0:T(8,128)(2,1)S(1)} %get-tuple-element.37.refs_6_), channel_id=1, source_target_pairs={{0,4},{2,6},{4,0},{6,2},{8,12},{10,14},{12,8},{14,10},{16,20},{18,... | collective-permute-start | bytes 98312 | tf_op jit(solution)/shard_map/ppermute | solution.py:191
  22.0 2.4 %collective-permute-start.7 = (bf16[64,256]{1,0:T(8,128)(2,1)S(1)}, bf16[64,256]{1,0:T(8,128)(2,1)S(1)}, u32[]{:S(2)}, u32[]{:S(2)}) collective-permute-start(bf16[64,256]{1,0:T(8,128)(2,1)S(1)} %get-tuple-element.37.refs_6_), channel_id=1, source_target_pairs={{4,8},{6,10},{12,16},{14,18},{20,24},{22,26},{8,4},{10,6},{16,12},... | collective-permute-start | bytes 98312 | tf_op jit(solution)/shard_map/ppermute | solution.py:191
  22.7 2.7 %collective-permute-start.5 = (bf16[64,256]{1,0:T(8,128)(2,1)S(1)}, bf16[64,256]{1,0:T(8,128)(2,1)S(1)}, u32[]{:S(2)}, u32[]{:S(2)}) collective-permute-start(bf16[64,256]{1,0:T(8,128)(2,1)S(1)} %get-tuple-element.37.refs_6_), channel_id=1, source_target_pairs={{0,2},{2,0},{4,6},{6,4},{8,10},{10,8},{12,14},{14,12},{16,18},{18,... | collective-permute-start | bytes 98312 | tf_op jit(solution)/shard_map/ppermute | solution.py:191
  23.4 2.1 %collective-permute-start.8 = (bf16[64,256]{1,0:T(8,128)(2,1)S(1)}, bf16[64,256]{1,0:T(8,128)(2,1)S(1)}, u32[]{:S(2)}, u32[]{:S(2)}) collective-permute-start(bf16[64,256]{1,0:T(8,128)(2,1)S(1)} %collective-permute-done.6.refs_8_), channel_id=1, source_target_pairs={{0,2},{2,0},{4,6},{6,4},{8,10},{10,8},{12,14},{14,12},{16,18},{18,... | collective-permute-start | bytes 98312 | tf_op jit(solution)/shard_map/ppermute | solution.py:191
  24.5 1.2 %collective-permute-start.9 = (bf16[64,256]{1,0:T(8,128)(2,1)S(1)}, bf16[64,256]{1,0:T(8,128)(2,1)S(1)}, u32[]{:S(2)}, u32[]{:S(2)}) collective-permute-start(bf16[64,256]{1,0:T(8,128)(2,1)S(1)} %collective-permute-done.7.refs_9_), channel_id=1, source_target_pairs={{0,2},{2,0},{4,6},{6,4},{8,10},{10,8},{12,14},{14,12},{16,18},{18,... | collective-permute-start | bytes 98312 | tf_op jit(solution)/shard_map/ppermute | solution.py:191
  28.4 1.6 %collective-permute-start.13 = (bf16[896,128]{1,0:T(8,128)(2,1)S(1)}, bf16[896,128]{1,0:T(8,128)(2,1)S(1)}, u32[]{:S(2)}, u32[]{:S(2)}) collective-permute-start(bf16[896,128]{1,0:T(8,128)(2,1)S(1)} %get-tuple-element.53), channel_id=1, source_target_pairs={{0,2},{2,0},{4,6},{6,4},{8,10},{10,8},{12,14},{14,12},{16,18},{18,... | collective-permute-start | bytes 688136 | tf_op jit(solution)/shard_map/ppermute | solution.py:191
  30.0 7.7 %collective-permute-start.14 = (bf16[224,128]{1,0:T(8,128)(2,1)S(1)}, bf16[224,128]{1,0:T(8,128)(2,1)S(1)}, u32[]{:S(2)}, u32[]{:S(2)}) collective-permute-start(bf16[224,128]{1,0:T(8,128)(2,1)S(1)} %get-tuple-element.55), channel_id=1, source_target_pairs={{0,8},{2,10},{4,12},{6,14},{8,0},{10,2},{12,4},{14,6},{16,24},{18,... | collective-permute-start | bytes 172040 | tf_op jit(solution)/shard_map/ppermute | solution.py:191
  35.3 4.7 %collective-permute-start.15 = (bf16[224,128]{1,0:T(8,128)(2,1)S(1)}, bf16[224,128]{1,0:T(8,128)(2,1)S(1)}, u32[]{:S(2)}, u32[]{:S(2)}) collective-permute-start(bf16[224,128]{1,0:T(8,128)(2,1)S(1)} %get-tuple-element.56), channel_id=1, source_target_pairs={{0,16},{2,18},{4,20},{6,22},{8,24},{10,26},{12,28},{14,30},{16,0},... | collective-permute-start | bytes 172040 | tf_op jit(solution)/shard_map/ppermute | solution.py:191
  37.7 4.9 %collective-permute-start.16 = (bf16[224,128]{1,0:T(8,128)(2,1)S(1)}, bf16[224,128]{1,0:T(8,128)(2,1)S(1)}, u32[]{:S(2)}, u32[]{:S(2)}) collective-permute-start(bf16[224,128]{1,0:T(8,128)(2,1)S(1)} %get-tuple-element.57), channel_id=1, source_target_pairs={{0,24},{2,26},{4,28},{6,30},{8,16},{10,18},{12,20},{14,22},{16,8},... | collective-permute-start | bytes 172040 | tf_op jit(solution)/shard_map/ppermute | solution.py:191
  42.7 3.1 %collective-permute-start.17 = (bf16[224,128]{1,0:T(8,128)(2,1)S(1)}, bf16[224,128]{1,0:T(8,128)(2,1)S(1)}, u32[]{:S(2)}, u32[]{:S(2)}) collective-permute-start(bf16[224,128]{1,0:T(8,128)(2,1)S(1)} %shard_map.82.own_ref), channel_id=1, source_target_pairs={{0,4},{2,6},{4,0},{6,2},{8,12},{10,14},{12,8},{14,10},{16,20},{18,... | collective-permute-start | bytes 172040 | tf_op jit(solution)/shard_map/ppermute | solution.py:191
  45.8 3.6 %collective-permute-start.18 = (bf16[224,128]{1,0:T(8,128)(2,1)S(1)}, bf16[224,128]{1,0:T(8,128)(2,1)S(1)}, u32[]{:S(2)}, u32[]{:S(2)}) collective-permute-start(bf16[224,128]{1,0:T(8,128)(2,1)S(1)} %shard_map.83.refs_0_), channel_id=1, source_target_pairs={{0,8},{2,10},{4,12},{6,14},{8,0},{10,2},{12,4},{14,6},{16,24},{18,... | collective-permute-start | bytes 172040 | tf_op jit(solution)/shard_map/ppermute | solution.py:191
  46.3 3.9 %collective-permute-start.19 = (bf16[224,128]{1,0:T(8,128)(2,1)S(1)}, bf16[224,128]{1,0:T(8,128)(2,1)S(1)}, u32[]{:S(2)}, u32[]{:S(2)}) collective-permute-start(bf16[224,128]{1,0:T(8,128)(2,1)S(1)} %shard_map.83.refs_0_), channel_id=1, source_target_pairs={{0,16},{2,18},{4,20},{6,22},{8,24},{10,26},{12,28},{14,30},{16,0},... | collective-permute-start | bytes 172040 | tf_op jit(solution)/shard_map/ppermute | solution.py:191
  47.4 4.9 %collective-permute-start.20 = (bf16[224,128]{1,0:T(8,128)(2,1)S(1)}, bf16[224,128]{1,0:T(8,128)(2,1)S(1)}, u32[]{:S(2)}, u32[]{:S(2)}) collective-permute-start(bf16[224,128]{1,0:T(8,128)(2,1)S(1)} %shard_map.83.refs_0_), channel_id=1, source_target_pairs={{0,24},{2,26},{4,28},{6,30},{8,16},{10,18},{12,20},{14,22},{16,8},... | collective-permute-start | bytes 172040 | tf_op jit(solution)/shard_map/ppermute | solution.py:191
  52.3 12.9 %collective-permute-start.21 = (bf16[896,128]{1,0:T(8,128)(2,1)S(1)}, bf16[896,128]{1,0:T(8,128)(2,1)S(1)}, u32[]{:S(2)}, u32[]{:S(2)}) collective-permute-start(bf16[896,128]{1,0:T(8,128)(2,1)S(1)} %shard_map.84.own_ref), channel_id=1, source_target_pairs={{0,2},{2,0},{4,6},{6,4},{8,10},{10,8},{12,14},{14,12},{16,18},{18,... | collective-permute-start | bytes 688136 | tf_op jit(solution)/shard_map/ppermute | solution.py:191
  57.1 2.6 %collective-permute-start.11 = (bf16[64,1024]{1,0:T(8,128)(2,1)S(1)}, bf16[64,1024]{1,0:T(8,128)(2,1)S(1)}, u32[]{:S(2)}, u32[]{:S(2)}) collective-permute-start(bf16[64,1024]{1,0:T(8,128)(2,1)S(1)} %get-tuple-element.46), channel_id=1, source_target_pairs={{0,2},{2,0},{4,6},{6,4},{8,10},{10,8},{12,14},{14,12},{16,18},{18,... | collective-permute-start | bytes 393224 | tf_op jit(solution)/shard_map/ppermute | solution.py:191
  57.2 6.3 %collective-permute-start.12 = (bf16[64,1024]{1,0:T(8,128)(2,1)S(1)}, bf16[64,1024]{1,0:T(8,128)(2,1)S(1)}, u32[]{:S(2)}, u32[]{:S(2)}) collective-permute-start(bf16[64,1024]{1,0:T(8,128)(2,1)S(1)} %get-tuple-element.47), channel_id=1, source_target_pairs={{0,0},{30,30},{2,4},{6,8},{10,12},{14,16},{18,20},{22,24},{26,28},... | collective-permute-start | bytes 393224 | tf_op jit(solution)/shard_map/ppermute | solution.py:191

commit v5 on v4

--- a/solution.py
+++ b/solution.py
@@ -532,21 +532,40 @@
     group = call(join_kernel, shaped((half, 128), BF16))(*pieces)
     partner = along(group, mirror(1))
 
-    def final_kernel(own_ref, got_ref, first_ref, second_ref, rows_ref):
-        core = lax.axis_index("space") % 2
-        rows_ref[pl.ds(pl.multiple_of(core * half, 16), half), :] = own_ref[...].astype(F32)
-        rows_ref[pl.ds(pl.multiple_of((1 - core) * half, 16), half), :] = got_ref[...].astype(F32)
-        unpack(rows_ref, 0, first_rows, first_ref, fine_scale)
-        unpack(rows_ref, half, second_rows, second_ref, low_scale)
-
+    def spread_kernel(mirrored):
+        def body(*refs):
+            source, (first_out, second_out, first_ref, second_ref, rows_ref, sem) = refs[0], refs[-6:]
+            core = lax.axis_index("space") % 2
+            rows_ref[...] = source[...].astype(F32)
+
+            def write(rows, near, far, scale):
+                unpack(rows_ref, 0, rows, near, scale)
+                copy = pltpu.make_async_copy(near, far, sem)
+                copy.start()
+                copy.wait()
+
+            @pl.when(core == mirrored)
+            def _():
+                write(first_rows, first_ref, first_out, fine_scale)
+
+            @pl.when(core != mirrored)
+            def _():
+                write(second_rows, second_ref, second_out, low_scale)
+
+        return body
+
+    first_shape, second_shape = (27, channels, channels), (27, filters, channels)
+    results = (jax.ShapeDtypeStruct(first_shape, F32), jax.ShapeDtypeStruct(second_shape, F32))
+    scratch = (
+        pltpu.VMEM(first_shape, F32),
+        pltpu.VMEM(second_shape, F32),
+        pltpu.VMEM((half, 128), F32),
+        pltpu.SemaphoreType.DMA,
+    )
+    early = call(spread_kernel(0), results, scratch, out_far=True)(group)
     first_grad, second_grad = call(
-        final_kernel,
-        (
-            jax.ShapeDtypeStruct((27, channels, channels), F32),
-            jax.ShapeDtypeStruct((27, filters, channels), F32),
-        ),
-        (pltpu.VMEM((2 * half, 128), F32),),
-    )(group, partner)
+        spread_kernel(1), results, scratch, far=(1, 2), aliases={1: 0, 2: 1}, out_far=True
+    )(partner, *early)
     return (features, volume_grad, first_grad, second_grad)
 
 

time: 66.9 us -> 67.7 us (1.012)
  Pallas kernels: 9.84 us -> 10.6 us
    pallas_call x11 -> x12, Pallas kernels: 9.84 us -> 10.6 us  [run(): return kernel(*near)]
  transfers between devices with their start and end apart: 22 -> 22, of which waited for: 12 -> 12; matrix products, arithmetic and copies ran while one was open for 0% -> 0% of each run, Pallas kernels for 6% -> 8%
where the time goes in v5:
time: 67.7 us; the launch traced here: 67.5 us
  starting transfers between devices  32.3 us (48%)
  waiting for transfers between devices  23.8 us (35%)
  Pallas kernels  10.6 us (16%)
  between operations  0.78 us (1%)
    ppermute x18, starting transfers between devices, along(): return lax.ppermute(piece, 'space', table)  25.4 us
    ppermute x18, waiting for transfers between devices, along(): return lax.ppermute(piece, 'space', table)  16.7 us
    pallas_call x12, Pallas kernels, run(): return kernel(*near)  10.6 us
    ppermute x4, waiting for transfers between devices, across(): return lax.ppermute(piece, ('space', 'filt'), pairs)  7.11 us
    ppermute x4, starting transfers between devices, across(): return lax.ppermute(piece, ('space', 'filt'), pairs)  6.98 us
  transfers between devices with their start and end apart: 22, of which 12 were waited for; matrix products, arithmetic and copies ran while one was open for 0% of the time, Pallas kernels for 8%

profile of v5, /device:TPU:1, one launch (start us, length us, event | category | flops | bytes accessed | tf_op | source)
XLA Modules:
  0.0 67.5 jit_solution(1018887804814132787)
XLA Ops:
  0.6 1.4 %shard_map.75 = (bf16[64,1280]{1,0:T(8,128)(2,1)S(1)}, bf16[64,768]{1,0:T(8,128)(2,1)S(1)}, bf16[14,64,128]{2,1,0:T(8,128)(2,1)S(1)}, bf16[27,64,64]{2,1,0:T(8,128)(2,1)S(1)}) custom-call(bf16[64,2,2,256]{3,2,1,0:T(2,128)(2,1)} %refs_0_.1, bf16[64,1,2,128]{3,2,1,0:T(2,128)(2,1)} %refs_1_.1, bf16[27,64,64]{2,1,0:T(8,128)(2,1)} %refs_2_.1, ...), custom_call_target="tpu_custom_call" | custom-call | tf_op jit(solution)/shard_map/pallas_call | solution.py:34
  2.1 2.1 %collective-permute-start = (bf16[64,1280]{1,0:T(8,128)(2,1)S(1)}, bf16[64,1280]{1,0:T(8,128)(2,1)S(1)}, u32[]{:S(2)}, u32[]{:S(2)}) collective-permute-start(bf16[64,1280]{1,0:T(8,128)(2,1)S(1)} %get-tuple-element.34.refs_0_), channel_id=1, source_target_pairs={{0,1},{1,0},{2,3},{3,2},{4,5},{5,4},{6,7},{7,6},{8,9},{9,8},{10,11... | collective-permute-start | bytes 491528 | tf_op jit(solution)/shard_map/ppermute | solution.py:195
  4.2 1.0 %collective-permute-start.1 = (bf16[64,1280]{1,0:T(8,128)(2,1)S(1)}, bf16[64,1280]{1,0:T(8,128)(2,1)S(1)}, u32[]{:S(2)}, u32[]{:S(2)}) collective-permute-start(bf16[64,1280]{1,0:T(8,128)(2,1)S(1)} %get-tuple-element.34.refs_0_), channel_id=1, source_target_pairs={{0,2},{2,0},{4,6},{6,4},{8,10},{10,8},{12,14},{14,12},{16,18},{18,... | collective-permute-start | bytes 491528 | tf_op jit(solution)/shard_map/ppermute | solution.py:191
  5.1 2.9 %collective-permute-done.refs_1_ = bf16[64,1280]{1,0:T(8,128)(2,1)S(1)} collective-permute-done((bf16[64,1280]{1,0:T(8,128)(2,1)S(1)}, bf16[64,1280]{1,0:T(8,128)(2,1)S(1)}, u32[]{:S(2)}, u32[]{:S(2)}) %collective-permute-start) | collective-permute-done | bytes 163872 | tf_op jit(solution)/shard_map/ppermute | solution.py:195
  8.1 1.3 %collective-permute-start.2 = (bf16[64,1280]{1,0:T(8,128)(2,1)S(1)}, bf16[64,1280]{1,0:T(8,128)(2,1)S(1)}, u32[]{:S(2)}, u32[]{:S(2)}) collective-permute-start(bf16[64,1280]{1,0:T(8,128)(2,1)S(1)} %collective-permute-done.refs_1_), channel_id=1, source_target_pairs={{0,2},{2,0},{4,6},{6,4},{8,10},{10,8},{12,14},{14,12},{16,18},{18,... | collective-permute-start | bytes 491528 | tf_op jit(solution)/shard_map/ppermute | solution.py:191
  9.3 1.5 %collective-permute-start.10 = (bf16[14,64,128]{2,1,0:T(8,128)(2,1)S(1)}, bf16[14,64,128]{2,1,0:T(8,128)(2,1)S(1)}, u32[]{:S(2)}, u32[]{:S(2)}) collective-permute-start(bf16[14,64,128]{2,1,0:T(8,128)(2,1)S(1)} %get-tuple-element.40.refs_0_), channel_id=1, source_target_pairs={{0,1},{1,0},{2,3},{3,2},{4,5},{5,4},{6,7},{7,6},{8,9},{9,8},{10,11... | collective-permute-start | bytes 688136 | tf_op jit(solution)/shard_map/ppermute | solution.py:195
  10.8 3.3 %collective-permute-start.3 = (bf16[64,768]{1,0:T(8,128)(2,1)S(1)}, bf16[64,768]{1,0:T(8,128)(2,1)S(1)}, u32[]{:S(2)}, u32[]{:S(2)}) collective-permute-start(bf16[64,768]{1,0:T(8,128)(2,1)S(1)} %get-tuple-element.35), channel_id=1, source_target_pairs={{0,0},{1,1},{30,30},{31,31},{2,4},{3,5},{6,8},{7,9},{10,12},{11,13... | collective-permute-start | bytes 294920 | tf_op jit(solution)/shard_map/ppermute | solution.py:195
  14.2 0.7 %shard_map.76 = (bf16[2,64,1024]{2,1,0:T(8,128)(2,1)S(1)}, f32[2,64,1024]{2,1,0:T(8,128)S(1)}, bf16[576,192]{1,0:T(8,128)(2,1)S(1)}) custom-call(bf16[64,1280]{1,0:T(8,128)(2,1)S(1)} %get-tuple-element.34.refs_0_, bf16[64,1280]{1,0:T(8,128)(2,1)S(1)} %collective-permute-done.refs_1_, bf16[27,64,64]{2,1,0:T(8,128)(2,1)S(1)} %get-tuple-element.36.refs_2_), custom_call_target="tpu_custom_call" | custom-call | tf_op jit(solution)/shard_map/pallas_call | solution.py:34
  14.9 2.1 %collective-permute-done.3.refs_2_.refs_4_ = bf16[64,768]{1,0:T(8,128)(2,1)S(1)} collective-permute-done((bf16[64,768]{1,0:T(8,128)(2,1)S(1)}, bf16[64,768]{1,0:T(8,128)(2,1)S(1)}, u32[]{:S(2)}, u32[]{:S(2)}) %collective-permute-start.3) | collective-permute-done | bytes 98336 | tf_op jit(solution)/shard_map/ppermute | solution.py:195
  17.0 2.1 %collective-permute-done.4.refs_3_.refs_5_ = bf16[64,768]{1,0:T(8,128)(2,1)S(1)} collective-permute-done((bf16[64,768]{1,0:T(8,128)(2,1)S(1)}, bf16[64,768]{1,0:T(8,128)(2,1)S(1)}, u32[]{:S(2)}, u32[]{:S(2)}) %collective-permute-start.4) | collective-permute-done | bytes 98336 | tf_op jit(solution)/shard_map/ppermute | solution.py:195
  19.1 0.7 %shard_map.77 = (bf16[64,256]{1,0:T(8,128)(2,1)S(1)}, f32[2,64,1024]{2,1,0:T(8,128)S(1)}, bf16[2,64,1024]{2,1,0:T(8,128)(2,1)S(1)}) custom-call(bf16[64,1280]{1,0:T(8,128)(2,1)S(1)} %collective-permute-done.1.refs_0_.refs_2_, bf16[64,1280]{1,0:T(8,128)(2,1)S(1)} %collective-permute-done.2.refs_1_.refs_3_, ...), custom_call_target="tpu_custom_call" | custom-call | tf_op jit(solution)/shard_map/pallas_call | solution.py:34
  19.8 2.2 %collective-permute-start.6 = (bf16[64,256]{1,0:T(8,128)(2,1)S(1)}, bf16[64,256]{1,0:T(8,128)(2,1)S(1)}, u32[]{:S(2)}, u32[]{:S(2)}) collective-permute-start(bf16[64,256]{1,0:T(8,128)(2,1)S(1)} %get-tuple-element.39.refs_6_), channel_id=1, source_target_pairs={{0,4},{2,6},{4,0},{6,2},{8,12},{10,14},{12,8},{14,10},{16,20},{18,... | collective-permute-start | bytes 98312 | tf_op jit(solution)/shard_map/ppermute | solution.py:191
  22.0 0.7 collective-permute-start.7
  23.4 1.1 %collective-permute-start.8 = (bf16[64,256]{1,0:T(8,128)(2,1)S(1)}, bf16[64,256]{1,0:T(8,128)(2,1)S(1)}, u32[]{:S(2)}, u32[]{:S(2)}) collective-permute-start(bf16[64,256]{1,0:T(8,128)(2,1)S(1)} %collective-permute-done.6.refs_8_), channel_id=1, source_target_pairs={{0,2},{2,0},{4,6},{6,4},{8,10},{10,8},{12,14},{14,12},{16,18},{18,... | collective-permute-start | bytes 98312 | tf_op jit(solution)/shard_map/ppermute | solution.py:191
  24.5 0.9 %shard_map.78 = (bf16[2,576,192]{2,1,0:T(8,128)(2,1)S(1)}, bf16[2,576,192]{2,1,0:T(8,128)(2,1)S(1)}, bf16[576,192]{1,0:T(8,128)(2,1)S(1)}, bf16[4,192,1024]{2,1,0:T(8,128)(2,1)S(1)}) custom-call(bf16[14,64,128]{2,1,0:T(8,128)(2,1)S(1)} %get-tuple-element.40.refs_0_, bf16[14,64,128]{2,1,0:T(8,128)(2,1)S(1)} %collective-permute-done.10.refs_1_, ...), custom_call_target="tpu_custom_call" | custom-call | tf_op jit(solution)/shard_map/pallas_call | solution.py:34
  25.7 2.7 %shard_map.79 = (bf16[64,256]{1,0:T(8,128)(2,1)S(1)}, bf16[2,64,1024]{2,1,0:T(8,128)(2,1)S(1)}, bf16[64,1024]{1,0:T(8,128)(2,1)S(1)}, bf16[64,1024]{1,0:T(8,128)...) custom-call(bf16[64,1280]{1,0:T(8,128)(2,1)S(1)} %get-tuple-element.34.refs_0_, ...), custom_call_target="tpu_custom_call" | custom-call | tf_op jit(solution)/shard_map/pallas_call | solution.py:34
  28.7 1.2 %collective-permute-done.13.got_ref = bf16[896,128]{1,0:T(8,128)(2,1)S(1)} collective-permute-done((bf16[896,128]{1,0:T(8,128)(2,1)S(1)}, bf16[896,128]{1,0:T(8,128)(2,1)S(1)}, u32[]{:S(2)}, u32[]{:S(2)}) %collective-permute-start.13) | collective-permute-done | bytes 229408 | tf_op jit(solution)/shard_map/ppermute | solution.py:191
  30.0 5.3 %collective-permute-start.14 = (bf16[224,128]{1,0:T(8,128)(2,1)S(1)}, bf16[224,128]{1,0:T(8,128)(2,1)S(1)}, u32[]{:S(2)}, u32[]{:S(2)}) collective-permute-start(bf16[224,128]{1,0:T(8,128)(2,1)S(1)} %get-tuple-element.57), channel_id=1, source_target_pairs={{0,8},{2,10},{4,12},{6,14},{8,0},{10,2},{12,4},{14,6},{16,24},{18,... | collective-permute-start | bytes 172040 | tf_op jit(solution)/shard_map/ppermute | solution.py:191
  35.3 2.5 %collective-permute-start.15 = (bf16[224,128]{1,0:T(8,128)(2,1)S(1)}, bf16[224,128]{1,0:T(8,128)(2,1)S(1)}, u32[]{:S(2)}, u32[]{:S(2)}) collective-permute-start(bf16[224,128]{1,0:T(8,128)(2,1)S(1)} %get-tuple-element.58), channel_id=1, source_target_pairs={{0,16},{2,18},{4,20},{6,22},{8,24},{10,26},{12,28},{14,30},{16,0},... | collective-permute-start | bytes 172040 | tf_op jit(solution)/shard_map/ppermute | solution.py:191
  37.7 2.3 %collective-permute-done.15.refs_1_ = bf16[224,128]{1,0:T(8,128)(2,1)S(1)} collective-permute-done((bf16[224,128]{1,0:T(8,128)(2,1)S(1)}, bf16[224,128]{1,0:T(8,128)(2,1)S(1)}, u32[]{:S(2)}, u32[]{:S(2)}) %collective-permute-start.15) | collective-permute-done | bytes 57376 | tf_op jit(solution)/shard_map/ppermute | solution.py:191
  40.0 2.6 %collective-permute-done.16.refs_2_ = bf16[224,128]{1,0:T(8,128)(2,1)S(1)} collective-permute-done((bf16[224,128]{1,0:T(8,128)(2,1)S(1)}, bf16[224,128]{1,0:T(8,128)(2,1)S(1)}, u32[]{:S(2)}, u32[]{:S(2)}) %collective-permute-start.16) | collective-permute-done | bytes 57376 | tf_op jit(solution)/shard_map/ppermute | solution.py:191
  42.8 3.0 %collective-permute-done.17.refs_0_ = bf16[224,128]{1,0:T(8,128)(2,1)S(1)} collective-permute-done((bf16[224,128]{1,0:T(8,128)(2,1)S(1)}, bf16[224,128]{1,0:T(8,128)(2,1)S(1)}, u32[]{:S(2)}, u32[]{:S(2)}) %collective-permute-start.17) | collective-permute-done | bytes 57376 | tf_op jit(solution)/shard_map/ppermute | solution.py:191
  46.3 1.2 %collective-permute-start.19 = (bf16[224,128]{1,0:T(8,128)(2,1)S(1)}, bf16[224,128]{1,0:T(8,128)(2,1)S(1)}, u32[]{:S(2)}, u32[]{:S(2)}) collective-permute-start(bf16[224,128]{1,0:T(8,128)(2,1)S(1)} %shard_map.83.refs_0_), channel_id=1, source_target_pairs={{0,16},{2,18},{4,20},{6,22},{8,24},{10,26},{12,28},{14,30},{16,0},... | collective-permute-start | bytes 172040 | tf_op jit(solution)/shard_map/ppermute | solution.py:191
  47.4 2.0 %collective-permute-start.20 = (bf16[224,128]{1,0:T(8,128)(2,1)S(1)}, bf16[224,128]{1,0:T(8,128)(2,1)S(1)}, u32[]{:S(2)}, u32[]{:S(2)}) collective-permute-start(bf16[224,128]{1,0:T(8,128)(2,1)S(1)} %shard_map.83.refs_0_), channel_id=1, source_target_pairs={{0,24},{2,26},{4,28},{6,30},{8,16},{10,18},{12,20},{14,22},{16,8},... | collective-permute-start | bytes 172040 | tf_op jit(solution)/shard_map/ppermute | solution.py:191
  49.4 0.8 %collective-permute-done.19.refs_2_ = bf16[224,128]{1,0:T(8,128)(2,1)S(1)} collective-permute-done((bf16[224,128]{1,0:T(8,128)(2,1)S(1)}, bf16[224,128]{1,0:T(8,128)(2,1)S(1)}, u32[]{:S(2)}, u32[]{:S(2)}) %collective-permute-start.19) | collective-permute-done | bytes 57376 | tf_op jit(solution)/shard_map/ppermute | solution.py:191
  50.2 2.1 %collective-permute-done.20.refs_3_ = bf16[224,128]{1,0:T(8,128)(2,1)S(1)} collective-permute-done((bf16[224,128]{1,0:T(8,128)(2,1)S(1)}, bf16[224,128]{1,0:T(8,128)(2,1)S(1)}, u32[]{:S(2)}, u32[]{:S(2)}) %collective-permute-start.20) | collective-permute-done | bytes 57376 | tf_op jit(solution)/shard_map/ppermute | solution.py:191
  52.3 4.8 %collective-permute-start.21 = (bf16[896,128]{1,0:T(8,128)(2,1)S(1)}, bf16[896,128]{1,0:T(8,128)(2,1)S(1)}, u32[]{:S(2)}, u32[]{:S(2)}) collective-permute-start(bf16[896,128]{1,0:T(8,128)(2,1)S(1)} %shard_map.84.refs_0_), channel_id=1, source_target_pairs={{0,2},{2,0},{4,6},{6,4},{8,10},{10,8},{12,14},{14,12},{16,18},{18,... | collective-permute-start | bytes 688136 | tf_op jit(solution)/shard_map/ppermute | solution.py:191
  57.2 2.5 %collective-permute-start.12 = (bf16[64,1024]{1,0:T(8,128)(2,1)S(1)}, bf16[64,1024]{1,0:T(8,128)(2,1)S(1)}, u32[]{:S(2)}, u32[]{:S(2)}) collective-permute-start(bf16[64,1024]{1,0:T(8,128)(2,1)S(1)} %get-tuple-element.49), channel_id=1, source_target_pairs={{0,0},{30,30},{2,4},{6,8},{10,12},{14,16},{18,20},{22,24},{26,28},... | collective-permute-start | bytes 393224 | tf_op jit(solution)/shard_map/ppermute | solution.py:191
  59.7 3.8 %collective-permute-done.12.b_ref = bf16[64,1024]{1,0:T(8,128)(2,1)S(1)} collective-permute-done((bf16[64,1024]{1,0:T(8,128)(2,1)S(1)}, bf16[64,1024]{1,0:T(8,128)(2,1)S(1)}, u32[]{:S(2)}, u32[]{:S(2)}) %collective-permute-start.12) | collective-permute-done | bytes 131104 | tf_op jit(solution)/shard_map/ppermute | solution.py:191
  63.5 1.7 %shard_map.80 = (bf16[64,2,2,256]{3,2,1,0:T(2,128)(2,1)}, bf16[64,1,2,128]{3,2,1,0:T(2,128)(2,1)}) custom-call(bf16[2,64,1024]{2,1,0:T(8,128)(2,1)S(1)} %get-tuple-element.47.own_ref, bf16[64,1024]{1,0:T(8,128)(2,1)S(1)} %collective-permute-done.11.a_ref, bf16[64,1024]{1,0:T(8,128)(2,1)S(1)} %collective-permute-done.12.b_ref, ...), custom_call_target="tpu_custom_call" | custom-call | tf_op jit(solution)/shard_map/pallas_call | solution.py:34
  65.2 1.1 %shard_map.85 = (f32[27,64,64]{2,1,0:T(8,128)}, f32[27,64,64]{2,1,0:T(8,128)}) custom-call(bf16[896,128]{1,0:T(8,128)(2,1)S(1)} %shard_map.84.refs_0_), custom_call_target="tpu_custom_call" | custom-call | tf_op jit(solution)/shard_map/pallas_call | solution.py:34
  66.3 1.1 %shard_map.86 = (f32[27,64,64]{2,1,0:T(8,128)}, f32[27,64,64]{2,1,0:T(8,128)}) custom-call(bf16[896,128]{1,0:T(8,128)(2,1)S(1)} %collective-permute-done.21.refs_0_, f32[27,64,64]{2,1,0:T(8,128)} %get-tuple-element.60.refs_1_, f32[27,64,64]{2,1,0:T(8,128)} %get-tuple-element.61.refs_2_), custom_call_target="tpu_custom_call", output_to_operand_aliasing={{0}: (1, {}), {1}: (2, {})} | custom-call | tf_op jit(solution)/shard_map/pallas_call | solution.py:34
  (24 shorter events, 2.1 us)
Async XLA Ops:
  2.1 6.0 %collective-permute-start = (bf16[64,1280]{1,0:T(8,128)(2,1)S(1)}, bf16[64,1280]{1,0:T(8,128)(2,1)S(1)}, u32[]{:S(2)}, u32[]{:S(2)}) collective-permute-start(bf16[64,1280]{1,0:T(8,128)(2,1)S(1)} %get-tuple-element.34.refs_0_), channel_id=1, source_target_pairs={{0,1},{1,0},{2,3},{3,2},{4,5},{5,4},{6,7},{7,6},{8,9},{9,8},{10,11... | collective-permute-start | bytes 491528 | tf_op jit(solution)/shard_map/ppermute | solution.py:195
  4.2 14.9 %collective-permute-start.1 = (bf16[64,1280]{1,0:T(8,128)(2,1)S(1)}, bf16[64,1280]{1,0:T(8,128)(2,1)S(1)}, u32[]{:S(2)}, u32[]{:S(2)}) collective-permute-start(bf16[64,1280]{1,0:T(8,128)(2,1)S(1)} %get-tuple-element.34.refs_0_), channel_id=1, source_target_pairs={{0,2},{2,0},{4,6},{6,4},{8,10},{10,8},{12,14},{14,12},{16,18},{18,... | collective-permute-start | bytes 491528 | tf_op jit(solution)/shard_map/ppermute | solution.py:191
  8.1 11.0 %collective-permute-start.2 = (bf16[64,1280]{1,0:T(8,128)(2,1)S(1)}, bf16[64,1280]{1,0:T(8,128)(2,1)S(1)}, u32[]{:S(2)}, u32[]{:S(2)}) collective-permute-start(bf16[64,1280]{1,0:T(8,128)(2,1)S(1)} %collective-permute-done.refs_1_), channel_id=1, source_target_pairs={{0,2},{2,0},{4,6},{6,4},{8,10},{10,8},{12,14},{14,12},{16,18},{18,... | collective-permute-start | bytes 491528 | tf_op jit(solution)/shard_map/ppermute | solution.py:191
  9.3 15.2 %collective-permute-start.10 = (bf16[14,64,128]{2,1,0:T(8,128)(2,1)S(1)}, bf16[14,64,128]{2,1,0:T(8,128)(2,1)S(1)}, u32[]{:S(2)}, u32[]{:S(2)}) collective-permute-start(bf16[14,64,128]{2,1,0:T(8,128)(2,1)S(1)} %get-tuple-element.40.refs_0_), channel_id=1, source_target_pairs={{0,1},{1,0},{2,3},{3,2},{4,5},{5,4},{6,7},{7,6},{8,9},{9,8},{10,11... | collective-permute-start | bytes 688136 | tf_op jit(solution)/shard_map/ppermute | solution.py:195
  10.8 6.2 %collective-permute-start.3 = (bf16[64,768]{1,0:T(8,128)(2,1)S(1)}, bf16[64,768]{1,0:T(8,128)(2,1)S(1)}, u32[]{:S(2)}, u32[]{:S(2)}) collective-permute-start(bf16[64,768]{1,0:T(8,128)(2,1)S(1)} %get-tuple-element.35), channel_id=1, source_target_pairs={{0,0},{1,1},{30,30},{31,31},{2,4},{3,5},{6,8},{7,9},{10,12},{11,13... | collective-permute-start | bytes 294920 | tf_op jit(solution)/shard_map/ppermute | solution.py:195
  14.1 5.0 %collective-permute-start.4 = (bf16[64,768]{1,0:T(8,128)(2,1)S(1)}, bf16[64,768]{1,0:T(8,128)(2,1)S(1)}, u32[]{:S(2)}, u32[]{:S(2)}) collective-permute-start(bf16[64,768]{1,0:T(8,128)(2,1)S(1)} %get-tuple-element.35), channel_id=1, source_target_pairs={{0,1},{1,0},{30,31},{31,30},{2,5},{3,4},{6,9},{7,8},{10,13},{11,12... | collective-permute-start | bytes 294920 | tf_op jit(solution)/shard_map/ppermute | solution.py:195
  19.8 3.5 %collective-permute-start.6 = (bf16[64,256]{1,0:T(8,128)(2,1)S(1)}, bf16[64,256]{1,0:T(8,128)(2,1)S(1)}, u32[]{:S(2)}, u32[]{:S(2)}) collective-permute-start(bf16[64,256]{1,0:T(8,128)(2,1)S(1)} %get-tuple-element.39.refs_6_), channel_id=1, source_target_pairs={{0,4},{2,6},{4,0},{6,2},{8,12},{10,14},{12,8},{14,10},{16,20},{18,... | collective-permute-start | bytes 98312 | tf_op jit(solution)/shard_map/ppermute | solution.py:191
  22.0 2.4 %collective-permute-start.7 = (bf16[64,256]{1,0:T(8,128)(2,1)S(1)}, bf16[64,256]{1,0:T(8,128)(2,1)S(1)}, u32[]{:S(2)}, u32[]{:S(2)}) collective-permute-start(bf16[64,256]{1,0:T(8,128)(2,1)S(1)} %get-tuple-element.39.refs_6_), channel_id=1, source_target_pairs={{4,8},{6,10},{12,16},{14,18},{20,24},{22,26},{8,4},{10,6},{16,12},... | collective-permute-start | bytes 98312 | tf_op jit(solution)/shard_map/ppermute | solution.py:191
  22.7 2.7 %collective-permute-start.5 = (bf16[64,256]{1,0:T(8,128)(2,1)S(1)}, bf16[64,256]{1,0:T(8,128)(2,1)S(1)}, u32[]{:S(2)}, u32[]{:S(2)}) collective-permute-start(bf16[64,256]{1,0:T(8,128)(2,1)S(1)} %get-tuple-element.39.refs_6_), channel_id=1, source_target_pairs={{0,2},{2,0},{4,6},{6,4},{8,10},{10,8},{12,14},{14,12},{16,18},{18,... | collective-permute-start | bytes 98312 | tf_op jit(solution)/shard_map/ppermute | solution.py:191
  23.4 2.1 %collective-permute-start.8 = (bf16[64,256]{1,0:T(8,128)(2,1)S(1)}, bf16[64,256]{1,0:T(8,128)(2,1)S(1)}, u32[]{:S(2)}, u32[]{:S(2)}) collective-permute-start(bf16[64,256]{1,0:T(8,128)(2,1)S(1)} %collective-permute-done.6.refs_8_), channel_id=1, source_target_pairs={{0,2},{2,0},{4,6},{6,4},{8,10},{10,8},{12,14},{14,12},{16,18},{18,... | collective-permute-start | bytes 98312 | tf_op jit(solution)/shard_map/ppermute | solution.py:191
  24.5 1.2 %collective-permute-start.9 = (bf16[64,256]{1,0:T(8,128)(2,1)S(1)}, bf16[64,256]{1,0:T(8,128)(2,1)S(1)}, u32[]{:S(2)}, u32[]{:S(2)}) collective-permute-start(bf16[64,256]{1,0:T(8,128)(2,1)S(1)} %collective-permute-done.7.refs_9_), channel_id=1, source_target_pairs={{0,2},{2,0},{4,6},{6,4},{8,10},{10,8},{12,14},{14,12},{16,18},{18,... | collective-permute-start | bytes 98312 | tf_op jit(solution)/shard_map/ppermute | solution.py:191
  28.4 1.6 %collective-permute-start.13 = (bf16[896,128]{1,0:T(8,128)(2,1)S(1)}, bf16[896,128]{1,0:T(8,128)(2,1)S(1)}, u32[]{:S(2)}, u32[]{:S(2)}) collective-permute-start(bf16[896,128]{1,0:T(8,128)(2,1)S(1)} %get-tuple-element.55), channel_id=1, source_target_pairs={{0,2},{2,0},{4,6},{6,4},{8,10},{10,8},{12,14},{14,12},{16,18},{18,... | collective-permute-start | bytes 688136 | tf_op jit(solution)/shard_map/ppermute | solution.py:191
  30.0 7.7 %collective-permute-start.14 = (bf16[224,128]{1,0:T(8,128)(2,1)S(1)}, bf16[224,128]{1,0:T(8,128)(2,1)S(1)}, u32[]{:S(2)}, u32[]{:S(2)}) collective-permute-start(bf16[224,128]{1,0:T(8,128)(2,1)S(1)} %get-tuple-element.57), channel_id=1, source_target_pairs={{0,8},{2,10},{4,12},{6,14},{8,0},{10,2},{12,4},{14,6},{16,24},{18,... | collective-permute-start | bytes 172040 | tf_op jit(solution)/shard_map/ppermute | solution.py:191
  35.3 4.7 %collective-permute-start.15 = (bf16[224,128]{1,0:T(8,128)(2,1)S(1)}, bf16[224,128]{1,0:T(8,128)(2,1)S(1)}, u32[]{:S(2)}, u32[]{:S(2)}) collective-permute-start(bf16[224,128]{1,0:T(8,128)(2,1)S(1)} %get-tuple-element.58), channel_id=1, source_target_pairs={{0,16},{2,18},{4,20},{6,22},{8,24},{10,26},{12,28},{14,30},{16,0},... | collective-permute-start | bytes 172040 | tf_op jit(solution)/shard_map/ppermute | solution.py:191
  37.7 4.9 %collective-permute-start.16 = (bf16[224,128]{1,0:T(8,128)(2,1)S(1)}, bf16[224,128]{1,0:T(8,128)(2,1)S(1)}, u32[]{:S(2)}, u32[]{:S(2)}) collective-permute-start(bf16[224,128]{1,0:T(8,128)(2,1)S(1)} %get-tuple-element.59), channel_id=1, source_target_pairs={{0,24},{2,26},{4,28},{6,30},{8,16},{10,18},{12,20},{14,22},{16,8},... | collective-permute-start | bytes 172040 | tf_op jit(solution)/shard_map/ppermute | solution.py:191
  42.7 3.1 %collective-permute-start.17 = (bf16[224,128]{1,0:T(8,128)(2,1)S(1)}, bf16[224,128]{1,0:T(8,128)(2,1)S(1)}, u32[]{:S(2)}, u32[]{:S(2)}) collective-permute-start(bf16[224,128]{1,0:T(8,128)(2,1)S(1)} %shard_map.82.own_ref), channel_id=1, source_target_pairs={{0,4},{2,6},{4,0},{6,2},{8,12},{10,14},{12,8},{14,10},{16,20},{18,... | collective-permute-start | bytes 172040 | tf_op jit(solution)/shard_map/ppermute | solution.py:191
  45.8 3.6 %collective-permute-start.18 = (bf16[224,128]{1,0:T(8,128)(2,1)S(1)}, bf16[224,128]{1,0:T(8,128)(2,1)S(1)}, u32[]{:S(2)}, u32[]{:S(2)}) collective-permute-start(bf16[224,128]{1,0:T(8,128)(2,1)S(1)} %shard_map.83.refs_0_), channel_id=1, source_target_pairs={{0,8},{2,10},{4,12},{6,14},{8,0},{10,2},{12,4},{14,6},{16,24},{18,... | collective-permute-start | bytes 172040 | tf_op jit(solution)/shard_map/ppermute | solution.py:191
  46.3 3.9 %collective-permute-start.19 = (bf16[224,128]{1,0:T(8,128)(2,1)S(1)}, bf16[224,128]{1,0:T(8,128)(2,1)S(1)}, u32[]{:S(2)}, u32[]{:S(2)}) collective-permute-start(bf16[224,128]{1,0:T(8,128)(2,1)S(1)} %shard_map.83.refs_0_), channel_id=1, source_target_pairs={{0,16},{2,18},{4,20},{6,22},{8,24},{10,26},{12,28},{14,30},{16,0},... | collective-permute-start | bytes 172040 | tf_op jit(solution)/shard_map/ppermute | solution.py:191
  47.4 4.9 %collective-permute-start.20 = (bf16[224,128]{1,0:T(8,128)(2,1)S(1)}, bf16[224,128]{1,0:T(8,128)(2,1)S(1)}, u32[]{:S(2)}, u32[]{:S(2)}) collective-permute-start(bf16[224,128]{1,0:T(8,128)(2,1)S(1)} %shard_map.83.refs_0_), channel_id=1, source_target_pairs={{0,24},{2,26},{4,28},{6,30},{8,16},{10,18},{12,20},{14,22},{16,8},... | collective-permute-start | bytes 172040 | tf_op jit(solution)/shard_map/ppermute | solution.py:191
  52.3 14.0 %collective-permute-start.21 = (bf16[896,128]{1,0:T(8,128)(2,1)S(1)}, bf16[896,128]{1,0:T(8,128)(2,1)S(1)}, u32[]{:S(2)}, u32[]{:S(2)}) collective-permute-start(bf16[896,128]{1,0:T(8,128)(2,1)S(1)} %shard_map.84.refs_0_), channel_id=1, source_target_pairs={{0,2},{2,0},{4,6},{6,4},{8,10},{10,8},{12,14},{14,12},{16,18},{18,... | collective-permute-start | bytes 688136 | tf_op jit(solution)/shard_map/ppermute | solution.py:191
  57.1 2.6 %collective-permute-start.11 = (bf16[64,1024]{1,0:T(8,128)(2,1)S(1)}, bf16[64,1024]{1,0:T(8,128)(2,1)S(1)}, u32[]{:S(2)}, u32[]{:S(2)}) collective-permute-start(bf16[64,1024]{1,0:T(8,128)(2,1)S(1)} %get-tuple-element.48), channel_id=1, source_target_pairs={{0,2},{2,0},{4,6},{6,4},{8,10},{10,8},{12,14},{14,12},{16,18},{18,... | collective-permute-start | bytes 393224 | tf_op jit(solution)/shard_map/ppermute | solution.py:191
  57.2 6.3 %collective-permute-start.12 = (bf16[64,1024]{1,0:T(8,128)(2,1)S(1)}, bf16[64,1024]{1,0:T(8,128)(2,1)S(1)}, u32[]{:S(2)}, u32[]{:S(2)}) collective-permute-start(bf16[64,1024]{1,0:T(8,128)(2,1)S(1)} %get-tuple-element.49), channel_id=1, source_target_pairs={{0,0},{30,30},{2,4},{6,8},{10,12},{14,16},{18,20},{22,24},{26,28},... | collective-permute-start | bytes 393224 | tf_op jit(solution)/shard_map/ppermute | solution.py:191

commit v6 on v5

--- a/solution.py
+++ b/solution.py
@@ -255,28 +255,31 @@
 
     def own_kernel(*refs):
         own_refs, taps = refs[:filt], refs[filt]
-        whole_ref, sums_ref, matrices = refs[filt + 1 :]
+        fine_ref, sums_ref, matrices, whole_ref = refs[filt + 1 :]
         forward_matrix(taps, matrices, channels)
         for plane in range(planes):
             pieces = [ref[:, plane * brick : (plane + 1) * brick] for ref in own_refs]
             join_rows(whole_ref, plane, pieces, brick)
         stacks = {1 + plane: stack3(whole_ref[plane], depth) for plane in range(planes)}
+        for plane in range(planes):
+            fine_ref[plane] = stacks[1 + plane]
         sums = conv_planes(matrices, stacks, planes, channels, depth)
         for plane in range(planes):
             sums_ref[plane] = sums[plane]
 
-    whole, own_sums, first_forward = call(
+    own_stacks, own_sums, first_forward = call(
         own_kernel,
         (
-            shaped((planes, channels, fine_cells), BF16),
+            shaped((planes, 3 * channels, fine_cells), BF16),
             shaped((planes, channels, fine_cells), F32),
             shaped((9 * channels, 3 * channels), BF16),
         ),
+        (pltpu.VMEM((planes, channels, fine_cells), BF16),),
     )(*own, first_taps)
 
     def first_kernel(*refs):
         a_refs, b_refs = refs[:filt], refs[filt : 2 * filt]
-        sums_ref, matrices, pooled_ref, slope_ref, sides_ref = refs[2 * filt :]
+        sums_ref, matrices, pooled_ref, slope_ref, fine_ref, sides_ref = refs[2 * filt :]
         index = lax.axis_index("space")
         odd = index % 2 == 1
         inside = jnp.logical_and(index > 0, index < space - 1)
@@ -290,6 +293,8 @@
         join_rows(sides_ref, 0, lefts, brick)
         join_rows(sides_ref, 1, rights, brick)
         stacks = {0: stack3(sides_ref[0], depth), planes + 1: stack3(sides_ref[1], depth)}
+        fine_ref[0] = stacks[0]
+        fine_ref[1] = stacks[planes + 1]
         sums = [sums_ref[plane] for plane in range(planes)]
         pre = conv_planes(matrices, stacks, planes, channels, depth, sums)
         hidden = [silu(value).astype(BF16) for value in pre]
@@ -314,13 +319,14 @@
                 total = total + sums[piece * channels : (piece + 1) * channels]
             pooled_ref[:, row * low_depth : (row + 1) * low_depth] = (0.125 * total).astype(BF16)
 
-    pooled, slope, sides = call(
+    pooled, slope, side_stacks = call(
         first_kernel,
         (
             shaped((channels, low_cells), BF16),
             shaped((planes, channels, fine_cells), F32),
-            shaped((2, channels, fine_cells), BF16),
-        ),
+            shaped((2, 3 * channels, fine_cells), BF16),
+        ),
+        (pltpu.VMEM((2, channels, fine_cells), BF16),),
     )(*side_a, *side_b, own_sums, first_forward)
 
     pool_d = along(pooled, table_d)
@@ -330,27 +336,24 @@
     pool_ad = along(pool_d, mirror(1))
 
     def matrix_kernel(*refs):
-        narrow_refs, taps, whole_ref, sides_ref = refs[:filt], refs[filt], refs[filt + 1], refs[filt + 2]
-        forward_ref, back_ref, first_ref, fine_ref = refs[filt + 3 :]
-        for slot, ref in enumerate(narrow_refs):
+        forward_ref, back_ref = refs[filt:]
+        for slot, ref in enumerate(refs[:filt]):
             values = [ref[t, :, :64] if t < 14 else ref[t - 13, :, 64:] for t in range(27)]
             forward_matrix(values, forward_ref.at[slot], filters)
             back_ref[slot] = backward_matrix(values)
-        first_ref[...] = backward_matrix([taps[t] for t in range(27)])
-        fine_ref[0] = stack3(sides_ref[0], depth)
-        fine_ref[planes + 1] = stack3(sides_ref[1], depth)
-        for plane in range(planes):
-            fine_ref[1 + plane] = stack3(whole_ref[plane], depth)
-
-    second_forward, second_back, first_back, fine_stacks = call(
+
+    second_forward, second_back = call(
         matrix_kernel,
         (
             shaped((filt, 9 * filters, 3 * channels), BF16),
             shaped((filt, 9 * channels, 3 * filters), BF16),
-            shaped((9 * channels, 3 * channels), BF16),
-            shaped((planes + 2, 3 * channels, fine_cells), BF16),
-        ),
-    )(*narrows, first_taps, whole, sides)
+        ),
+    )(*narrows)
+
+    def back_kernel(taps, out_ref):
+        out_ref[...] = backward_matrix([taps[t] for t in range(27)])
+
+    first_back = call(back_kernel, shaped((9 * channels, 3 * channels), BF16))(first_taps)
 
     first_rows, second_rows = 9 * channels, 9 * filters
     packed_first, packed_second = first_rows * 3 // 2, second_rows * 3 // 2
@@ -358,15 +361,15 @@
     unit = 16 * far_side
     half = -(-max(packed_first, packed_second) // unit) * unit
     chunk = half // far_side
+    edge_blocks = fine_cells // 128
 
     def middle_kernel(*refs):
         own_refs, a_refs, b_refs = refs[:filt], refs[filt : 2 * filt], refs[2 * filt : 3 * filt]
         pool_ref, pa_ref, px_ref, pd_ref, pax_ref, pad_ref = refs[3 * filt : 3 * filt + 6]
-        forward_ref, back_ref, slope_ref, fine_ref = refs[3 * filt + 6 : 3 * filt + 10]
-        features_ref, down_ref, edge_a_ref, edge_b_ref, keep_ref, send_ref = refs[
-            3 * filt + 10 : 3 * filt + 16
+        forward_ref, back_ref, slope_ref, own_fine, side_fine = refs[
+            3 * filt + 6 : 3 * filt + 11
         ]
-        parts_ref = refs[3 * filt + 16]
+        features_ref, down_ref, edge_b_ref, keep_ref, send_ref, parts_ref = refs[3 * filt + 11 :]
         index = lax.axis_index("space")
         odd = index % 2 == 1
         up = (index // 2) % 2 == 1
@@ -424,23 +427,25 @@
         grads = [(hidden_grad * slope_ref[p]).astype(BF16) for p in range(planes)]
         for plane in range(planes):
             down_ref[plane] = grads[plane]
-        edge_a_ref[...] = pick(odd, grads[0], grads[planes - 1])
+        edge_a = pick(odd, grads[0], grads[planes - 1])
+        for block in range(edge_blocks):
+            start = half + block * channels
+            send_ref[start : start + channels, :] = edge_a[:, block * 128 : (block + 1) * 128]
         edge_b_ref[...] = pick(odd, grads[planes - 1], grads[0])
-        fine_stacks = [fine_ref[p] for p in range(planes + 2)]
+        fine_stacks = [side_fine[0]] + [own_fine[p] for p in range(planes)] + [side_fine[1]]
         first_sums = packed(weight_planes(grads, fine_stacks, depth), half)
         second_sums = packed(second_sums, half)
         keep_ref[...] = pick(odd, second_sums, first_sums)
-        send_ref[...] = pick(odd, first_sums, second_sums).astype(BF16)
-
-    flat_features, first_down, edge_a, edge_b, keep, send = call(
+        send_ref[:half, :] = pick(odd, first_sums, second_sums).astype(BF16)
+
+    flat_features, first_down, edge_b, keep, send = call(
         middle_kernel,
         (
             shaped((filters, low_cells), BF16),
             shaped((planes, channels, fine_cells), BF16),
             shaped((channels, fine_cells), BF16),
-            shaped((channels, fine_cells), BF16),
             shaped((half, 128), F32),
-            shaped((half, 128), BF16),
+            shaped((half + edge_blocks * channels, 128), BF16),
         ),
         (
             pltpu.VMEM((filt, channels, low_cells), BF16),
@@ -458,14 +463,15 @@
         second_forward,
         second_back,
         slope,
-        fine_stacks,
+        own_stacks,
+        side_stacks,
     )
 
-    got = along(send, mirror(1))
+    got_core = along(send, mirror(1))
 
     def split_kernel(keep_ref, got_ref, *refs):
         out_refs, rows_ref = refs[:-1], refs[-1]
-        rows_ref[...] = keep_ref[...] + got_ref[...].astype(F32)
+        rows_ref[...] = keep_ref[...] + got_ref[:half, :].astype(F32)
         high = lax.axis_index("space") // 4
         out_refs[0][...] = rows_ref[pl.ds(pl.multiple_of(high * chunk, 16), chunk), :]
         for k in range(1, far_side):
@@ -476,9 +482,9 @@
         split_kernel,
         (shaped((chunk, 128), F32),) + (shaped((chunk, 128), BF16),) * (far_side - 1),
         (pltpu.VMEM((half, 128), F32),),
-    )(keep, got)
+    )(keep, got_core)
     got = [along(sends[k - 1], mirror(4 * k)) for k in range(1, far_side)]
-    halo_a, halo_b = along(edge_a, mirror(1)), along(edge_b, table_b)
+    halo_a, halo_b = got_core, along(edge_b, table_b)
 
     def sum_kernel(own_ref, *refs):
         total = own_ref[...].astype(F32)
@@ -493,7 +499,14 @@
         index = lax.axis_index("space")
         odd = index % 2 == 1
         inside = jnp.logical_and(index > 0, index < space - 1)
-        got_a, got_b = a_ref[...], b_ref[...]
+        got_a = jnp.concatenate(
+            [
+                a_ref[half + k * channels : half + (k + 1) * channels, :]
+                for k in range(edge_blocks)
+            ],
+            axis=1,
+        )
+        got_b = b_ref[...]
         got_b = pick(inside, got_b, jnp.zeros_like(got_b))
         values = [pick(odd, got_a, got_b)] + [own_ref[p] for p in range(planes)]
         values.append(pick(odd, got_b, got_a))

time: 67.7 us -> 66.9 us (0.988)
  starting transfers between devices: 32.3 us -> 30.5 us
  waiting for transfers between devices: 23.8 us -> 24.8 us
    ppermute x18 -> x17, starting transfers between devices: 25.4 us -> 23.6 us  [along(): return lax.ppermute(piece, 'space', table)]
    ppermute x18 -> x17, waiting for transfers between devices: 16.7 us -> 17.3 us  [along(): return lax.ppermute(piece, 'space', table)]
    pallas_call x12 -> x13, Pallas kernels: 10.6 us -> 10.4 us  [run(): return kernel(*near)]
  transfers between devices with their start and end apart: 22 -> 21, of which waited for: 12 -> 12; matrix products, arithmetic and copies ran while one was open for 0% -> 0% of each run, Pallas kernels for 8% -> 7%
where the time goes in v6:
time: 66.9 us; the launch traced here: 66.4 us
  starting transfers between devices  30.5 us (46%)
  waiting for transfers between devices  24.8 us (37%)
  Pallas kernels  10.4 us (16%)
  between operations  0.77 us (1%)
    ppermute x17, starting transfers between devices, along(): return lax.ppermute(piece, 'space', table)  23.6 us
    ppermute x17, waiting for transfers between devices, along(): return lax.ppermute(piece, 'space', table)  17.3 us
    pallas_call x13, Pallas kernels, run(): return kernel(*near)  10.4 us
    ppermute x4, waiting for transfers between devices, across(): return lax.ppermute(piece, ('space', 'filt'), pairs)  7.5 us
    ppermute x4, starting transfers between devices, across(): return lax.ppermute(piece, ('space', 'filt'), pairs)  6.92 us
  transfers between devices with their start and end apart: 21, of which 12 were waited for; matrix products, arithmetic and copies ran while one was open for 0% of the time, Pallas kernels for 7%

profile of v6, /device:TPU:1, one launch (start us, length us, event | category | flops | bytes accessed | tf_op | source)
XLA Modules:
  0.0 66.4 jit_solution(4925059135287942110)
XLA Ops:
  0.6 1.4 %shard_map.75 = (bf16[64,1280]{1,0:T(8,128)(2,1)S(1)}, bf16[64,768]{1,0:T(8,128)(2,1)S(1)}, bf16[14,64,128]{2,1,0:T(8,128)(2,1)S(1)}, bf16[27,64,64]{2,1,0:T(8,128)(2,1)S(1)}) custom-call(bf16[64,2,2,256]{3,2,1,0:T(2,128)(2,1)} %refs_0_.1, bf16[64,1,2,128]{3,2,1,0:T(2,128)(2,1)} %refs_1_.1, bf16[27,64,64]{2,1,0:T(8,128)(2,1)} %refs_2_.1, ...), custom_call_target="tpu_custom_call" | custom-call | tf_op jit(solution)/shard_map/pallas_call | solution.py:34
  2.1 2.1 %collective-permute-start = (bf16[64,1280]{1,0:T(8,128)(2,1)S(1)}, bf16[64,1280]{1,0:T(8,128)(2,1)S(1)}, u32[]{:S(2)}, u32[]{:S(2)}) collective-permute-start(bf16[64,1280]{1,0:T(8,128)(2,1)S(1)} %get-tuple-element.31.refs_0_), channel_id=1, source_target_pairs={{0,1},{1,0},{2,3},{3,2},{4,5},{5,4},{6,7},{7,6},{8,9},{9,8},{10,11... | collective-permute-start | bytes 491528 | tf_op jit(solution)/shard_map/ppermute | solution.py:195
  4.2 1.0 %collective-permute-start.1 = (bf16[64,1280]{1,0:T(8,128)(2,1)S(1)}, bf16[64,1280]{1,0:T(8,128)(2,1)S(1)}, u32[]{:S(2)}, u32[]{:S(2)}) collective-permute-start(bf16[64,1280]{1,0:T(8,128)(2,1)S(1)} %get-tuple-element.31.refs_0_), channel_id=1, source_target_pairs={{0,2},{2,0},{4,6},{6,4},{8,10},{10,8},{12,14},{14,12},{16,18},{18,... | collective-permute-start | bytes 491528 | tf_op jit(solution)/shard_map/ppermute | solution.py:191
  5.1 2.9 %collective-permute-done.refs_1_ = bf16[64,1280]{1,0:T(8,128)(2,1)S(1)} collective-permute-done((bf16[64,1280]{1,0:T(8,128)(2,1)S(1)}, bf16[64,1280]{1,0:T(8,128)(2,1)S(1)}, u32[]{:S(2)}, u32[]{:S(2)}) %collective-permute-start) | collective-permute-done | bytes 163872 | tf_op jit(solution)/shard_map/ppermute | solution.py:195
  8.1 1.3 %collective-permute-start.2 = (bf16[64,1280]{1,0:T(8,128)(2,1)S(1)}, bf16[64,1280]{1,0:T(8,128)(2,1)S(1)}, u32[]{:S(2)}, u32[]{:S(2)}) collective-permute-start(bf16[64,1280]{1,0:T(8,128)(2,1)S(1)} %collective-permute-done.refs_1_), channel_id=1, source_target_pairs={{0,2},{2,0},{4,6},{6,4},{8,10},{10,8},{12,14},{14,12},{16,18},{18,... | collective-permute-start | bytes 491528 | tf_op jit(solution)/shard_map/ppermute | solution.py:191
  9.3 1.5 %collective-permute-start.10 = (bf16[14,64,128]{2,1,0:T(8,128)(2,1)S(1)}, bf16[14,64,128]{2,1,0:T(8,128)(2,1)S(1)}, u32[]{:S(2)}, u32[]{:S(2)}) collective-permute-start(bf16[14,64,128]{2,1,0:T(8,128)(2,1)S(1)} %get-tuple-element.37.refs_0_), channel_id=1, source_target_pairs={{0,1},{1,0},{2,3},{3,2},{4,5},{5,4},{6,7},{7,6},{8,9},{9,8},{10,11... | collective-permute-start | bytes 688136 | tf_op jit(solution)/shard_map/ppermute | solution.py:195
  10.8 1.4 %collective-permute-start.4 = (bf16[64,768]{1,0:T(8,128)(2,1)S(1)}, bf16[64,768]{1,0:T(8,128)(2,1)S(1)}, u32[]{:S(2)}, u32[]{:S(2)}) collective-permute-start(bf16[64,768]{1,0:T(8,128)(2,1)S(1)} %get-tuple-element.32), channel_id=1, source_target_pairs={{0,1},{1,0},{30,31},{31,30},{2,5},{3,4},{6,9},{7,8},{10,13},{11,12... | collective-permute-start | bytes 294920 | tf_op jit(solution)/shard_map/ppermute | solution.py:195
  12.2 2.0 %collective-permute-start.3 = (bf16[64,768]{1,0:T(8,128)(2,1)S(1)}, bf16[64,768]{1,0:T(8,128)(2,1)S(1)}, u32[]{:S(2)}, u32[]{:S(2)}) collective-permute-start(bf16[64,768]{1,0:T(8,128)(2,1)S(1)} %get-tuple-element.32), channel_id=1, source_target_pairs={{0,0},{1,1},{30,30},{31,31},{2,4},{3,5},{6,8},{7,9},{10,12},{11,13... | collective-permute-start | bytes 294920 | tf_op jit(solution)/shard_map/ppermute | solution.py:195
  14.2 0.7 %shard_map.76 = (bf16[2,192,1024]{2,1,0:T(8,128)(2,1)S(1)}, f32[2,64,1024]{2,1,0:T(8,128)S(1)}, bf16[576,192]{1,0:T(8,128)(2,1)S(1)}) custom-call(bf16[64,1280]{1,0:T(8,128)(2,1)S(1)} %get-tuple-element.31.refs_0_, bf16[64,1280]{1,0:T(8,128)(2,1)S(1)} %collective-permute-done.refs_1_, bf16[27,64,64]{2,1,0:T(8,128)(2,1)S(1)} %get-tuple-element.33.refs_2_.taps), custom_call_target="tpu_custom_call" | custom-call | tf_op jit(solution)/shard_map/pallas_call | solution.py:34
  14.9 4.1 %collective-permute-done.4.refs_3_.refs_5_ = bf16[64,768]{1,0:T(8,128)(2,1)S(1)} collective-permute-done((bf16[64,768]{1,0:T(8,128)(2,1)S(1)}, bf16[64,768]{1,0:T(8,128)(2,1)S(1)}, u32[]{:S(2)}, u32[]{:S(2)}) %collective-permute-start.4) | collective-permute-done | bytes 98336 | tf_op jit(solution)/shard_map/ppermute | solution.py:195
  19.4 0.7 %shard_map.77 = (bf16[64,256]{1,0:T(8,128)(2,1)S(1)}, f32[2,64,1024]{2,1,0:T(8,128)S(1)}, bf16[2,192,1024]{2,1,0:T(8,128)(2,1)S(1)}) custom-call(bf16[64,1280]{1,0:T(8,128)(2,1)S(1)} %collective-permute-done.1.refs_0_.refs_2_, bf16[64,1280]{1,0:T(8,128)(2,1)S(1)} %collective-permute-done.2.refs_1_.refs_3_, ...), custom_call_target="tpu_custom_call" | custom-call | tf_op jit(solution)/shard_map/pallas_call | solution.py:34
  20.2 0.7 collective-permute-start.7
  20.9 4.5 %collective-permute-start.6 = (bf16[64,256]{1,0:T(8,128)(2,1)S(1)}, bf16[64,256]{1,0:T(8,128)(2,1)S(1)}, u32[]{:S(2)}, u32[]{:S(2)}) collective-permute-start(bf16[64,256]{1,0:T(8,128)(2,1)S(1)} %get-tuple-element.36.refs_6_), channel_id=1, source_target_pairs={{0,4},{2,6},{4,0},{6,2},{8,12},{10,14},{12,8},{14,10},{16,20},{18,... | collective-permute-start | bytes 98312 | tf_op jit(solution)/shard_map/ppermute | solution.py:191
  25.9 0.8 %collective-permute-done.6.refs_8_ = bf16[64,256]{1,0:T(8,128)(2,1)S(1)} collective-permute-done((bf16[64,256]{1,0:T(8,128)(2,1)S(1)}, bf16[64,256]{1,0:T(8,128)(2,1)S(1)}, u32[]{:S(2)}, u32[]{:S(2)}) %collective-permute-start.6) | collective-permute-done | bytes 32800 | tf_op jit(solution)/shard_map/ppermute | solution.py:191
  27.3 0.6 collective-permute-done.8.refs_10_
  27.9 2.7 %shard_map.79 = (bf16[64,256]{1,0:T(8,128)(2,1)S(1)}, bf16[2,64,1024]{2,1,0:T(8,128)(2,1)S(1)}, bf16[64,1024]{1,0:T(8,128)(2,1)S(1)}, f32[896,128]{1,0:T(8,128)S(1)}, bf16[1408,128]{1,0:T(8,128)(2,1)S(1)}) custom-call(bf16[64,1280]{1,0:T(8,128)(2,1)S(1)} %get-tuple-element.31.refs_0_, bf16[64,1280]{1,0:T(8,128)(2,1)S(1)} %collective-permute-done.refs_1_, ...), custom_call_target="tpu_custom_call" | custom-call | tf_op jit(solution)/shard_map/pallas_call | solution.py:34
  30.8 1.5 %collective-permute-done.11.a_ref.got_ref = bf16[1408,128]{1,0:T(8,128)(2,1)S(1)} collective-permute-done((bf16[1408,128]{1,0:T(8,128)(2,1)S(1)}, bf16[1408,128]{1,0:T(8,128)(2,1)S(1)}, u32[]{:S(2)}, u32[]{:S(2)}) %collective-permute-start.11) | collective-permute-done | bytes 360480 | tf_op jit(solution)/shard_map/ppermute | solution.py:191
  32.4 2.7 %collective-permute-start.13 = (bf16[224,128]{1,0:T(8,128)(2,1)S(1)}, bf16[224,128]{1,0:T(8,128)(2,1)S(1)}, u32[]{:S(2)}, u32[]{:S(2)}) collective-permute-start(bf16[224,128]{1,0:T(8,128)(2,1)S(1)} %get-tuple-element.51), channel_id=1, source_target_pairs={{0,8},{2,10},{4,12},{6,14},{8,0},{10,2},{12,4},{14,6},{16,24},{18,... | collective-permute-start | bytes 172040 | tf_op jit(solution)/shard_map/ppermute | solution.py:191
  35.2 2.4 %collective-permute-start.14 = (bf16[224,128]{1,0:T(8,128)(2,1)S(1)}, bf16[224,128]{1,0:T(8,128)(2,1)S(1)}, u32[]{:S(2)}, u32[]{:S(2)}) collective-permute-start(bf16[224,128]{1,0:T(8,128)(2,1)S(1)} %get-tuple-element.52), channel_id=1, source_target_pairs={{0,16},{2,18},{4,20},{6,22},{8,24},{10,26},{12,28},{14,30},{16,0},... | collective-permute-start | bytes 172040 | tf_op jit(solution)/shard_map/ppermute | solution.py:191
  37.6 1.6 %collective-permute-done.14.refs_1_ = bf16[224,128]{1,0:T(8,128)(2,1)S(1)} collective-permute-done((bf16[224,128]{1,0:T(8,128)(2,1)S(1)}, bf16[224,128]{1,0:T(8,128)(2,1)S(1)}, u32[]{:S(2)}, u32[]{:S(2)}) %collective-permute-start.14) | collective-permute-done | bytes 57376 | tf_op jit(solution)/shard_map/ppermute | solution.py:191
  39.1 3.4 %collective-permute-done.15.refs_2_ = bf16[224,128]{1,0:T(8,128)(2,1)S(1)} collective-permute-done((bf16[224,128]{1,0:T(8,128)(2,1)S(1)}, bf16[224,128]{1,0:T(8,128)(2,1)S(1)}, u32[]{:S(2)}, u32[]{:S(2)}) %collective-permute-start.15) | collective-permute-done | bytes 57376 | tf_op jit(solution)/shard_map/ppermute | solution.py:191
  42.7 3.0 %collective-permute-done.16.refs_0_ = bf16[224,128]{1,0:T(8,128)(2,1)S(1)} collective-permute-done((bf16[224,128]{1,0:T(8,128)(2,1)S(1)}, bf16[224,128]{1,0:T(8,128)(2,1)S(1)}, u32[]{:S(2)}, u32[]{:S(2)}) %collective-permute-start.16) | collective-permute-done | bytes 57376 | tf_op jit(solution)/shard_map/ppermute | solution.py:191
  45.6 1.4 %collective-permute-start.19 = (bf16[224,128]{1,0:T(8,128)(2,1)S(1)}, bf16[224,128]{1,0:T(8,128)(2,1)S(1)}, u32[]{:S(2)}, u32[]{:S(2)}) collective-permute-start(bf16[224,128]{1,0:T(8,128)(2,1)S(1)} %shard_map.84.refs_0_), channel_id=1, source_target_pairs={{0,24},{2,26},{4,28},{6,30},{8,16},{10,18},{12,20},{14,22},{16,8},... | collective-permute-start | bytes 172040 | tf_op jit(solution)/shard_map/ppermute | solution.py:191
  47.6 1.6 %collective-permute-start.17 = (bf16[224,128]{1,0:T(8,128)(2,1)S(1)}, bf16[224,128]{1,0:T(8,128)(2,1)S(1)}, u32[]{:S(2)}, u32[]{:S(2)}) collective-permute-start(bf16[224,128]{1,0:T(8,128)(2,1)S(1)} %shard_map.84.refs_0_), channel_id=1, source_target_pairs={{0,8},{2,10},{4,12},{6,14},{8,0},{10,2},{12,4},{14,6},{16,24},{18,... | collective-permute-start | bytes 172040 | tf_op jit(solution)/shard_map/ppermute | solution.py:191
  49.2 1.3 %collective-permute-done.19.refs_3_ = bf16[224,128]{1,0:T(8,128)(2,1)S(1)} collective-permute-done((bf16[224,128]{1,0:T(8,128)(2,1)S(1)}, bf16[224,128]{1,0:T(8,128)(2,1)S(1)}, u32[]{:S(2)}, u32[]{:S(2)}) %collective-permute-start.19) | collective-permute-done | bytes 57376 | tf_op jit(solution)/shard_map/ppermute | solution.py:191
  50.6 1.6 %collective-permute-done.18.refs_2_ = bf16[224,128]{1,0:T(8,128)(2,1)S(1)} collective-permute-done((bf16[224,128]{1,0:T(8,128)(2,1)S(1)}, bf16[224,128]{1,0:T(8,128)(2,1)S(1)}, u32[]{:S(2)}, u32[]{:S(2)}) %collective-permute-start.18) | collective-permute-done | bytes 57376 | tf_op jit(solution)/shard_map/ppermute | solution.py:191
  52.2 3.9 %collective-permute-start.20 = (bf16[896,128]{1,0:T(8,128)(2,1)S(1)}, bf16[896,128]{1,0:T(8,128)(2,1)S(1)}, u32[]{:S(2)}, u32[]{:S(2)}) collective-permute-start(bf16[896,128]{1,0:T(8,128)(2,1)S(1)} %shard_map.85.refs_0_), channel_id=1, source_target_pairs={{0,2},{2,0},{4,6},{6,4},{8,10},{10,8},{12,14},{14,12},{16,18},{18,... | collective-permute-start | bytes 688136 | tf_op jit(solution)/shard_map/ppermute | solution.py:191
  56.1 2.5 %collective-permute-start.12 = (bf16[64,1024]{1,0:T(8,128)(2,1)S(1)}, bf16[64,1024]{1,0:T(8,128)(2,1)S(1)}, u32[]{:S(2)}, u32[]{:S(2)}) collective-permute-start(bf16[64,1024]{1,0:T(8,128)(2,1)S(1)} %get-tuple-element.45), channel_id=1, source_target_pairs={{0,0},{30,30},{2,4},{6,8},{10,12},{14,16},{18,20},{22,24},{26,28},... | collective-permute-start | bytes 393224 | tf_op jit(solution)/shard_map/ppermute | solution.py:191
  58.8 3.6 %collective-permute-done.12.b_ref = bf16[64,1024]{1,0:T(8,128)(2,1)S(1)} collective-permute-done((bf16[64,1024]{1,0:T(8,128)(2,1)S(1)}, bf16[64,1024]{1,0:T(8,128)(2,1)S(1)}, u32[]{:S(2)}, u32[]{:S(2)}) %collective-permute-start.12) | collective-permute-done | bytes 131104 | tf_op jit(solution)/shard_map/ppermute | solution.py:191
  62.4 1.7 %shard_map.81 = (bf16[64,2,2,256]{3,2,1,0:T(2,128)(2,1)}, bf16[64,1,2,128]{3,2,1,0:T(2,128)(2,1)}) custom-call(bf16[2,64,1024]{2,1,0:T(8,128)(2,1)S(1)} %get-tuple-element.43.own_ref, bf16[1408,128]{1,0:T(8,128)(2,1)S(1)} %collective-permute-done.11.a_ref.got_ref, bf16[64,1024]{1,0:T(8,128)(2,1)S(1)} %collective-permute-done.12.b_ref, ...), custom_call_target="tpu_custom_call" | custom-call | tf_op jit(solution)/shard_map/pallas_call | solution.py:34
  64.1 1.1 %shard_map.86 = (f32[27,64,64]{2,1,0:T(8,128)}, f32[27,64,64]{2,1,0:T(8,128)}) custom-call(bf16[896,128]{1,0:T(8,128)(2,1)S(1)} %shard_map.85.refs_0_), custom_call_target="tpu_custom_call" | custom-call | tf_op jit(solution)/shard_map/pallas_call | solution.py:34
  65.3 1.1 %shard_map.87 = (f32[27,64,64]{2,1,0:T(8,128)}, f32[27,64,64]{2,1,0:T(8,128)}) custom-call(bf16[896,128]{1,0:T(8,128)(2,1)S(1)} %collective-permute-done.20.refs_0_, f32[27,64,64]{2,1,0:T(8,128)} %get-tuple-element.54.refs_1_, f32[27,64,64]{2,1,0:T(8,128)} %get-tuple-element.55.refs_2_), custom_call_target="tpu_custom_call", output_to_operand_aliasing={{0}: (1, {}), {1}: (2, {})} | custom-call | tf_op jit(solution)/shard_map/pallas_call | solution.py:34
  (23 shorter events, 2.8 us)
Async XLA Ops:
  2.1 6.0 %collective-permute-start = (bf16[64,1280]{1,0:T(8,128)(2,1)S(1)}, bf16[64,1280]{1,0:T(8,128)(2,1)S(1)}, u32[]{:S(2)}, u32[]{:S(2)}) collective-permute-start(bf16[64,1280]{1,0:T(8,128)(2,1)S(1)} %get-tuple-element.31.refs_0_), channel_id=1, source_target_pairs={{0,1},{1,0},{2,3},{3,2},{4,5},{5,4},{6,7},{7,6},{8,9},{9,8},{10,11... | collective-permute-start | bytes 491528 | tf_op jit(solution)/shard_map/ppermute | solution.py:195
  4.2 15.3 %collective-permute-start.1 = (bf16[64,1280]{1,0:T(8,128)(2,1)S(1)}, bf16[64,1280]{1,0:T(8,128)(2,1)S(1)}, u32[]{:S(2)}, u32[]{:S(2)}) collective-permute-start(bf16[64,1280]{1,0:T(8,128)(2,1)S(1)} %get-tuple-element.31.refs_0_), channel_id=1, source_target_pairs={{0,2},{2,0},{4,6},{6,4},{8,10},{10,8},{12,14},{14,12},{16,18},{18,... | collective-permute-start | bytes 491528 | tf_op jit(solution)/shard_map/ppermute | solution.py:191
  8.1 11.4 %collective-permute-start.2 = (bf16[64,1280]{1,0:T(8,128)(2,1)S(1)}, bf16[64,1280]{1,0:T(8,128)(2,1)S(1)}, u32[]{:S(2)}, u32[]{:S(2)}) collective-permute-start(bf16[64,1280]{1,0:T(8,128)(2,1)S(1)} %collective-permute-done.refs_1_), channel_id=1, source_target_pairs={{0,2},{2,0},{4,6},{6,4},{8,10},{10,8},{12,14},{14,12},{16,18},{18,... | collective-permute-start | bytes 491528 | tf_op jit(solution)/shard_map/ppermute | solution.py:191
  9.3 17.5 %collective-permute-start.10 = (bf16[14,64,128]{2,1,0:T(8,128)(2,1)S(1)}, bf16[14,64,128]{2,1,0:T(8,128)(2,1)S(1)}, u32[]{:S(2)}, u32[]{:S(2)}) collective-permute-start(bf16[14,64,128]{2,1,0:T(8,128)(2,1)S(1)} %get-tuple-element.37.refs_0_), channel_id=1, source_target_pairs={{0,1},{1,0},{2,3},{3,2},{4,5},{5,4},{6,7},{7,6},{8,9},{9,8},{10,11... | collective-permute-start | bytes 688136 | tf_op jit(solution)/shard_map/ppermute | solution.py:195
  10.8 8.2 %collective-permute-start.4 = (bf16[64,768]{1,0:T(8,128)(2,1)S(1)}, bf16[64,768]{1,0:T(8,128)(2,1)S(1)}, u32[]{:S(2)}, u32[]{:S(2)}) collective-permute-start(bf16[64,768]{1,0:T(8,128)(2,1)S(1)} %get-tuple-element.32), channel_id=1, source_target_pairs={{0,1},{1,0},{30,31},{31,30},{2,5},{3,4},{6,9},{7,8},{10,13},{11,12... | collective-permute-start | bytes 294920 | tf_op jit(solution)/shard_map/ppermute | solution.py:195
  12.2 7.3 %collective-permute-start.3 = (bf16[64,768]{1,0:T(8,128)(2,1)S(1)}, bf16[64,768]{1,0:T(8,128)(2,1)S(1)}, u32[]{:S(2)}, u32[]{:S(2)}) collective-permute-start(bf16[64,768]{1,0:T(8,128)(2,1)S(1)} %get-tuple-element.32), channel_id=1, source_target_pairs={{0,0},{1,1},{30,30},{31,31},{2,4},{3,5},{6,8},{7,9},{10,12},{11,13... | collective-permute-start | bytes 294920 | tf_op jit(solution)/shard_map/ppermute | solution.py:195
  20.2 5.2 %collective-permute-start.7 = (bf16[64,256]{1,0:T(8,128)(2,1)S(1)}, bf16[64,256]{1,0:T(8,128)(2,1)S(1)}, u32[]{:S(2)}, u32[]{:S(2)}) collective-permute-start(bf16[64,256]{1,0:T(8,128)(2,1)S(1)} %get-tuple-element.36.refs_6_), channel_id=1, source_target_pairs={{4,8},{6,10},{12,16},{14,18},{20,24},{22,26},{8,4},{10,6},{16,12},... | collective-permute-start | bytes 98312 | tf_op jit(solution)/shard_map/ppermute | solution.py:191
  20.9 5.9 %collective-permute-start.6 = (bf16[64,256]{1,0:T(8,128)(2,1)S(1)}, bf16[64,256]{1,0:T(8,128)(2,1)S(1)}, u32[]{:S(2)}, u32[]{:S(2)}) collective-permute-start(bf16[64,256]{1,0:T(8,128)(2,1)S(1)} %get-tuple-element.36.refs_6_), channel_id=1, source_target_pairs={{0,4},{2,6},{4,0},{6,2},{8,12},{10,14},{12,8},{14,10},{16,20},{18,... | collective-permute-start | bytes 98312 | tf_op jit(solution)/shard_map/ppermute | solution.py:191
  25.4 1.9 %collective-permute-start.5 = (bf16[64,256]{1,0:T(8,128)(2,1)S(1)}, bf16[64,256]{1,0:T(8,128)(2,1)S(1)}, u32[]{:S(2)}, u32[]{:S(2)}) collective-permute-start(bf16[64,256]{1,0:T(8,128)(2,1)S(1)} %get-tuple-element.36.refs_6_), channel_id=1, source_target_pairs={{0,2},{2,0},{4,6},{6,4},{8,10},{10,8},{12,14},{14,12},{16,18},{18,... | collective-permute-start | bytes 98312 | tf_op jit(solution)/shard_map/ppermute | solution.py:191
  25.4 1.9 %collective-permute-start.9 = (bf16[64,256]{1,0:T(8,128)(2,1)S(1)}, bf16[64,256]{1,0:T(8,128)(2,1)S(1)}, u32[]{:S(2)}, u32[]{:S(2)}) collective-permute-start(bf16[64,256]{1,0:T(8,128)(2,1)S(1)} %collective-permute-done.7.refs_9_), channel_id=1, source_target_pairs={{0,2},{2,0},{4,6},{6,4},{8,10},{10,8},{12,14},{14,12},{16,18},{18,... | collective-permute-start | bytes 98312 | tf_op jit(solution)/shard_map/ppermute | solution.py:191
  26.7 1.2 %collective-permute-start.8 = (bf16[64,256]{1,0:T(8,128)(2,1)S(1)}, bf16[64,256]{1,0:T(8,128)(2,1)S(1)}, u32[]{:S(2)}, u32[]{:S(2)}) collective-permute-start(bf16[64,256]{1,0:T(8,128)(2,1)S(1)} %collective-permute-done.6.refs_8_), channel_id=1, source_target_pairs={{0,2},{2,0},{4,6},{6,4},{8,10},{10,8},{12,14},{14,12},{16,18},{18,... | collective-permute-start | bytes 98312 | tf_op jit(solution)/shard_map/ppermute | solution.py:191
  30.6 1.7 %collective-permute-start.11 = (bf16[1408,128]{1,0:T(8,128)(2,1)S(1)}, bf16[1408,128]{1,0:T(8,128)(2,1)S(1)}, u32[]{:S(2)}, u32[]{:S(2)}) collective-permute-start(bf16[1408,128]{1,0:T(8,128)(2,1)S(1)} %get-tuple-element.44), channel_id=1, source_target_pairs={{0,2},{2,0},{4,6},{6,4},{8,10},{10,8},{12,14},{14,12},{16,18},{18,... | collective-permute-start | bytes 1081352 | tf_op jit(solution)/shard_map/ppermute | solution.py:191
  32.4 5.1 %collective-permute-start.13 = (bf16[224,128]{1,0:T(8,128)(2,1)S(1)}, bf16[224,128]{1,0:T(8,128)(2,1)S(1)}, u32[]{:S(2)}, u32[]{:S(2)}) collective-permute-start(bf16[224,128]{1,0:T(8,128)(2,1)S(1)} %get-tuple-element.51), channel_id=1, source_target_pairs={{0,8},{2,10},{4,12},{6,14},{8,0},{10,2},{12,4},{14,6},{16,24},{18,... | collective-permute-start | bytes 172040 | tf_op jit(solution)/shard_map/ppermute | solution.py:191
  35.2 4.0 %collective-permute-start.14 = (bf16[224,128]{1,0:T(8,128)(2,1)S(1)}, bf16[224,128]{1,0:T(8,128)(2,1)S(1)}, u32[]{:S(2)}, u32[]{:S(2)}) collective-permute-start(bf16[224,128]{1,0:T(8,128)(2,1)S(1)} %get-tuple-element.52), channel_id=1, source_target_pairs={{0,16},{2,18},{4,20},{6,22},{8,24},{10,26},{12,28},{14,30},{16,0},... | collective-permute-start | bytes 172040 | tf_op jit(solution)/shard_map/ppermute | solution.py:191
  37.6 4.9 %collective-permute-start.15 = (bf16[224,128]{1,0:T(8,128)(2,1)S(1)}, bf16[224,128]{1,0:T(8,128)(2,1)S(1)}, u32[]{:S(2)}, u32[]{:S(2)}) collective-permute-start(bf16[224,128]{1,0:T(8,128)(2,1)S(1)} %get-tuple-element.53), channel_id=1, source_target_pairs={{0,24},{2,26},{4,28},{6,30},{8,16},{10,18},{12,20},{14,22},{16,8},... | collective-permute-start | bytes 172040 | tf_op jit(solution)/shard_map/ppermute | solution.py:191
  42.5 3.1 %collective-permute-start.16 = (bf16[224,128]{1,0:T(8,128)(2,1)S(1)}, bf16[224,128]{1,0:T(8,128)(2,1)S(1)}, u32[]{:S(2)}, u32[]{:S(2)}) collective-permute-start(bf16[224,128]{1,0:T(8,128)(2,1)S(1)} %shard_map.83.own_ref), channel_id=1, source_target_pairs={{0,4},{2,6},{4,0},{6,2},{8,12},{10,14},{12,8},{14,10},{16,20},{18,... | collective-permute-start | bytes 172040 | tf_op jit(solution)/shard_map/ppermute | solution.py:191
  45.6 4.9 %collective-permute-start.19 = (bf16[224,128]{1,0:T(8,128)(2,1)S(1)}, bf16[224,128]{1,0:T(8,128)(2,1)S(1)}, u32[]{:S(2)}, u32[]{:S(2)}) collective-permute-start(bf16[224,128]{1,0:T(8,128)(2,1)S(1)} %shard_map.84.refs_0_), channel_id=1, source_target_pairs={{0,24},{2,26},{4,28},{6,30},{8,16},{10,18},{12,20},{14,22},{16,8},... | collective-permute-start | bytes 172040 | tf_op jit(solution)/shard_map/ppermute | solution.py:191
  47.1 5.1 %collective-permute-start.18 = (bf16[224,128]{1,0:T(8,128)(2,1)S(1)}, bf16[224,128]{1,0:T(8,128)(2,1)S(1)}, u32[]{:S(2)}, u32[]{:S(2)}) collective-permute-start(bf16[224,128]{1,0:T(8,128)(2,1)S(1)} %shard_map.84.refs_0_), channel_id=1, source_target_pairs={{0,16},{2,18},{4,20},{6,22},{8,24},{10,26},{12,28},{14,30},{16,0},... | collective-permute-start | bytes 172040 | tf_op jit(solution)/shard_map/ppermute | solution.py:191
  47.6 4.6 %collective-permute-start.17 = (bf16[224,128]{1,0:T(8,128)(2,1)S(1)}, bf16[224,128]{1,0:T(8,128)(2,1)S(1)}, u32[]{:S(2)}, u32[]{:S(2)}) collective-permute-start(bf16[224,128]{1,0:T(8,128)(2,1)S(1)} %shard_map.84.refs_0_), channel_id=1, source_target_pairs={{0,8},{2,10},{4,12},{6,14},{8,0},{10,2},{12,4},{14,6},{16,24},{18,... | collective-permute-start | bytes 172040 | tf_op jit(solution)/shard_map/ppermute | solution.py:191
  52.2 13.0 %collective-permute-start.20 = (bf16[896,128]{1,0:T(8,128)(2,1)S(1)}, bf16[896,128]{1,0:T(8,128)(2,1)S(1)}, u32[]{:S(2)}, u32[]{:S(2)}) collective-permute-start(bf16[896,128]{1,0:T(8,128)(2,1)S(1)} %shard_map.85.refs_0_), channel_id=1, source_target_pairs={{0,2},{2,0},{4,6},{6,4},{8,10},{10,8},{12,14},{14,12},{16,18},{18,... | collective-permute-start | bytes 688136 | tf_op jit(solution)/shard_map/ppermute | solution.py:191
  56.1 6.3 %collective-permute-start.12 = (bf16[64,1024]{1,0:T(8,128)(2,1)S(1)}, bf16[64,1024]{1,0:T(8,128)(2,1)S(1)}, u32[]{:S(2)}, u32[]{:S(2)}) collective-permute-start(bf16[64,1024]{1,0:T(8,128)(2,1)S(1)} %get-tuple-element.45), channel_id=1, source_target_pairs={{0,0},{30,30},{2,4},{6,8},{10,12},{14,16},{18,20},{22,24},{26,28},... | collective-permute-start | bytes 393224 | tf_op jit(solution)/shard_map/ppermute | solution.py:191

commit v7 on v6

--- a/solution.py
+++ b/solution.py
@@ -119,18 +119,19 @@
     return jnp.concatenate(pieces, axis=0)
 
 
-def unpack(source, base, rows, out, scale):
+def unpack(source, rows, out, scale, pairs):
     half = rows // 2
     outputs = rows // 9
-    for pair in range(9):
-        main = source[base + pair * outputs : base + (pair + 1) * outputs, :].astype(F32) * scale
+    for pair in pairs:
+        begin = pair * outputs
+        main = source[begin : begin + outputs, :].astype(F32) * scale
         out[3 * pair] = main[:, :64]
         out[3 * pair + 1] = main[:, 64:]
-    for piece in range(0, 9 * outputs, 8):
-        row = piece if piece < half else piece - half
-        tail = source[base + rows + row : base + rows + row + 8, :].astype(F32) * scale
-        side = tail[:, :64] if piece < half else tail[:, 64:]
-        out[3 * (piece // outputs) + 2, piece % outputs : piece % outputs + 8, :] = side
+        for piece in range(begin, begin + outputs, 8):
+            row = rows + (piece if piece < half else piece - half)
+            tail = source[row : row + 8, :].astype(F32) * scale
+            side = tail[:, :64] if piece < half else tail[:, 64:]
+            out[3 * pair + 2, piece - begin : piece - begin + 8, :] = side
 
 
 def forward_matrix(taps, target, outputs):
@@ -394,19 +395,24 @@
                 [packed[k * filters : (k + 1) * filters] for k in range(blocks)], axis=1
             ).astype(F32)
 
-        for slot in range(filt):
-            pre = conv_planes(forward_ref.at[slot], stacks, 3, filters, low_depth)
+        pres = [
+            conv_planes(forward_ref.at[slot], stacks, 3, filters, low_depth)
+            for slot in range(filt)
+        ]
+        all_downs = []
+        for slot, pre in enumerate(pres):
             cot_own = cot_of(own_refs[slot][:, planes * brick :])
             cot_a = cot_of(a_refs[slot][:, planes * brick :])
             cot_b = cot_of(b_refs[slot][:, brick:])
             cot_b = pick(inside, cot_b, jnp.zeros_like(cot_b))
             cots = [pick(odd, cot_a, cot_b), cot_own, pick(odd, cot_b, cot_a)]
-            downs = [
-                (value * silu_slope(pre[plane])).astype(BF16) for plane, value in enumerate(cots)
-            ]
-            if slot == 0:
-                features_ref[...] = silu(pre[1]).astype(BF16)
-                second_sums = weight_planes([downs[1]], [stacks[1], stacks[2], stacks[3]], low_depth)
+            all_downs.append(
+                [(value * silu_slope(pre[plane])).astype(BF16) for plane, value in enumerate(cots)]
+            )
+        own_sides = [stacks[1], stacks[2], stacks[3]]
+        second_sums = weight_planes([all_downs[0][1]], own_sides, low_depth)
+        features_ref[...] = silu(pres[0][1]).astype(BF16)
+        for slot, downs in enumerate(all_downs):
             down_stacks = {k: stack3(value, low_depth) for k, value in enumerate(downs)}
             (part,) = conv_planes(back_ref.at[slot], down_stacks, 1, channels, low_depth)
             parts_ref[lax.axis_index("filt") ^ slot] = part.astype(BF16)
@@ -552,10 +558,16 @@
             rows_ref[...] = source[...].astype(F32)
 
             def write(rows, near, far, scale):
-                unpack(rows_ref, 0, rows, near, scale)
-                copy = pltpu.make_async_copy(near, far, sem)
-                copy.start()
-                copy.wait()
+                copies = []
+                for step in range(3):
+                    unpack(rows_ref, rows, near, scale, range(3 * step, 3 * step + 3))
+                    taps = pl.ds(9 * step, 9)
+                    copies.append(
+                        pltpu.make_async_copy(near.at[taps], far.at[taps], sem.at[step])
+                    )
+                    copies[-1].start()
+                for copy in copies:
+                    copy.wait()
 
             @pl.when(core == mirrored)
             def _():
@@ -573,7 +585,7 @@
         pltpu.VMEM(first_shape, F32),
         pltpu.VMEM(second_shape, F32),
         pltpu.VMEM((half, 128), F32),
-        pltpu.SemaphoreType.DMA,
+        pltpu.SemaphoreType.DMA((3,)),
     )
     early = call(spread_kernel(0), results, scratch, out_far=True)(group)
     first_grad, second_grad = call(

time: 66.9 us -> 66.5 us (level)
  no operation moved by 1% of the time
where the time goes in v7:
time: 66.5 us; the launch traced here: 65.9 us
  starting transfers between devices  30.4 us (46%)
  waiting for transfers between devices  24.9 us (37%)
  Pallas kernels  9.89 us (15%)
  between operations  0.78 us (1%)
    ppermute x17, starting transfers between devices, along(): return lax.ppermute(piece, 'space', table)  23.5 us
    ppermute x17, waiting for transfers between devices, along(): return lax.ppermute(piece, 'space', table)  17.4 us
    pallas_call x13, Pallas kernels, run(): return kernel(*near)  9.89 us
    ppermute x4, waiting for transfers between devices, across(): return lax.ppermute(piece, ('space', 'filt'), pairs)  7.5 us
    ppermute x4, starting transfers between devices, across(): return lax.ppermute(piece, ('space', 'filt'), pairs)  6.92 us
  transfers between devices with their start and end apart: 21, of which 12 were waited for; matrix products, arithmetic and copies ran while one was open for 0% of the time, Pallas kernels for 7%

profile of v7, /device:TPU:1, one launch (start us, length us, event | category | flops | bytes accessed | tf_op | source)
XLA Modules:
  0.0 65.9 jit_solution(12324400436329051987)
XLA Ops:
  0.6 1.4 %shard_map.75 = (bf16[64,1280]{1,0:T(8,128)(2,1)S(1)}, bf16[64,768]{1,0:T(8,128)(2,1)S(1)}, bf16[14,64,128]{2,1,0:T(8,128)(2,1)S(1)}, bf16[27,64,64]{2,1,0:T(8,128)(2,1)S(1)}) custom-call(bf16[64,2,2,256]{3,2,1,0:T(2,128)(2,1)} %refs_0_.1, bf16[64,1,2,128]{3,2,1,0:T(2,128)(2,1)} %refs_1_.1, bf16[27,64,64]{2,1,0:T(8,128)(2,1)} %refs_2_.1, ...), custom_call_target="tpu_custom_call" | custom-call | tf_op jit(solution)/shard_map/pallas_call | solution.py:34
  2.1 2.1 %collective-permute-start = (bf16[64,1280]{1,0:T(8,128)(2,1)S(1)}, bf16[64,1280]{1,0:T(8,128)(2,1)S(1)}, u32[]{:S(2)}, u32[]{:S(2)}) collective-permute-start(bf16[64,1280]{1,0:T(8,128)(2,1)S(1)} %get-tuple-element.31.refs_0_), channel_id=1, source_target_pairs={{0,1},{1,0},{2,3},{3,2},{4,5},{5,4},{6,7},{7,6},{8,9},{9,8},{10,11... | collective-permute-start | bytes 491528 | tf_op jit(solution)/shard_map/ppermute | solution.py:196
  4.2 1.0 %collective-permute-start.1 = (bf16[64,1280]{1,0:T(8,128)(2,1)S(1)}, bf16[64,1280]{1,0:T(8,128)(2,1)S(1)}, u32[]{:S(2)}, u32[]{:S(2)}) collective-permute-start(bf16[64,1280]{1,0:T(8,128)(2,1)S(1)} %get-tuple-element.31.refs_0_), channel_id=1, source_target_pairs={{0,2},{2,0},{4,6},{6,4},{8,10},{10,8},{12,14},{14,12},{16,18},{18,... | collective-permute-start | bytes 491528 | tf_op jit(solution)/shard_map/ppermute | solution.py:192
  5.1 2.9 %collective-permute-done.refs_1_ = bf16[64,1280]{1,0:T(8,128)(2,1)S(1)} collective-permute-done((bf16[64,1280]{1,0:T(8,128)(2,1)S(1)}, bf16[64,1280]{1,0:T(8,128)(2,1)S(1)}, u32[]{:S(2)}, u32[]{:S(2)}) %collective-permute-start) | collective-permute-done | bytes 163872 | tf_op jit(solution)/shard_map/ppermute | solution.py:196
  8.1 1.3 %collective-permute-start.2 = (bf16[64,1280]{1,0:T(8,128)(2,1)S(1)}, bf16[64,1280]{1,0:T(8,128)(2,1)S(1)}, u32[]{:S(2)}, u32[]{:S(2)}) collective-permute-start(bf16[64,1280]{1,0:T(8,128)(2,1)S(1)} %collective-permute-done.refs_1_), channel_id=1, source_target_pairs={{0,2},{2,0},{4,6},{6,4},{8,10},{10,8},{12,14},{14,12},{16,18},{18,... | collective-permute-start | bytes 491528 | tf_op jit(solution)/shard_map/ppermute | solution.py:192
  9.3 1.5 %collective-permute-start.10 = (bf16[14,64,128]{2,1,0:T(8,128)(2,1)S(1)}, bf16[14,64,128]{2,1,0:T(8,128)(2,1)S(1)}, u32[]{:S(2)}, u32[]{:S(2)}) collective-permute-start(bf16[14,64,128]{2,1,0:T(8,128)(2,1)S(1)} %get-tuple-element.37.refs_0_), channel_id=1, source_target_pairs={{0,1},{1,0},{2,3},{3,2},{4,5},{5,4},{6,7},{7,6},{8,9},{9,8},{10,11... | collective-permute-start | bytes 688136 | tf_op jit(solution)/shard_map/ppermute | solution.py:196
  10.8 1.4 %collective-permute-start.4 = (bf16[64,768]{1,0:T(8,128)(2,1)S(1)}, bf16[64,768]{1,0:T(8,128)(2,1)S(1)}, u32[]{:S(2)}, u32[]{:S(2)}) collective-permute-start(bf16[64,768]{1,0:T(8,128)(2,1)S(1)} %get-tuple-element.32), channel_id=1, source_target_pairs={{0,1},{1,0},{30,31},{31,30},{2,5},{3,4},{6,9},{7,8},{10,13},{11,12... | collective-permute-start | bytes 294920 | tf_op jit(solution)/shard_map/ppermute | solution.py:196
  12.2 2.0 %collective-permute-start.3 = (bf16[64,768]{1,0:T(8,128)(2,1)S(1)}, bf16[64,768]{1,0:T(8,128)(2,1)S(1)}, u32[]{:S(2)}, u32[]{:S(2)}) collective-permute-start(bf16[64,768]{1,0:T(8,128)(2,1)S(1)} %get-tuple-element.32), channel_id=1, source_target_pairs={{0,0},{1,1},{30,30},{31,31},{2,4},{3,5},{6,8},{7,9},{10,12},{11,13... | collective-permute-start | bytes 294920 | tf_op jit(solution)/shard_map/ppermute | solution.py:196
  14.2 0.7 %shard_map.76 = (bf16[2,192,1024]{2,1,0:T(8,128)(2,1)S(1)}, f32[2,64,1024]{2,1,0:T(8,128)S(1)}, bf16[576,192]{1,0:T(8,128)(2,1)S(1)}) custom-call(bf16[64,1280]{1,0:T(8,128)(2,1)S(1)} %get-tuple-element.31.refs_0_, bf16[64,1280]{1,0:T(8,128)(2,1)S(1)} %collective-permute-done.refs_1_, bf16[27,64,64]{2,1,0:T(8,128)(2,1)S(1)} %get-tuple-element.33.refs_2_.taps), custom_call_target="tpu_custom_call" | custom-call | tf_op jit(solution)/shard_map/pallas_call | solution.py:34
  14.9 4.1 %collective-permute-done.4.refs_3_.refs_5_ = bf16[64,768]{1,0:T(8,128)(2,1)S(1)} collective-permute-done((bf16[64,768]{1,0:T(8,128)(2,1)S(1)}, bf16[64,768]{1,0:T(8,128)(2,1)S(1)}, u32[]{:S(2)}, u32[]{:S(2)}) %collective-permute-start.4) | collective-permute-done | bytes 98336 | tf_op jit(solution)/shard_map/ppermute | solution.py:196
  19.4 0.7 %shard_map.77 = (bf16[64,256]{1,0:T(8,128)(2,1)S(1)}, f32[2,64,1024]{2,1,0:T(8,128)S(1)}, bf16[2,192,1024]{2,1,0:T(8,128)(2,1)S(1)}) custom-call(bf16[64,1280]{1,0:T(8,128)(2,1)S(1)} %collective-permute-done.1.refs_0_.refs_2_, bf16[64,1280]{1,0:T(8,128)(2,1)S(1)} %collective-permute-done.2.refs_1_.refs_3_, ...), custom_call_target="tpu_custom_call" | custom-call | tf_op jit(solution)/shard_map/pallas_call | solution.py:34
  20.2 0.7 %collective-permute-start.7 = (bf16[64,256]{1,0:T(8,128)(2,1)S(1)}, bf16[64,256]{1,0:T(8,128)(2,1)S(1)}, u32[]{:S(2)}, u32[]{:S(2)}) collective-permute-start(bf16[64,256]{1,0:T(8,128)(2,1)S(1)} %get-tuple-element.36.refs_6_), channel_id=1, source_target_pairs={{4,8},{6,10},{12,16},{14,18},{20,24},{22,26},{8,4},{10,6},{16,12},... | collective-permute-start | bytes 98312 | tf_op jit(solution)/shard_map/ppermute | solution.py:192
  20.9 4.5 %collective-permute-start.6 = (bf16[64,256]{1,0:T(8,128)(2,1)S(1)}, bf16[64,256]{1,0:T(8,128)(2,1)S(1)}, u32[]{:S(2)}, u32[]{:S(2)}) collective-permute-start(bf16[64,256]{1,0:T(8,128)(2,1)S(1)} %get-tuple-element.36.refs_6_), channel_id=1, source_target_pairs={{0,4},{2,6},{4,0},{6,2},{8,12},{10,14},{12,8},{14,10},{16,20},{18,... | collective-permute-start | bytes 98312 | tf_op jit(solution)/shard_map/ppermute | solution.py:192
  25.9 0.8 %collective-permute-done.6.refs_8_ = bf16[64,256]{1,0:T(8,128)(2,1)S(1)} collective-permute-done((bf16[64,256]{1,0:T(8,128)(2,1)S(1)}, bf16[64,256]{1,0:T(8,128)(2,1)S(1)}, u32[]{:S(2)}, u32[]{:S(2)}) %collective-permute-start.6) | collective-permute-done | bytes 32800 | tf_op jit(solution)/shard_map/ppermute | solution.py:192
  27.3 0.6 collective-permute-done.8.refs_10_
  27.9 2.4 %shard_map.79 = (bf16[64,256]{1,0:T(8,128)(2,1)S(1)}, bf16[2,64,1024]{2,1,0:T(8,128)(2,1)S(1)}, bf16[64,1024]{1,0:T(8,128)(2,1)S(1)}, f32[896,128]{1,0:T(8,128)S(1)}, bf16[1408,128]{1,0:T(8,128)(2,1)S(1)}) custom-call(bf16[64,1280]{1,0:T(8,128)(2,1)S(1)} %get-tuple-element.31.refs_0_, bf16[64,1280]{1,0:T(8,128)(2,1)S(1)} %collective-permute-done.refs_1_, ...), custom_call_target="tpu_custom_call" | custom-call | tf_op jit(solution)/shard_map/pallas_call | solution.py:34
  30.5 1.5 %collective-permute-done.11.a_ref.got_ref = bf16[1408,128]{1,0:T(8,128)(2,1)S(1)} collective-permute-done((bf16[1408,128]{1,0:T(8,128)(2,1)S(1)}, bf16[1408,128]{1,0:T(8,128)(2,1)S(1)}, u32[]{:S(2)}, u32[]{:S(2)}) %collective-permute-start.11) | collective-permute-done | bytes 360480 | tf_op jit(solution)/shard_map/ppermute | solution.py:192
  32.1 2.7 %collective-permute-start.13 = (bf16[224,128]{1,0:T(8,128)(2,1)S(1)}, bf16[224,128]{1,0:T(8,128)(2,1)S(1)}, u32[]{:S(2)}, u32[]{:S(2)}) collective-permute-start(bf16[224,128]{1,0:T(8,128)(2,1)S(1)} %get-tuple-element.51), channel_id=1, source_target_pairs={{0,8},{2,10},{4,12},{6,14},{8,0},{10,2},{12,4},{14,6},{16,24},{18,... | collective-permute-start | bytes 172040 | tf_op jit(solution)/shard_map/ppermute | solution.py:192
  34.9 2.4 %collective-permute-start.14 = (bf16[224,128]{1,0:T(8,128)(2,1)S(1)}, bf16[224,128]{1,0:T(8,128)(2,1)S(1)}, u32[]{:S(2)}, u32[]{:S(2)}) collective-permute-start(bf16[224,128]{1,0:T(8,128)(2,1)S(1)} %get-tuple-element.52), channel_id=1, source_target_pairs={{0,16},{2,18},{4,20},{6,22},{8,24},{10,26},{12,28},{14,30},{16,0},... | collective-permute-start | bytes 172040 | tf_op jit(solution)/shard_map/ppermute | solution.py:192
  37.3 1.6 %collective-permute-done.14.refs_1_ = bf16[224,128]{1,0:T(8,128)(2,1)S(1)} collective-permute-done((bf16[224,128]{1,0:T(8,128)(2,1)S(1)}, bf16[224,128]{1,0:T(8,128)(2,1)S(1)}, u32[]{:S(2)}, u32[]{:S(2)}) %collective-permute-start.14) | collective-permute-done | bytes 57376 | tf_op jit(solution)/shard_map/ppermute | solution.py:192
  38.8 3.4 %collective-permute-done.15.refs_2_ = bf16[224,128]{1,0:T(8,128)(2,1)S(1)} collective-permute-done((bf16[224,128]{1,0:T(8,128)(2,1)S(1)}, bf16[224,128]{1,0:T(8,128)(2,1)S(1)}, u32[]{:S(2)}, u32[]{:S(2)}) %collective-permute-start.15) | collective-permute-done | bytes 57376 | tf_op jit(solution)/shard_map/ppermute | solution.py:192
  42.3 3.0 %collective-permute-done.16.refs_0_ = bf16[224,128]{1,0:T(8,128)(2,1)S(1)} collective-permute-done((bf16[224,128]{1,0:T(8,128)(2,1)S(1)}, bf16[224,128]{1,0:T(8,128)(2,1)S(1)}, u32[]{:S(2)}, u32[]{:S(2)}) %collective-permute-start.16) | collective-permute-done | bytes 57376 | tf_op jit(solution)/shard_map/ppermute | solution.py:192
  45.3 1.4 %collective-permute-start.19 = (bf16[224,128]{1,0:T(8,128)(2,1)S(1)}, bf16[224,128]{1,0:T(8,128)(2,1)S(1)}, u32[]{:S(2)}, u32[]{:S(2)}) collective-permute-start(bf16[224,128]{1,0:T(8,128)(2,1)S(1)} %shard_map.84.refs_0_), channel_id=1, source_target_pairs={{0,24},{2,26},{4,28},{6,30},{8,16},{10,18},{12,20},{14,22},{16,8},... | collective-permute-start | bytes 172040 | tf_op jit(solution)/shard_map/ppermute | solution.py:192
  47.3 1.6 %collective-permute-start.17 = (bf16[224,128]{1,0:T(8,128)(2,1)S(1)}, bf16[224,128]{1,0:T(8,128)(2,1)S(1)}, u32[]{:S(2)}, u32[]{:S(2)}) collective-permute-start(bf16[224,128]{1,0:T(8,128)(2,1)S(1)} %shard_map.84.refs_0_), channel_id=1, source_target_pairs={{0,8},{2,10},{4,12},{6,14},{8,0},{10,2},{12,4},{14,6},{16,24},{18,... | collective-permute-start | bytes 172040 | tf_op jit(solution)/shard_map/ppermute | solution.py:192
  48.9 1.3 %collective-permute-done.19.refs_3_ = bf16[224,128]{1,0:T(8,128)(2,1)S(1)} collective-permute-done((bf16[224,128]{1,0:T(8,128)(2,1)S(1)}, bf16[224,128]{1,0:T(8,128)(2,1)S(1)}, u32[]{:S(2)}, u32[]{:S(2)}) %collective-permute-start.19) | collective-permute-done | bytes 57376 | tf_op jit(solution)/shard_map/ppermute | solution.py:192
  50.3 1.6 %collective-permute-done.18.refs_2_ = bf16[224,128]{1,0:T(8,128)(2,1)S(1)} collective-permute-done((bf16[224,128]{1,0:T(8,128)(2,1)S(1)}, bf16[224,128]{1,0:T(8,128)(2,1)S(1)}, u32[]{:S(2)}, u32[]{:S(2)}) %collective-permute-start.18) | collective-permute-done | bytes 57376 | tf_op jit(solution)/shard_map/ppermute | solution.py:192
  51.9 3.9 %collective-permute-start.20 = (bf16[896,128]{1,0:T(8,128)(2,1)S(1)}, bf16[896,128]{1,0:T(8,128)(2,1)S(1)}, u32[]{:S(2)}, u32[]{:S(2)}) collective-permute-start(bf16[896,128]{1,0:T(8,128)(2,1)S(1)} %shard_map.85.refs_0_), channel_id=1, source_target_pairs={{0,2},{2,0},{4,6},{6,4},{8,10},{10,8},{12,14},{14,12},{16,18},{18,... | collective-permute-start | bytes 688136 | tf_op jit(solution)/shard_map/ppermute | solution.py:192
  55.8 2.5 %collective-permute-start.12 = (bf16[64,1024]{1,0:T(8,128)(2,1)S(1)}, bf16[64,1024]{1,0:T(8,128)(2,1)S(1)}, u32[]{:S(2)}, u32[]{:S(2)}) collective-permute-start(bf16[64,1024]{1,0:T(8,128)(2,1)S(1)} %get-tuple-element.45), channel_id=1, source_target_pairs={{0,0},{30,30},{2,4},{6,8},{10,12},{14,16},{18,20},{22,24},{26,28},... | collective-permute-start | bytes 393224 | tf_op jit(solution)/shard_map/ppermute | solution.py:192
  58.5 3.6 %collective-permute-done.12.b_ref = bf16[64,1024]{1,0:T(8,128)(2,1)S(1)} collective-permute-done((bf16[64,1024]{1,0:T(8,128)(2,1)S(1)}, bf16[64,1024]{1,0:T(8,128)(2,1)S(1)}, u32[]{:S(2)}, u32[]{:S(2)}) %collective-permute-start.12) | collective-permute-done | bytes 131104 | tf_op jit(solution)/shard_map/ppermute | solution.py:192
  62.1 1.7 %shard_map.81 = (bf16[64,2,2,256]{3,2,1,0:T(2,128)(2,1)}, bf16[64,1,2,128]{3,2,1,0:T(2,128)(2,1)}) custom-call(bf16[2,64,1024]{2,1,0:T(8,128)(2,1)S(1)} %get-tuple-element.43.own_ref, bf16[1408,128]{1,0:T(8,128)(2,1)S(1)} %collective-permute-done.11.a_ref.got_ref, bf16[64,1024]{1,0:T(8,128)(2,1)S(1)} %collective-permute-done.12.b_ref, ...), custom_call_target="tpu_custom_call" | custom-call | tf_op jit(solution)/shard_map/pallas_call | solution.py:34
  63.8 1.1 %shard_map.86 = (f32[27,64,64]{2,1,0:T(8,128)}, f32[27,64,64]{2,1,0:T(8,128)}) custom-call(bf16[896,128]{1,0:T(8,128)(2,1)S(1)} %shard_map.85.refs_0_), custom_call_target="tpu_custom_call" | custom-call | tf_op jit(solution)/shard_map/pallas_call | solution.py:34
  64.9 1.0 %shard_map.87 = (f32[27,64,64]{2,1,0:T(8,128)}, f32[27,64,64]{2,1,0:T(8,128)}) custom-call(bf16[896,128]{1,0:T(8,128)(2,1)S(1)} %collective-permute-done.20.refs_0_, f32[27,64,64]{2,1,0:T(8,128)} %get-tuple-element.54.refs_1_, f32[27,64,64]{2,1,0:T(8,128)} %get-tuple-element.55.refs_2_), custom_call_target="tpu_custom_call", output_to_operand_aliasing={{0}: (1, {}), {1}: (2, {})} | custom-call | tf_op jit(solution)/shard_map/pallas_call | solution.py:34
  (23 shorter events, 2.7 us)
Async XLA Ops:
  2.1 6.0 %collective-permute-start = (bf16[64,1280]{1,0:T(8,128)(2,1)S(1)}, bf16[64,1280]{1,0:T(8,128)(2,1)S(1)}, u32[]{:S(2)}, u32[]{:S(2)}) collective-permute-start(bf16[64,1280]{1,0:T(8,128)(2,1)S(1)} %get-tuple-element.31.refs_0_), channel_id=1, source_target_pairs={{0,1},{1,0},{2,3},{3,2},{4,5},{5,4},{6,7},{7,6},{8,9},{9,8},{10,11... | collective-permute-start | bytes 491528 | tf_op jit(solution)/shard_map/ppermute | solution.py:196
  4.2 15.3 %collective-permute-start.1 = (bf16[64,1280]{1,0:T(8,128)(2,1)S(1)}, bf16[64,1280]{1,0:T(8,128)(2,1)S(1)}, u32[]{:S(2)}, u32[]{:S(2)}) collective-permute-start(bf16[64,1280]{1,0:T(8,128)(2,1)S(1)} %get-tuple-element.31.refs_0_), channel_id=1, source_target_pairs={{0,2},{2,0},{4,6},{6,4},{8,10},{10,8},{12,14},{14,12},{16,18},{18,... | collective-permute-start | bytes 491528 | tf_op jit(solution)/shard_map/ppermute | solution.py:192
  8.1 11.4 %collective-permute-start.2 = (bf16[64,1280]{1,0:T(8,128)(2,1)S(1)}, bf16[64,1280]{1,0:T(8,128)(2,1)S(1)}, u32[]{:S(2)}, u32[]{:S(2)}) collective-permute-start(bf16[64,1280]{1,0:T(8,128)(2,1)S(1)} %collective-permute-done.refs_1_), channel_id=1, source_target_pairs={{0,2},{2,0},{4,6},{6,4},{8,10},{10,8},{12,14},{14,12},{16,18},{18,... | collective-permute-start | bytes 491528 | tf_op jit(solution)/shard_map/ppermute | solution.py:192
  9.3 17.5 %collective-permute-start.10 = (bf16[14,64,128]{2,1,0:T(8,128)(2,1)S(1)}, bf16[14,64,128]{2,1,0:T(8,128)(2,1)S(1)}, u32[]{:S(2)}, u32[]{:S(2)}) collective-permute-start(bf16[14,64,128]{2,1,0:T(8,128)(2,1)S(1)} %get-tuple-element.37.refs_0_), channel_id=1, source_target_pairs={{0,1},{1,0},{2,3},{3,2},{4,5},{5,4},{6,7},{7,6},{8,9},{9,8},{10,11... | collective-permute-start | bytes 688136 | tf_op jit(solution)/shard_map/ppermute | solution.py:196
  10.8 8.2 %collective-permute-start.4 = (bf16[64,768]{1,0:T(8,128)(2,1)S(1)}, bf16[64,768]{1,0:T(8,128)(2,1)S(1)}, u32[]{:S(2)}, u32[]{:S(2)}) collective-permute-start(bf16[64,768]{1,0:T(8,128)(2,1)S(1)} %get-tuple-element.32), channel_id=1, source_target_pairs={{0,1},{1,0},{30,31},{31,30},{2,5},{3,4},{6,9},{7,8},{10,13},{11,12... | collective-permute-start | bytes 294920 | tf_op jit(solution)/shard_map/ppermute | solution.py:196
  12.2 7.3 %collective-permute-start.3 = (bf16[64,768]{1,0:T(8,128)(2,1)S(1)}, bf16[64,768]{1,0:T(8,128)(2,1)S(1)}, u32[]{:S(2)}, u32[]{:S(2)}) collective-permute-start(bf16[64,768]{1,0:T(8,128)(2,1)S(1)} %get-tuple-element.32), channel_id=1, source_target_pairs={{0,0},{1,1},{30,30},{31,31},{2,4},{3,5},{6,8},{7,9},{10,12},{11,13... | collective-permute-start | bytes 294920 | tf_op jit(solution)/shard_map/ppermute | solution.py:196
  20.2 5.2 %collective-permute-start.7 = (bf16[64,256]{1,0:T(8,128)(2,1)S(1)}, bf16[64,256]{1,0:T(8,128)(2,1)S(1)}, u32[]{:S(2)}, u32[]{:S(2)}) collective-permute-start(bf16[64,256]{1,0:T(8,128)(2,1)S(1)} %get-tuple-element.36.refs_6_), channel_id=1, source_target_pairs={{4,8},{6,10},{12,16},{14,18},{20,24},{22,26},{8,4},{10,6},{16,12},... | collective-permute-start | bytes 98312 | tf_op jit(solution)/shard_map/ppermute | solution.py:192
  20.9 5.9 %collective-permute-start.6 = (bf16[64,256]{1,0:T(8,128)(2,1)S(1)}, bf16[64,256]{1,0:T(8,128)(2,1)S(1)}, u32[]{:S(2)}, u32[]{:S(2)}) collective-permute-start(bf16[64,256]{1,0:T(8,128)(2,1)S(1)} %get-tuple-element.36.refs_6_), channel_id=1, source_target_pairs={{0,4},{2,6},{4,0},{6,2},{8,12},{10,14},{12,8},{14,10},{16,20},{18,... | collective-permute-start | bytes 98312 | tf_op jit(solution)/shard_map/ppermute | solution.py:192
  25.4 1.9 %collective-permute-start.5 = (bf16[64,256]{1,0:T(8,128)(2,1)S(1)}, bf16[64,256]{1,0:T(8,128)(2,1)S(1)}, u32[]{:S(2)}, u32[]{:S(2)}) collective-permute-start(bf16[64,256]{1,0:T(8,128)(2,1)S(1)} %get-tuple-element.36.refs_6_), channel_id=1, source_target_pairs={{0,2},{2,0},{4,6},{6,4},{8,10},{10,8},{12,14},{14,12},{16,18},{18,... | collective-permute-start | bytes 98312 | tf_op jit(solution)/shard_map/ppermute | solution.py:192
  25.4 1.9 %collective-permute-start.9 = (bf16[64,256]{1,0:T(8,128)(2,1)S(1)}, bf16[64,256]{1,0:T(8,128)(2,1)S(1)}, u32[]{:S(2)}, u32[]{:S(2)}) collective-permute-start(bf16[64,256]{1,0:T(8,128)(2,1)S(1)} %collective-permute-done.7.refs_9_), channel_id=1, source_target_pairs={{0,2},{2,0},{4,6},{6,4},{8,10},{10,8},{12,14},{14,12},{16,18},{18,... | collective-permute-start | bytes 98312 | tf_op jit(solution)/shard_map/ppermute | solution.py:192
  26.7 1.2 %collective-permute-start.8 = (bf16[64,256]{1,0:T(8,128)(2,1)S(1)}, bf16[64,256]{1,0:T(8,128)(2,1)S(1)}, u32[]{:S(2)}, u32[]{:S(2)}) collective-permute-start(bf16[64,256]{1,0:T(8,128)(2,1)S(1)} %collective-permute-done.6.refs_8_), channel_id=1, source_target_pairs={{0,2},{2,0},{4,6},{6,4},{8,10},{10,8},{12,14},{14,12},{16,18},{18,... | collective-permute-start | bytes 98312 | tf_op jit(solution)/shard_map/ppermute | solution.py:192
  30.3 1.7 %collective-permute-start.11 = (bf16[1408,128]{1,0:T(8,128)(2,1)S(1)}, bf16[1408,128]{1,0:T(8,128)(2,1)S(1)}, u32[]{:S(2)}, u32[]{:S(2)}) collective-permute-start(bf16[1408,128]{1,0:T(8,128)(2,1)S(1)} %get-tuple-element.44), channel_id=1, source_target_pairs={{0,2},{2,0},{4,6},{6,4},{8,10},{10,8},{12,14},{14,12},{16,18},{18,... | collective-permute-start | bytes 1081352 | tf_op jit(solution)/shard_map/ppermute | solution.py:192
  32.1 5.1 %collective-permute-start.13 = (bf16[224,128]{1,0:T(8,128)(2,1)S(1)}, bf16[224,128]{1,0:T(8,128)(2,1)S(1)}, u32[]{:S(2)}, u32[]{:S(2)}) collective-permute-start(bf16[224,128]{1,0:T(8,128)(2,1)S(1)} %get-tuple-element.51), channel_id=1, source_target_pairs={{0,8},{2,10},{4,12},{6,14},{8,0},{10,2},{12,4},{14,6},{16,24},{18,... | collective-permute-start | bytes 172040 | tf_op jit(solution)/shard_map/ppermute | solution.py:192
  34.9 4.0 %collective-permute-start.14 = (bf16[224,128]{1,0:T(8,128)(2,1)S(1)}, bf16[224,128]{1,0:T(8,128)(2,1)S(1)}, u32[]{:S(2)}, u32[]{:S(2)}) collective-permute-start(bf16[224,128]{1,0:T(8,128)(2,1)S(1)} %get-tuple-element.52), channel_id=1, source_target_pairs={{0,16},{2,18},{4,20},{6,22},{8,24},{10,26},{12,28},{14,30},{16,0},... | collective-permute-start | bytes 172040 | tf_op jit(solution)/shard_map/ppermute | solution.py:192
  37.3 4.9 %collective-permute-start.15 = (bf16[224,128]{1,0:T(8,128)(2,1)S(1)}, bf16[224,128]{1,0:T(8,128)(2,1)S(1)}, u32[]{:S(2)}, u32[]{:S(2)}) collective-permute-start(bf16[224,128]{1,0:T(8,128)(2,1)S(1)} %get-tuple-element.53), channel_id=1, source_target_pairs={{0,24},{2,26},{4,28},{6,30},{8,16},{10,18},{12,20},{14,22},{16,8},... | collective-permute-start | bytes 172040 | tf_op jit(solution)/shard_map/ppermute | solution.py:192
  42.2 3.1 %collective-permute-start.16 = (bf16[224,128]{1,0:T(8,128)(2,1)S(1)}, bf16[224,128]{1,0:T(8,128)(2,1)S(1)}, u32[]{:S(2)}, u32[]{:S(2)}) collective-permute-start(bf16[224,128]{1,0:T(8,128)(2,1)S(1)} %shard_map.83.own_ref), channel_id=1, source_target_pairs={{0,4},{2,6},{4,0},{6,2},{8,12},{10,14},{12,8},{14,10},{16,20},{18,... | collective-permute-start | bytes 172040 | tf_op jit(solution)/shard_map/ppermute | solution.py:192
  45.3 4.9 %collective-permute-start.19 = (bf16[224,128]{1,0:T(8,128)(2,1)S(1)}, bf16[224,128]{1,0:T(8,128)(2,1)S(1)}, u32[]{:S(2)}, u32[]{:S(2)}) collective-permute-start(bf16[224,128]{1,0:T(8,128)(2,1)S(1)} %shard_map.84.refs_0_), channel_id=1, source_target_pairs={{0,24},{2,26},{4,28},{6,30},{8,16},{10,18},{12,20},{14,22},{16,8},... | collective-permute-start | bytes 172040 | tf_op jit(solution)/shard_map/ppermute | solution.py:192
  46.8 5.1 %collective-permute-start.18 = (bf16[224,128]{1,0:T(8,128)(2,1)S(1)}, bf16[224,128]{1,0:T(8,128)(2,1)S(1)}, u32[]{:S(2)}, u32[]{:S(2)}) collective-permute-start(bf16[224,128]{1,0:T(8,128)(2,1)S(1)} %shard_map.84.refs_0_), channel_id=1, source_target_pairs={{0,16},{2,18},{4,20},{6,22},{8,24},{10,26},{12,28},{14,30},{16,0},... | collective-permute-start | bytes 172040 | tf_op jit(solution)/shard_map/ppermute | solution.py:192
  47.3 4.6 %collective-permute-start.17 = (bf16[224,128]{1,0:T(8,128)(2,1)S(1)}, bf16[224,128]{1,0:T(8,128)(2,1)S(1)}, u32[]{:S(2)}, u32[]{:S(2)}) collective-permute-start(bf16[224,128]{1,0:T(8,128)(2,1)S(1)} %shard_map.84.refs_0_), channel_id=1, source_target_pairs={{0,8},{2,10},{4,12},{6,14},{8,0},{10,2},{12,4},{14,6},{16,24},{18,... | collective-permute-start | bytes 172040 | tf_op jit(solution)/shard_map/ppermute | solution.py:192
  51.9 13.0 %collective-permute-start.20 = (bf16[896,128]{1,0:T(8,128)(2,1)S(1)}, bf16[896,128]{1,0:T(8,128)(2,1)S(1)}, u32[]{:S(2)}, u32[]{:S(2)}) collective-permute-start(bf16[896,128]{1,0:T(8,128)(2,1)S(1)} %shard_map.85.refs_0_), channel_id=1, source_target_pairs={{0,2},{2,0},{4,6},{6,4},{8,10},{10,8},{12,14},{14,12},{16,18},{18,... | collective-permute-start | bytes 688136 | tf_op jit(solution)/shard_map/ppermute | solution.py:192
  55.8 6.3 %collective-permute-start.12 = (bf16[64,1024]{1,0:T(8,128)(2,1)S(1)}, bf16[64,1024]{1,0:T(8,128)(2,1)S(1)}, u32[]{:S(2)}, u32[]{:S(2)}) collective-permute-start(bf16[64,1024]{1,0:T(8,128)(2,1)S(1)} %get-tuple-element.45), channel_id=1, source_target_pairs={{0,0},{30,30},{2,4},{6,8},{10,12},{14,16},{18,20},{22,24},{26,28},... | collective-permute-start | bytes 393224 | tf_op jit(solution)/shard_map/ppermute | solution.py:192

commit v8 on v7

--- a/solution.py
+++ b/solution.py
@@ -197,22 +197,31 @@
 
 
     def message_kernel(*refs):
-        far_refs, own_ref, edge_ref, narrow_ref, first_ref = refs[:4], *refs[4:8]
-        cells_ref, cot_ref, second_ref, sems = refs[8:]
+        far_refs, own_ref, edge_ref, second_ref, first_ref = refs[:4], *refs[4:8]
+        cells_ref, cot_ref, sems = refs[8:]
         odd = lax.axis_index("space") % 2 == 1
-        copies = [
-            pltpu.make_async_copy(source, target, sems.at[k])
+        split = channels // 2
+        parts = [pl.ds(0, split), pl.ds(split, channels - split)]
+        loads = [
+            pltpu.make_async_copy(far_refs[0].at[part], cells_ref.at[part], sems.at[4 * k])
+            for k, part in enumerate(parts)
+        ]
+        for load in loads:
+            load.start()
+        copies = [None] + [
+            pltpu.make_async_copy(source, target, sems.at[1 + k])
             for k, (source, target) in enumerate(
-                zip(far_refs, (cells_ref, cot_ref, second_ref, first_ref))
+                zip(far_refs[1:], (cot_ref, second_ref, first_ref))
             )
         ]
-        for copy in copies:
+        for copy in copies[1:]:
             copy.start()
-        copies[0].wait()
-        for plane in range(planes):
-            for row in range(brick_y):
-                start = (plane * brick_y + row) * depth
-                own_ref[:, start : start + depth] = cells_ref[:, plane, row, :]
+        for load, part in zip(loads, parts):
+            load.wait()
+            for plane in range(planes):
+                for row in range(brick_y):
+                    start = (plane * brick_y + row) * depth
+                    own_ref[part, start : start + depth] = cells_ref[part, plane, row, :]
         copies[1].wait()
         width = low_y // blocks
         for row in range(low_y):
@@ -228,23 +237,20 @@
         edge_ref[:, brick:] = own_ref[:, planes * brick :]
 
         copies[2].wait()
-        for tap in range(14):
-            narrow_ref[tap] = jnp.concatenate([second_ref[tap], second_ref[tap + 13]], axis=1)
         copies[3].wait()
 
-    own_message, edge_message, narrow, first_taps = call(
+    own_message, edge_message, second_taps, first_taps = call(
         message_kernel,
         (
             shaped((channels, planes * brick + extra), BF16),
             shaped((channels, brick + extra), BF16),
-            shaped((14, filters, 128), BF16),
+            shaped(second_weight.shape, BF16),
             shaped(first_weight.shape, BF16),
         ),
         (
             pltpu.VMEM(volume.shape, BF16),
             pltpu.VMEM(cotangent.shape, BF16),
-            pltpu.VMEM(second_weight.shape, BF16),
-            pltpu.SemaphoreType.DMA((4,)),
+            pltpu.SemaphoreType.DMA((5,)),
         ),
         far=(0, 1, 2, 3),
     )(volume, cotangent, second_weight, first_weight)
@@ -252,6 +258,11 @@
     side_b = [across(edge_message, table_b, slot) for slot in range(filt)]
     side_a = [along(message, mirror(1)) for message in own]
 
+    def narrow_kernel(taps, out_ref):
+        for tap in range(14):
+            out_ref[tap] = jnp.concatenate([taps[tap], taps[tap + 13]], axis=1)
+
+    narrow = call(narrow_kernel, shaped((14, filters, 128), BF16))(second_taps)
     narrows = [narrow] + [across(narrow, mirror(0), slot) for slot in range(1, filt)]
 
     def own_kernel(*refs):
@@ -411,7 +422,6 @@
             )
         own_sides = [stacks[1], stacks[2], stacks[3]]
         second_sums = weight_planes([all_downs[0][1]], own_sides, low_depth)
-        features_ref[...] = silu(pres[0][1]).astype(BF16)
         for slot, downs in enumerate(all_downs):
             down_stacks = {k: stack3(value, low_depth) for k, value in enumerate(downs)}
             (part,) = conv_planes(back_ref.at[slot], down_stacks, 1, channels, low_depth)
@@ -441,6 +451,7 @@
         fine_stacks = [side_fine[0]] + [own_fine[p] for p in range(planes)] + [side_fine[1]]
         first_sums = packed(weight_planes(grads, fine_stacks, depth), half)
         second_sums = packed(second_sums, half)
+        features_ref[...] = silu(pres[0][1]).astype(BF16)
         keep_ref[...] = pick(odd, second_sums, first_sums)
         send_ref[:half, :] = pick(odd, first_sums, second_sums).astype(BF16)
 

time: 66.5 us -> 66.5 us (level)
    pallas_call x13 -> x14, Pallas kernels: 9.89 us -> 9.86 us  [run(): return kernel(*near)]
  transfers between devices with their start and end apart: 21 -> 21, of which waited for: 12 -> 12; matrix products, arithmetic and copies ran while one was open for 0% -> 0% of each run, Pallas kernels for 7% -> 8%
where the time goes in v8:
time: 66.5 us; the launch traced here: 66 us
  starting transfers between devices  30.5 us (46%)
  waiting for transfers between devices  24.8 us (37%)
  Pallas kernels  9.86 us (15%)
  between operations  0.78 us (1%)
    ppermute x17, starting transfers between devices, along(): return lax.ppermute(piece, 'space', table)  23.5 us
    ppermute x17, waiting for transfers between devices, along(): return lax.ppermute(piece, 'space', table)  17.4 us
    pallas_call x14, Pallas kernels, run(): return kernel(*near)  9.86 us
    ppermute x4, waiting for transfers between devices, across(): return lax.ppermute(piece, ('space', 'filt'), pairs)  7.43 us
    ppermute x4, starting transfers between devices, across(): return lax.ppermute(piece, ('space', 'filt'), pairs)  7.06 us
  transfers between devices with their start and end apart: 21, of which 12 were waited for; matrix products, arithmetic and copies ran while one was open for 0% of the time, Pallas kernels for 8%

profile of v8, /device:TPU:1, one launch (start us, length us, event | category | flops | bytes accessed | tf_op | source)
XLA Modules:
  0.0 66.0 jit_solution(10866720449913936013)
XLA Ops:
  0.6 1.3 %shard_map.75 = (bf16[64,1280]{1,0:T(8,128)(2,1)S(1)}, bf16[64,768]{1,0:T(8,128)(2,1)S(1)}, bf16[27,64,64]{2,1,0:T(8,128)(2,1)S(1)}, bf16[27,64,64]{2,1,0:T(8,128)(2,1)S(1)}) custom-call(bf16[64,2,2,256]{3,2,1,0:T(2,128)(2,1)} %refs_0_.1, bf16[64,1,2,128]{3,2,1,0:T(2,128)(2,1)} %refs_1_.1, bf16[27,64,64]{2,1,0:T(8,128)(2,1)} %refs_2_.1, ...), custom_call_target="tpu_custom_call" | custom-call | tf_op jit(solution)/shard_map/pallas_call | solution.py:34
  1.9 2.1 %collective-permute-start = (bf16[64,1280]{1,0:T(8,128)(2,1)S(1)}, bf16[64,1280]{1,0:T(8,128)(2,1)S(1)}, u32[]{:S(2)}, u32[]{:S(2)}) collective-permute-start(bf16[64,1280]{1,0:T(8,128)(2,1)S(1)} %get-tuple-element.31.refs_0_), channel_id=1, source_target_pairs={{0,1},{1,0},{2,3},{3,2},{4,5},{5,4},{6,7},{7,6},{8,9},{9,8},{10,11... | collective-permute-start | bytes 491528 | tf_op jit(solution)/shard_map/ppermute | solution.py:196
  4.0 1.0 %collective-permute-start.1 = (bf16[64,1280]{1,0:T(8,128)(2,1)S(1)}, bf16[64,1280]{1,0:T(8,128)(2,1)S(1)}, u32[]{:S(2)}, u32[]{:S(2)}) collective-permute-start(bf16[64,1280]{1,0:T(8,128)(2,1)S(1)} %get-tuple-element.31.refs_0_), channel_id=1, source_target_pairs={{0,2},{2,0},{4,6},{6,4},{8,10},{10,8},{12,14},{14,12},{16,18},{18,... | collective-permute-start | bytes 491528 | tf_op jit(solution)/shard_map/ppermute | solution.py:192
  5.0 2.9 %collective-permute-done.refs_1_ = bf16[64,1280]{1,0:T(8,128)(2,1)S(1)} collective-permute-done((bf16[64,1280]{1,0:T(8,128)(2,1)S(1)}, bf16[64,1280]{1,0:T(8,128)(2,1)S(1)}, u32[]{:S(2)}, u32[]{:S(2)}) %collective-permute-start) | collective-permute-done | bytes 163872 | tf_op jit(solution)/shard_map/ppermute | solution.py:196
  7.9 1.3 %collective-permute-start.2 = (bf16[64,1280]{1,0:T(8,128)(2,1)S(1)}, bf16[64,1280]{1,0:T(8,128)(2,1)S(1)}, u32[]{:S(2)}, u32[]{:S(2)}) collective-permute-start(bf16[64,1280]{1,0:T(8,128)(2,1)S(1)} %collective-permute-done.refs_1_), channel_id=1, source_target_pairs={{0,2},{2,0},{4,6},{6,4},{8,10},{10,8},{12,14},{14,12},{16,18},{18,... | collective-permute-start | bytes 491528 | tf_op jit(solution)/shard_map/ppermute | solution.py:192
  9.3 1.5 %collective-permute-start.10 = (bf16[14,64,128]{2,1,0:T(8,128)(2,1)S(1)}, bf16[14,64,128]{2,1,0:T(8,128)(2,1)S(1)}, u32[]{:S(2)}, u32[]{:S(2)}) collective-permute-start(bf16[14,64,128]{2,1,0:T(8,128)(2,1)S(1)} %shard_map.78.refs_0_), channel_id=1, source_target_pairs={{0,1},{1,0},{2,3},{3,2},{4,5},{5,4},{6,7},{7,6},{8,9},{9,8},{10,11... | collective-permute-start | bytes 688136 | tf_op jit(solution)/shard_map/ppermute | solution.py:196
  10.8 1.4 %collective-permute-start.4 = (bf16[64,768]{1,0:T(8,128)(2,1)S(1)}, bf16[64,768]{1,0:T(8,128)(2,1)S(1)}, u32[]{:S(2)}, u32[]{:S(2)}) collective-permute-start(bf16[64,768]{1,0:T(8,128)(2,1)S(1)} %get-tuple-element.32), channel_id=1, source_target_pairs={{0,1},{1,0},{30,31},{31,30},{2,5},{3,4},{6,9},{7,8},{10,13},{11,12... | collective-permute-start | bytes 294920 | tf_op jit(solution)/shard_map/ppermute | solution.py:196
  12.2 2.1 %collective-permute-start.3 = (bf16[64,768]{1,0:T(8,128)(2,1)S(1)}, bf16[64,768]{1,0:T(8,128)(2,1)S(1)}, u32[]{:S(2)}, u32[]{:S(2)}) collective-permute-start(bf16[64,768]{1,0:T(8,128)(2,1)S(1)} %get-tuple-element.32), channel_id=1, source_target_pairs={{0,0},{1,1},{30,30},{31,31},{2,4},{3,5},{6,8},{7,9},{10,12},{11,13... | collective-permute-start | bytes 294920 | tf_op jit(solution)/shard_map/ppermute | solution.py:196
  14.3 0.7 %shard_map.76 = (bf16[2,192,1024]{2,1,0:T(8,128)(2,1)S(1)}, f32[2,64,1024]{2,1,0:T(8,128)S(1)}, bf16[576,192]{1,0:T(8,128)(2,1)S(1)}) custom-call(bf16[64,1280]{1,0:T(8,128)(2,1)S(1)} %get-tuple-element.31.refs_0_, bf16[64,1280]{1,0:T(8,128)(2,1)S(1)} %collective-permute-done.refs_1_, bf16[27,64,64]{2,1,0:T(8,128)(2,1)S(1)} %get-tuple-element.33.refs_2_.taps), custom_call_target="tpu_custom_call" | custom-call | tf_op jit(solution)/shard_map/pallas_call | solution.py:34
  15.0 4.1 %collective-permute-done.4.refs_3_.refs_5_ = bf16[64,768]{1,0:T(8,128)(2,1)S(1)} collective-permute-done((bf16[64,768]{1,0:T(8,128)(2,1)S(1)}, bf16[64,768]{1,0:T(8,128)(2,1)S(1)}, u32[]{:S(2)}, u32[]{:S(2)}) %collective-permute-start.4) | collective-permute-done | bytes 98336 | tf_op jit(solution)/shard_map/ppermute | solution.py:196
  19.5 0.7 %shard_map.77 = (bf16[64,256]{1,0:T(8,128)(2,1)S(1)}, f32[2,64,1024]{2,1,0:T(8,128)S(1)}, bf16[2,192,1024]{2,1,0:T(8,128)(2,1)S(1)}) custom-call(bf16[64,1280]{1,0:T(8,128)(2,1)S(1)} %collective-permute-done.1.refs_0_.refs_2_, bf16[64,1280]{1,0:T(8,128)(2,1)S(1)} %collective-permute-done.2.refs_1_.refs_3_, ...), custom_call_target="tpu_custom_call" | custom-call | tf_op jit(solution)/shard_map/pallas_call | solution.py:34
  20.2 0.7 %collective-permute-start.7 = (bf16[64,256]{1,0:T(8,128)(2,1)S(1)}, bf16[64,256]{1,0:T(8,128)(2,1)S(1)}, u32[]{:S(2)}, u32[]{:S(2)}) collective-permute-start(bf16[64,256]{1,0:T(8,128)(2,1)S(1)} %get-tuple-element.36.refs_6_), channel_id=1, source_target_pairs={{4,8},{6,10},{12,16},{14,18},{20,24},{22,26},{8,4},{10,6},{16,12},... | collective-permute-start | bytes 98312 | tf_op jit(solution)/shard_map/ppermute | solution.py:192
  20.9 4.5 %collective-permute-start.6 = (bf16[64,256]{1,0:T(8,128)(2,1)S(1)}, bf16[64,256]{1,0:T(8,128)(2,1)S(1)}, u32[]{:S(2)}, u32[]{:S(2)}) collective-permute-start(bf16[64,256]{1,0:T(8,128)(2,1)S(1)} %get-tuple-element.36.refs_6_), channel_id=1, source_target_pairs={{0,4},{2,6},{4,0},{6,2},{8,12},{10,14},{12,8},{14,10},{16,20},{18,... | collective-permute-start | bytes 98312 | tf_op jit(solution)/shard_map/ppermute | solution.py:192
  26.0 0.8 %collective-permute-done.6.refs_8_ = bf16[64,256]{1,0:T(8,128)(2,1)S(1)} collective-permute-done((bf16[64,256]{1,0:T(8,128)(2,1)S(1)}, bf16[64,256]{1,0:T(8,128)(2,1)S(1)}, u32[]{:S(2)}, u32[]{:S(2)}) %collective-permute-start.6) | collective-permute-done | bytes 32800 | tf_op jit(solution)/shard_map/ppermute | solution.py:192
  27.4 0.6 collective-permute-done.8.refs_10_
  28.0 2.4 %shard_map.80 = (bf16[64,256]{1,0:T(8,128)(2,1)S(1)}, bf16[2,64,1024]{2,1,0:T(8,128)(2,1)S(1)}, bf16[64,1024]{1,0:T(8,128)(2,1)S(1)}, f32[896,128]{1,0:T(8,128)S(1)}, bf16[1408,128]{1,0:T(8,128)(2,1)S(1)}) custom-call(bf16[64,1280]{1,0:T(8,128)(2,1)S(1)} %get-tuple-element.31.refs_0_, bf16[64,1280]{1,0:T(8,128)(2,1)S(1)} %collective-permute-done.refs_1_, ...), custom_call_target="tpu_custom_call" | custom-call | tf_op jit(solution)/shard_map/pallas_call | solution.py:34
  30.6 1.5 %collective-permute-done.11.a_ref.got_ref = bf16[1408,128]{1,0:T(8,128)(2,1)S(1)} collective-permute-done((bf16[1408,128]{1,0:T(8,128)(2,1)S(1)}, bf16[1408,128]{1,0:T(8,128)(2,1)S(1)}, u32[]{:S(2)}, u32[]{:S(2)}) %collective-permute-start.11) | collective-permute-done | bytes 360480 | tf_op jit(solution)/shard_map/ppermute | solution.py:192
  32.2 2.7 %collective-permute-start.13 = (bf16[224,128]{1,0:T(8,128)(2,1)S(1)}, bf16[224,128]{1,0:T(8,128)(2,1)S(1)}, u32[]{:S(2)}, u32[]{:S(2)}) collective-permute-start(bf16[224,128]{1,0:T(8,128)(2,1)S(1)} %get-tuple-element.51), channel_id=1, source_target_pairs={{0,8},{2,10},{4,12},{6,14},{8,0},{10,2},{12,4},{14,6},{16,24},{18,... | collective-permute-start | bytes 172040 | tf_op jit(solution)/shard_map/ppermute | solution.py:192
  34.9 2.4 %collective-permute-start.14 = (bf16[224,128]{1,0:T(8,128)(2,1)S(1)}, bf16[224,128]{1,0:T(8,128)(2,1)S(1)}, u32[]{:S(2)}, u32[]{:S(2)}) collective-permute-start(bf16[224,128]{1,0:T(8,128)(2,1)S(1)} %get-tuple-element.52), channel_id=1, source_target_pairs={{0,16},{2,18},{4,20},{6,22},{8,24},{10,26},{12,28},{14,30},{16,0},... | collective-permute-start | bytes 172040 | tf_op jit(solution)/shard_map/ppermute | solution.py:192
  37.3 1.6 %collective-permute-done.14.refs_1_ = bf16[224,128]{1,0:T(8,128)(2,1)S(1)} collective-permute-done((bf16[224,128]{1,0:T(8,128)(2,1)S(1)}, bf16[224,128]{1,0:T(8,128)(2,1)S(1)}, u32[]{:S(2)}, u32[]{:S(2)}) %collective-permute-start.14) | collective-permute-done | bytes 57376 | tf_op jit(solution)/shard_map/ppermute | solution.py:192
  38.9 3.4 %collective-permute-done.15.refs_2_ = bf16[224,128]{1,0:T(8,128)(2,1)S(1)} collective-permute-done((bf16[224,128]{1,0:T(8,128)(2,1)S(1)}, bf16[224,128]{1,0:T(8,128)(2,1)S(1)}, u32[]{:S(2)}, u32[]{:S(2)}) %collective-permute-start.15) | collective-permute-done | bytes 57376 | tf_op jit(solution)/shard_map/ppermute | solution.py:192
  42.3 3.0 %collective-permute-done.16.refs_0_ = bf16[224,128]{1,0:T(8,128)(2,1)S(1)} collective-permute-done((bf16[224,128]{1,0:T(8,128)(2,1)S(1)}, bf16[224,128]{1,0:T(8,128)(2,1)S(1)}, u32[]{:S(2)}, u32[]{:S(2)}) %collective-permute-start.16) | collective-permute-done | bytes 57376 | tf_op jit(solution)/shard_map/ppermute | solution.py:192
  45.4 1.4 %collective-permute-start.19 = (bf16[224,128]{1,0:T(8,128)(2,1)S(1)}, bf16[224,128]{1,0:T(8,128)(2,1)S(1)}, u32[]{:S(2)}, u32[]{:S(2)}) collective-permute-start(bf16[224,128]{1,0:T(8,128)(2,1)S(1)} %shard_map.85.refs_0_), channel_id=1, source_target_pairs={{0,24},{2,26},{4,28},{6,30},{8,16},{10,18},{12,20},{14,22},{16,8},... | collective-permute-start | bytes 172040 | tf_op jit(solution)/shard_map/ppermute | solution.py:192
  47.4 1.6 %collective-permute-start.17 = (bf16[224,128]{1,0:T(8,128)(2,1)S(1)}, bf16[224,128]{1,0:T(8,128)(2,1)S(1)}, u32[]{:S(2)}, u32[]{:S(2)}) collective-permute-start(bf16[224,128]{1,0:T(8,128)(2,1)S(1)} %shard_map.85.refs_0_), channel_id=1, source_target_pairs={{0,8},{2,10},{4,12},{6,14},{8,0},{10,2},{12,4},{14,6},{16,24},{18,... | collective-permute-start | bytes 172040 | tf_op jit(solution)/shard_map/ppermute | solution.py:192
  49.0 1.3 %collective-permute-done.19.refs_3_ = bf16[224,128]{1,0:T(8,128)(2,1)S(1)} collective-permute-done((bf16[224,128]{1,0:T(8,128)(2,1)S(1)}, bf16[224,128]{1,0:T(8,128)(2,1)S(1)}, u32[]{:S(2)}, u32[]{:S(2)}) %collective-permute-start.19) | collective-permute-done | bytes 57376 | tf_op jit(solution)/shard_map/ppermute | solution.py:192
  50.3 1.6 %collective-permute-done.18.refs_2_ = bf16[224,128]{1,0:T(8,128)(2,1)S(1)} collective-permute-done((bf16[224,128]{1,0:T(8,128)(2,1)S(1)}, bf16[224,128]{1,0:T(8,128)(2,1)S(1)}, u32[]{:S(2)}, u32[]{:S(2)}) %collective-permute-start.18) | collective-permute-done | bytes 57376 | tf_op jit(solution)/shard_map/ppermute | solution.py:192
  51.9 3.9 %collective-permute-start.20 = (bf16[896,128]{1,0:T(8,128)(2,1)S(1)}, bf16[896,128]{1,0:T(8,128)(2,1)S(1)}, u32[]{:S(2)}, u32[]{:S(2)}) collective-permute-start(bf16[896,128]{1,0:T(8,128)(2,1)S(1)} %shard_map.86.refs_0_), channel_id=1, source_target_pairs={{0,2},{2,0},{4,6},{6,4},{8,10},{10,8},{12,14},{14,12},{16,18},{18,... | collective-permute-start | bytes 688136 | tf_op jit(solution)/shard_map/ppermute | solution.py:192
  55.9 2.5 %collective-permute-start.12 = (bf16[64,1024]{1,0:T(8,128)(2,1)S(1)}, bf16[64,1024]{1,0:T(8,128)(2,1)S(1)}, u32[]{:S(2)}, u32[]{:S(2)}) collective-permute-start(bf16[64,1024]{1,0:T(8,128)(2,1)S(1)} %get-tuple-element.45), channel_id=1, source_target_pairs={{0,0},{30,30},{2,4},{6,8},{10,12},{14,16},{18,20},{22,24},{26,28},... | collective-permute-start | bytes 393224 | tf_op jit(solution)/shard_map/ppermute | solution.py:192
  58.6 3.6 %collective-permute-done.12.b_ref = bf16[64,1024]{1,0:T(8,128)(2,1)S(1)} collective-permute-done((bf16[64,1024]{1,0:T(8,128)(2,1)S(1)}, bf16[64,1024]{1,0:T(8,128)(2,1)S(1)}, u32[]{:S(2)}, u32[]{:S(2)}) %collective-permute-start.12) | collective-permute-done | bytes 131104 | tf_op jit(solution)/shard_map/ppermute | solution.py:192
  62.1 1.7 %shard_map.82 = (bf16[64,2,2,256]{3,2,1,0:T(2,128)(2,1)}, bf16[64,1,2,128]{3,2,1,0:T(2,128)(2,1)}) custom-call(bf16[2,64,1024]{2,1,0:T(8,128)(2,1)S(1)} %get-tuple-element.43.own_ref, bf16[1408,128]{1,0:T(8,128)(2,1)S(1)} %collective-permute-done.11.a_ref.got_ref, bf16[64,1024]{1,0:T(8,128)(2,1)S(1)} %collective-permute-done.12.b_ref, ...), custom_call_target="tpu_custom_call" | custom-call | tf_op jit(solution)/shard_map/pallas_call | solution.py:34
  63.9 1.1 %shard_map.87 = (f32[27,64,64]{2,1,0:T(8,128)}, f32[27,64,64]{2,1,0:T(8,128)}) custom-call(bf16[896,128]{1,0:T(8,128)(2,1)S(1)} %shard_map.86.refs_0_), custom_call_target="tpu_custom_call" | custom-call | tf_op jit(solution)/shard_map/pallas_call | solution.py:34
  64.9 1.0 %shard_map.88 = (f32[27,64,64]{2,1,0:T(8,128)}, f32[27,64,64]{2,1,0:T(8,128)}) custom-call(bf16[896,128]{1,0:T(8,128)(2,1)S(1)} %collective-permute-done.20.refs_0_, f32[27,64,64]{2,1,0:T(8,128)} %get-tuple-element.54.refs_1_, f32[27,64,64]{2,1,0:T(8,128)} %get-tuple-element.55.refs_2_), custom_call_target="tpu_custom_call", output_to_operand_aliasing={{0}: (1, {}), {1}: (2, {})} | custom-call | tf_op jit(solution)/shard_map/pallas_call | solution.py:34
  (24 shorter events, 2.9 us)
Async XLA Ops:
  1.9 6.0 %collective-permute-start = (bf16[64,1280]{1,0:T(8,128)(2,1)S(1)}, bf16[64,1280]{1,0:T(8,128)(2,1)S(1)}, u32[]{:S(2)}, u32[]{:S(2)}) collective-permute-start(bf16[64,1280]{1,0:T(8,128)(2,1)S(1)} %get-tuple-element.31.refs_0_), channel_id=1, source_target_pairs={{0,1},{1,0},{2,3},{3,2},{4,5},{5,4},{6,7},{7,6},{8,9},{9,8},{10,11... | collective-permute-start | bytes 491528 | tf_op jit(solution)/shard_map/ppermute | solution.py:196
  4.0 15.5 %collective-permute-start.1 = (bf16[64,1280]{1,0:T(8,128)(2,1)S(1)}, bf16[64,1280]{1,0:T(8,128)(2,1)S(1)}, u32[]{:S(2)}, u32[]{:S(2)}) collective-permute-start(bf16[64,1280]{1,0:T(8,128)(2,1)S(1)} %get-tuple-element.31.refs_0_), channel_id=1, source_target_pairs={{0,2},{2,0},{4,6},{6,4},{8,10},{10,8},{12,14},{14,12},{16,18},{18,... | collective-permute-start | bytes 491528 | tf_op jit(solution)/shard_map/ppermute | solution.py:192
  7.9 11.6 %collective-permute-start.2 = (bf16[64,1280]{1,0:T(8,128)(2,1)S(1)}, bf16[64,1280]{1,0:T(8,128)(2,1)S(1)}, u32[]{:S(2)}, u32[]{:S(2)}) collective-permute-start(bf16[64,1280]{1,0:T(8,128)(2,1)S(1)} %collective-permute-done.refs_1_), channel_id=1, source_target_pairs={{0,2},{2,0},{4,6},{6,4},{8,10},{10,8},{12,14},{14,12},{16,18},{18,... | collective-permute-start | bytes 491528 | tf_op jit(solution)/shard_map/ppermute | solution.py:192
  9.3 17.6 %collective-permute-start.10 = (bf16[14,64,128]{2,1,0:T(8,128)(2,1)S(1)}, bf16[14,64,128]{2,1,0:T(8,128)(2,1)S(1)}, u32[]{:S(2)}, u32[]{:S(2)}) collective-permute-start(bf16[14,64,128]{2,1,0:T(8,128)(2,1)S(1)} %shard_map.78.refs_0_), channel_id=1, source_target_pairs={{0,1},{1,0},{2,3},{3,2},{4,5},{5,4},{6,7},{7,6},{8,9},{9,8},{10,11... | collective-permute-start | bytes 688136 | tf_op jit(solution)/shard_map/ppermute | solution.py:196
  10.8 8.2 %collective-permute-start.4 = (bf16[64,768]{1,0:T(8,128)(2,1)S(1)}, bf16[64,768]{1,0:T(8,128)(2,1)S(1)}, u32[]{:S(2)}, u32[]{:S(2)}) collective-permute-start(bf16[64,768]{1,0:T(8,128)(2,1)S(1)} %get-tuple-element.32), channel_id=1, source_target_pairs={{0,1},{1,0},{30,31},{31,30},{2,5},{3,4},{6,9},{7,8},{10,13},{11,12... | collective-permute-start | bytes 294920 | tf_op jit(solution)/shard_map/ppermute | solution.py:196
  12.2 7.3 %collective-permute-start.3 = (bf16[64,768]{1,0:T(8,128)(2,1)S(1)}, bf16[64,768]{1,0:T(8,128)(2,1)S(1)}, u32[]{:S(2)}, u32[]{:S(2)}) collective-permute-start(bf16[64,768]{1,0:T(8,128)(2,1)S(1)} %get-tuple-element.32), channel_id=1, source_target_pairs={{0,0},{1,1},{30,30},{31,31},{2,4},{3,5},{6,8},{7,9},{10,12},{11,13... | collective-permute-start | bytes 294920 | tf_op jit(solution)/shard_map/ppermute | solution.py:196
  20.2 5.2 %collective-permute-start.7 = (bf16[64,256]{1,0:T(8,128)(2,1)S(1)}, bf16[64,256]{1,0:T(8,128)(2,1)S(1)}, u32[]{:S(2)}, u32[]{:S(2)}) collective-permute-start(bf16[64,256]{1,0:T(8,128)(2,1)S(1)} %get-tuple-element.36.refs_6_), channel_id=1, source_target_pairs={{4,8},{6,10},{12,16},{14,18},{20,24},{22,26},{8,4},{10,6},{16,12},... | collective-permute-start | bytes 98312 | tf_op jit(solution)/shard_map/ppermute | solution.py:192
  20.9 5.9 %collective-permute-start.6 = (bf16[64,256]{1,0:T(8,128)(2,1)S(1)}, bf16[64,256]{1,0:T(8,128)(2,1)S(1)}, u32[]{:S(2)}, u32[]{:S(2)}) collective-permute-start(bf16[64,256]{1,0:T(8,128)(2,1)S(1)} %get-tuple-element.36.refs_6_), channel_id=1, source_target_pairs={{0,4},{2,6},{4,0},{6,2},{8,12},{10,14},{12,8},{14,10},{16,20},{18,... | collective-permute-start | bytes 98312 | tf_op jit(solution)/shard_map/ppermute | solution.py:192
  25.5 1.9 %collective-permute-start.5 = (bf16[64,256]{1,0:T(8,128)(2,1)S(1)}, bf16[64,256]{1,0:T(8,128)(2,1)S(1)}, u32[]{:S(2)}, u32[]{:S(2)}) collective-permute-start(bf16[64,256]{1,0:T(8,128)(2,1)S(1)} %get-tuple-element.36.refs_6_), channel_id=1, source_target_pairs={{0,2},{2,0},{4,6},{6,4},{8,10},{10,8},{12,14},{14,12},{16,18},{18,... | collective-permute-start | bytes 98312 | tf_op jit(solution)/shard_map/ppermute | solution.py:192
  25.5 1.9 %collective-permute-start.9 = (bf16[64,256]{1,0:T(8,128)(2,1)S(1)}, bf16[64,256]{1,0:T(8,128)(2,1)S(1)}, u32[]{:S(2)}, u32[]{:S(2)}) collective-permute-start(bf16[64,256]{1,0:T(8,128)(2,1)S(1)} %collective-permute-done.7.refs_9_), channel_id=1, source_target_pairs={{0,2},{2,0},{4,6},{6,4},{8,10},{10,8},{12,14},{14,12},{16,18},{18,... | collective-permute-start | bytes 98312 | tf_op jit(solution)/shard_map/ppermute | solution.py:192
  26.8 1.2 %collective-permute-start.8 = (bf16[64,256]{1,0:T(8,128)(2,1)S(1)}, bf16[64,256]{1,0:T(8,128)(2,1)S(1)}, u32[]{:S(2)}, u32[]{:S(2)}) collective-permute-start(bf16[64,256]{1,0:T(8,128)(2,1)S(1)} %collective-permute-done.6.refs_8_), channel_id=1, source_target_pairs={{0,2},{2,0},{4,6},{6,4},{8,10},{10,8},{12,14},{14,12},{16,18},{18,... | collective-permute-start | bytes 98312 | tf_op jit(solution)/shard_map/ppermute | solution.py:192
  30.4 1.7 %collective-permute-start.11 = (bf16[1408,128]{1,0:T(8,128)(2,1)S(1)}, bf16[1408,128]{1,0:T(8,128)(2,1)S(1)}, u32[]{:S(2)}, u32[]{:S(2)}) collective-permute-start(bf16[1408,128]{1,0:T(8,128)(2,1)S(1)} %get-tuple-element.44), channel_id=1, source_target_pairs={{0,2},{2,0},{4,6},{6,4},{8,10},{10,8},{12,14},{14,12},{16,18},{18,... | collective-permute-start | bytes 1081352 | tf_op jit(solution)/shard_map/ppermute | solution.py:192
  32.2 5.1 %collective-permute-start.13 = (bf16[224,128]{1,0:T(8,128)(2,1)S(1)}, bf16[224,128]{1,0:T(8,128)(2,1)S(1)}, u32[]{:S(2)}, u32[]{:S(2)}) collective-permute-start(bf16[224,128]{1,0:T(8,128)(2,1)S(1)} %get-tuple-element.51), channel_id=1, source_target_pairs={{0,8},{2,10},{4,12},{6,14},{8,0},{10,2},{12,4},{14,6},{16,24},{18,... | collective-permute-start | bytes 172040 | tf_op jit(solution)/shard_map/ppermute | solution.py:192
  34.9 4.0 %collective-permute-start.14 = (bf16[224,128]{1,0:T(8,128)(2,1)S(1)}, bf16[224,128]{1,0:T(8,128)(2,1)S(1)}, u32[]{:S(2)}, u32[]{:S(2)}) collective-permute-start(bf16[224,128]{1,0:T(8,128)(2,1)S(1)} %get-tuple-element.52), channel_id=1, source_target_pairs={{0,16},{2,18},{4,20},{6,22},{8,24},{10,26},{12,28},{14,30},{16,0},... | collective-permute-start | bytes 172040 | tf_op jit(solution)/shard_map/ppermute | solution.py:192
  37.3 4.9 %collective-permute-start.15 = (bf16[224,128]{1,0:T(8,128)(2,1)S(1)}, bf16[224,128]{1,0:T(8,128)(2,1)S(1)}, u32[]{:S(2)}, u32[]{:S(2)}) collective-permute-start(bf16[224,128]{1,0:T(8,128)(2,1)S(1)} %get-tuple-element.53), channel_id=1, source_target_pairs={{0,24},{2,26},{4,28},{6,30},{8,16},{10,18},{12,20},{14,22},{16,8},... | collective-permute-start | bytes 172040 | tf_op jit(solution)/shard_map/ppermute | solution.py:192
  42.2 3.1 %collective-permute-start.16 = (bf16[224,128]{1,0:T(8,128)(2,1)S(1)}, bf16[224,128]{1,0:T(8,128)(2,1)S(1)}, u32[]{:S(2)}, u32[]{:S(2)}) collective-permute-start(bf16[224,128]{1,0:T(8,128)(2,1)S(1)} %shard_map.84.own_ref), channel_id=1, source_target_pairs={{0,4},{2,6},{4,0},{6,2},{8,12},{10,14},{12,8},{14,10},{16,20},{18,... | collective-permute-start | bytes 172040 | tf_op jit(solution)/shard_map/ppermute | solution.py:192
  45.4 4.9 %collective-permute-start.19 = (bf16[224,128]{1,0:T(8,128)(2,1)S(1)}, bf16[224,128]{1,0:T(8,128)(2,1)S(1)}, u32[]{:S(2)}, u32[]{:S(2)}) collective-permute-start(bf16[224,128]{1,0:T(8,128)(2,1)S(1)} %shard_map.85.refs_0_), channel_id=1, source_target_pairs={{0,24},{2,26},{4,28},{6,30},{8,16},{10,18},{12,20},{14,22},{16,8},... | collective-permute-start | bytes 172040 | tf_op jit(solution)/shard_map/ppermute | solution.py:192
  46.8 5.1 %collective-permute-start.18 = (bf16[224,128]{1,0:T(8,128)(2,1)S(1)}, bf16[224,128]{1,0:T(8,128)(2,1)S(1)}, u32[]{:S(2)}, u32[]{:S(2)}) collective-permute-start(bf16[224,128]{1,0:T(8,128)(2,1)S(1)} %shard_map.85.refs_0_), channel_id=1, source_target_pairs={{0,16},{2,18},{4,20},{6,22},{8,24},{10,26},{12,28},{14,30},{16,0},... | collective-permute-start | bytes 172040 | tf_op jit(solution)/shard_map/ppermute | solution.py:192
  47.4 4.6 %collective-permute-start.17 = (bf16[224,128]{1,0:T(8,128)(2,1)S(1)}, bf16[224,128]{1,0:T(8,128)(2,1)S(1)}, u32[]{:S(2)}, u32[]{:S(2)}) collective-permute-start(bf16[224,128]{1,0:T(8,128)(2,1)S(1)} %shard_map.85.refs_0_), channel_id=1, source_target_pairs={{0,8},{2,10},{4,12},{6,14},{8,0},{10,2},{12,4},{14,6},{16,24},{18,... | collective-permute-start | bytes 172040 | tf_op jit(solution)/shard_map/ppermute | solution.py:192
  51.9 13.0 %collective-permute-start.20 = (bf16[896,128]{1,0:T(8,128)(2,1)S(1)}, bf16[896,128]{1,0:T(8,128)(2,1)S(1)}, u32[]{:S(2)}, u32[]{:S(2)}) collective-permute-start(bf16[896,128]{1,0:T(8,128)(2,1)S(1)} %shard_map.86.refs_0_), channel_id=1, source_target_pairs={{0,2},{2,0},{4,6},{6,4},{8,10},{10,8},{12,14},{14,12},{16,18},{18,... | collective-permute-start | bytes 688136 | tf_op jit(solution)/shard_map/ppermute | solution.py:192
  55.9 6.3 %collective-permute-start.12 = (bf16[64,1024]{1,0:T(8,128)(2,1)S(1)}, bf16[64,1024]{1,0:T(8,128)(2,1)S(1)}, u32[]{:S(2)}, u32[]{:S(2)}) collective-permute-start(bf16[64,1024]{1,0:T(8,128)(2,1)S(1)} %get-tuple-element.45), channel_id=1, source_target_pairs={{0,0},{30,30},{2,4},{6,8},{10,12},{14,16},{18,20},{22,24},{26,28},... | collective-permute-start | bytes 393224 | tf_op jit(solution)/shard_map/ppermute | solution.py:192
